TPU v7x, 128 devices: a whole 4x4x4 slice. The times are simulated.
128 devices in a mesh: dp: 16 (over z_lo, x, core), mp: 8 (over y, z_hi).
Axes of the slice: x: 4, y: 4, z: 4 (z_hi: 2, z_lo: 2; z = z_hi * 2 + z_lo), core: 2. Of those that a mesh axis runs over, the one named last changes fastest.
Arguments:
- fields: bfloat16 [16, 128, 20, 128, 128], P('dp', 'mp'), may hold values from -6 to 6
- cotangent: bfloat16 [16, 128, 20, 128, 128], P('dp', 'mp'), may hold values from -3 to 3
- spectral_weight: bfloat16 [32, 2, 20, 20, 512], P('dp', None, None, None, 'mp'), may hold values from -5 to 5
- conv_weight: bfloat16 [20, 20], replicated, may hold values from -1.25 to 1.25
- conv_bias: float32 [20], replicated, may hold values from -3 to 3
Outputs:
- spectral_grad: float32 [32, 2, 20, 20, 512], P('dp', None, None, None, 'mp')
All inputs are finite; a program needn't handle non-finite values.
Results may differ from a plain program's by a relative error of at most 0.0085.
Values may be sent and summed in bfloat16 or wider, within the bound.
No kernel may reach another device: no remote copies, remote signals or barrier semaphores. Data moves between devices by JAX's collectives and lax.ppermute only.
A program may use at most 256 MiB of HBM per device.

v0:
```python
import math

import jax
import jax.numpy as jnp
from jax import lax
from jax.sharding import PartitionSpec as P

X = 128
Y = 128
Z = 128
C = 20
KX = 32
KY = 32
KZ = 16


inv_root_two = 0.7071067811865476
inv_root_two_pi = 0.3989422804014327
highest = lax.Precision.HIGHEST


def kept_modes(count, length):
    indices = jnp.arange(count, dtype=jnp.int32)
    return jnp.where(indices < count // 2, indices, length - count + indices)


def gelu_slope(values):
    return (
        0.5 * (1.0 + lax.erf(values * inv_root_two))
        + values * jnp.exp(-0.5 * values * values) * inv_root_two_pi
    )


def dft_tables(kept, length):
    cells = jnp.arange(length, dtype=jnp.int32)
    phases = 2.0 * math.pi / length * (kept[:, None] * cells[None, :] % length).astype(jnp.float32)
    return (jnp.cos(phases), jnp.sin(phases))


def split_parts(values):
    upper = values.astype(jnp.bfloat16)
    lower = (values - upper.astype(jnp.float32)).astype(jnp.bfloat16)
    return (upper, lower)


def two_pass(form, data_bf, table_pair):
    first = jnp.einsum(form, data_bf, table_pair[0], preferred_element_type=jnp.float32)
    return first + jnp.einsum(form, data_bf, table_pair[1], preferred_element_type=jnp.float32)


def three_pass(form, data_f32, table_pair):
    data_hi, data_lo = split_parts(data_f32)
    total = jnp.einsum(form, data_hi, table_pair[0], preferred_element_type=jnp.float32)
    total = total + jnp.einsum(form, data_hi, table_pair[1], preferred_element_type=jnp.float32)
    return total + jnp.einsum(form, data_lo, table_pair[0], preferred_element_type=jnp.float32)


def mix_modes(modes_in, weights):
    spec_re = modes_in[..., 0, :, :]
    spec_im = modes_in[..., 1, :, :]
    real_w = weights[..., 0, :, :, :]
    imag_w = weights[..., 1, :, :, :]
    out_re = jnp.einsum("...cm,...com->...om", spec_re, real_w, precision=highest) - jnp.einsum(
        "...cm,...com->...om", spec_im, imag_w, precision=highest
    )
    out_im = jnp.einsum("...cm,...com->...om", spec_re, imag_w, precision=highest) + jnp.einsum(
        "...cm,...com->...om", spec_im, real_w, precision=highest
    )
    return jnp.stack([out_re, out_im], axis=-3)


def grad_term(modes_in, back_modes):
    spec_re = modes_in[..., 0, :, :]
    spec_im = modes_in[..., 1, :, :]
    back_re = back_modes[..., 0, :, :]
    back_im = back_modes[..., 1, :, :]
    grad_re = jnp.einsum("...cm,...om->...com", spec_re, back_re, precision=highest) + jnp.einsum(
        "...cm,...om->...com", spec_im, back_im, precision=highest
    )
    grad_im = jnp.einsum("...cm,...om->...com", spec_re, back_im, precision=highest) - jnp.einsum(
        "...cm,...om->...com", spec_im, back_re, precision=highest
    )
    return jnp.stack([grad_re, grad_im], axis=-4)


def shards(fields, cotangent, spectral_weight, conv_weight, conv_bias):
    slab_len = fields.shape[1]
    ky_local = KY // lax.axis_size("mp")
    cos_x, sin_x = dft_tables(kept_modes(KX, X), X)
    cos_y, sin_y = dft_tables(kept_modes(KY, Y), Y)
    modes_z = jnp.arange(KZ, dtype=jnp.int32)
    cos_z, sin_z = dft_tables(modes_z, Z)
    weight_z = jnp.where(modes_z == 0, 1.0, 2.0).astype(jnp.float32) / (X * Y * Z)
    table_y = split_parts(jnp.concatenate([cos_y.T, -sin_y.T], axis=1))
    table_z = jnp.concatenate([cos_z.T, -sin_z.T], axis=1)
    inverse_re = jnp.concatenate([weight_z[:, None] * cos_z, -weight_z[:, None] * sin_z], axis=0)
    inverse_im = jnp.concatenate([weight_z[:, None] * sin_z, weight_z[:, None] * cos_z], axis=0)
    inverse_y = split_parts(jnp.concatenate([cos_y, -sin_y], axis=0))
    scale_modes = jnp.tile(weight_z, ky_local)

    def forward_modes(volume):
        along_y = two_pass("xcyz,yk->xckz", volume, table_y)
        along_yz = jnp.einsum("xckz,zm->xckm", along_y, table_z, precision=highest)
        a_cos = along_yz[:, :, :KY, :KZ]
        a_sin = along_yz[:, :, :KY, KZ:]
        b_cos = along_yz[:, :, KY:, :KZ]
        b_sin = along_yz[:, :, KY:, KZ:]
        packed = jnp.stack([a_cos - b_sin, b_cos + a_sin], axis=3)
        packed = jnp.transpose(packed, (0, 2, 1, 3, 4)).reshape(slab_len, KY, -1)
        moved = lax.all_to_all(packed, "mp", split_axis=1, concat_axis=0, tiled=True)
        flat_modes = moved.reshape(X, -1)
        with_cos = jnp.dot(cos_x, flat_modes, precision=highest).reshape(KX, ky_local, C, 2, KZ)
        with_sin = jnp.dot(sin_x, flat_modes, precision=highest).reshape(KX, ky_local, C, 2, KZ)
        real_part = with_cos[:, :, :, 0] + with_sin[:, :, :, 1]
        imag_part = with_cos[:, :, :, 1] - with_sin[:, :, :, 0]
        stacked = jnp.stack([real_part, imag_part], axis=1)
        return jnp.transpose(stacked, (0, 1, 3, 2, 4)).reshape(KX, 2, C, ky_local * KZ)

    volume = fields[0]
    spectra = forward_modes(volume)
    conv_term = jnp.einsum("xcyz,co->xoyz", volume, conv_weight, preferred_element_type=jnp.float32)
    spec_rows = spectra
    mixed_modes = mix_modes(
        spec_rows, lax.all_gather(spectral_weight, "dp", axis=0, tiled=True).astype(jnp.float32)
    )
    flat_mixed = mixed_modes.reshape(KX, -1)
    back_cos = jnp.dot(cos_x.T, flat_mixed, precision=highest).reshape(X, 2, C, ky_local, KZ)
    back_sin = jnp.dot(sin_x.T, flat_mixed, precision=highest).reshape(X, 2, C, ky_local, KZ)
    real_part = back_cos[:, 0] - back_sin[:, 1]
    imag_part = back_sin[:, 0] + back_cos[:, 1]
    outgoing = jnp.transpose(jnp.stack([real_part, imag_part], axis=3), (0, 2, 1, 3, 4)).reshape(
        X, ky_local, -1
    )
    slabs = lax.all_to_all(outgoing, "mp", split_axis=0, concat_axis=1, tiled=True).reshape(
        slab_len, KY, C, 2 * KZ
    )
    along_re = jnp.einsum("xkcm,mz->xkcz", slabs, inverse_re, precision=highest)
    along_im = jnp.einsum("xkcm,mz->xkcz", slabs, inverse_im, precision=highest)
    spectral = three_pass("xkcz,ky->xcyz", jnp.concatenate([along_re, along_im], axis=1), inverse_y)
    pre_act = spectral + conv_term + conv_bias[:, None, None]
    grad_pre = (cotangent[0].astype(jnp.float32) * gelu_slope(pre_act)).astype(jnp.bfloat16)
    back_spectra = forward_modes(grad_pre) * scale_modes
    spec_rows = spectra
    return lax.psum_scatter(
        grad_term(spec_rows, back_spectra), "dp", scatter_dimension=0, tiled=True
    )


def solution(mesh):
    return jax.shard_map(
        shards,
        mesh=mesh,
        in_specs=(
            P("dp", "mp", None, None, None),
            P("dp", "mp", None, None, None),
            P("dp", None, None, None, "mp"),
            P(),
            P(),
        ),
        out_specs=P("dp", None, None, None, "mp"),
        check_vma=False,
    )
```

profile of v0, /device:TPU:1, one launch (start us, length us, event | category | flops | bytes accessed | tf_op | source)
XLA Modules:
  0.0 500.8 jit_solution(13986098638984320614)
XLA Ops:
  7.5 9.5 %fusion.112 = f32[64,16,20,128]{3,0,2,1:T(8,128)} fusion(f32[128,32]{0,1:T(8,128)S(1)} %get-tuple-element.30, f32[128,32]{0,1:T(8,128)S(1)} %get-tuple-element.29, bf16[1,16,20,128,128]{4,3,2,1,0:T(8,128)(2,1)} %param.5), kind=kOutput, calls=%fused_computation.163 | convolution fusion | flops 671129600 | bytes 21004288 | tf_op jit(solution)/shard_map/xcyz,yk->xckz/dot_general | solution.py:48
  17.0 5.0 fusion.118
  22.0 31.4 %fusion.11 = f32[16,20,64,32]{2,3,1,0:T(8,128)S(1)} fusion(f32[64,16,20,128]{3,0,2,1:T(8,128)} %fusion.118, f32[64,16,20,128]{3,0,2,1:T(8,128)} %fusion.112, f32[128,16]{0,1:T(8,128)S(1)} %get-tuple-element.31, f32[128,16]{0,1:T(8,128)S(1)} %get-tuple-element.32), kind=kOutput, calls=%fused_computation.15 | convolution fusion | flops 1009258496 | bytes 23609344 | tf_op jit(solution)/shard_map/xckz,zm->xckm/dot_general | solution.py:103
  55.2 3.0 copy.81
  58.2 5.1 %copy.82 = f32[16,32,640]{2,0,1:T(8,128)} copy(f32[16,32,640]{1,2,0:T(8,128)} %bitcast.232) | data formatting | bytes 2621440 | tf_op jit(solution)/shard_map/reshape | solution.py:109
  63.3 8.6 %all-to-all-start = ((f32[16,32,640]{2,0,1:T(8,128)}), f32[16,32,640]{2,0,1:T(8,128)S(1)}, u32[]{:S(2)}, u32[]{:S(2)}) async-start(f32[16,32,640]{2,0,1:T(8,128)} %copy.82), calls=%async_computation | async-start | bytes 2621440 | tf_op jit(solution)/shard_map/all_to_all | solution.py:110
  72.1 19.1 %all-to-all-done = f32[16,32,640]{2,0,1:T(8,128)S(1)} async-done(((f32[16,32,640]{2,0,1:T(8,128)}), f32[16,32,640]{2,0,1:T(8,128)S(1)}, u32[]{:S(2)}, u32[]{:S(2)}) %all-to-all-start) | async-done | bytes 1310752 | tf_op jit(solution)/shard_map/all_to_all | solution.py:110
  92.2 2.1 fusion.38
  97.3 15.0 %fusion.159 = (bf16[32,1,20,20,64]{4,1,3,2,0:T(2,128)(2,1)S(1)}, bf16[32,1,20,20,64]{4,1,3,2,0:T(2,128)(2,1)S(1)}) fusion(bf16[32,2,20,20,64]{4,1,3,2,0:T(2,128)(2,1)} %all-gather.2.cloned.1.call-done), kind=kLoop, calls=%fused_computation.207 | loop fusion | bytes 6553600 | tf_op jit(solution)/shard_map/slice | solution.py:61
  112.4 6.3 %fusion.18 = (f32[32,64,20]{1,0,2:T(8,128)S(1)}, f32[32,64,20]{1,0,2:T(8,128)S(1)}, f32[32,64,20]{1,0,2:T(8,128)S(1)}, f32[32,64,20]{1,0,2:T(8,128)S(1)}) fusion(f32[32,64,20]{1,0,2:T(8,128)S(1)} %copy.168, bf16[32,1,20,20,64]{4,1,3,2,0:T(2,128)(2,1)S(1)} %get-tuple-element.12, f32[32,64,20]{1,0,2:T(8,128)S(1)} %copy.167, ...), kind=kLoop, calls=%fused_computation.27 | loop fusion | flops 8028160 | bytes 4259840
  120.1 2.2 fusion.34
  122.3 2.2 fusion.32
  126.6 4.0 all-to-all-start.1
  130.6 17.7 %fusion.7 = f32[20,16,128,128]{3,0,2,1:T(8,128)} fusion(bf16[16,20,128,128]{3,2,1,0:T(8,128)(2,1)} %bitcast.229, bf16[20,20]{1,0:T(8,128)(2,1)S(1)} %copy-done), kind=kOutput, calls=%fused_computation.10 | convolution fusion | flops 209715200 | bytes 31458080 | tf_op jit(solution)/shard_map/xcyz,co->xoyz/dot_general | solution.py:121
  149.1 3.9 reshape.183
  152.9 11.7 %fusion.22 = f32[16,32,20,128]{3,1,2,0:T(8,128)S(1)} fusion(f32[16,32,20,32]{3,2,0,1:T(8,128)} %reshape.183, f32[16,128]{1,0:T(8,128)S(1)} %get-tuple-element.33, f32[16,128]{1,0:T(8,128)S(1)} %get-tuple-element.28), kind=kOutput, calls=%fused_computation.35 | convolution fusion | flops 503320576 | bytes 6569984 | tf_op jit(solution)/shard_map/xkcm,mz->xkcz/dot_general | solution.py:137
  164.7 7.8 %fusion.20 = f32[16,32,20,128]{3,1,2,0:T(8,128)S(1)} fusion(f32[16,32,20,32]{3,2,0,1:T(8,128)S(1)} %copy-done.5, f32[16,128]{1,0:T(8,128)S(1)} %get-tuple-element.28, f32[16,128]{1,0:T(8,128)S(1)} %get-tuple-element.27), kind=kOutput, calls=%fused_computation.33 | convolution fusion | flops 503320576 | bytes 6569984 | tf_op jit(solution)/shard_map/xkcm,mz->xkcz/dot_general | solution.py:138
  172.5 8.6 %fusion.41 = f32[128,16,20,128]{3,0,2,1:T(8,128)} fusion(f32[16,32,20,128]{3,1,2,0:T(8,128)S(1)} %fusion.20, f32[16,32,20,128]{3,1,2,0:T(8,128)S(1)} %fusion.22, f32[32,128]{1,0:T(8,128)S(1)} %get-tuple-element.26, f32[32,128]{1,0:T(8,128)S(1)} %get-tuple-element.25), kind=kOutput, calls=%fused_computation.62 | convolution fusion | flops 681615360 | bytes 31490048 | tf_op jit(solution)/shard_map/xkcz,ky->xcyz/dot_general | solution.py:54
  181.0 8.5 %fusion.43 = f32[128,16,20,128]{3,0,2,1:T(8,128)} fusion(f32[16,32,20,128]{3,1,2,0:T(8,128)S(1)} %fusion.20, f32[16,32,20,128]{3,1,2,0:T(8,128)S(1)} %fusion.22, f32[32,128]{1,0:T(8,128)S(1)} %get-tuple-element.26, f32[32,128]{1,0:T(8,128)S(1)} %get-tuple-element.25), kind=kOutput, calls=%fused_computation.63 | convolution fusion | flops 681607168 | bytes 31490048 | tf_op jit(solution)/shard_map/xkcz,ky->xcyz/dot_general | solution.py:53
  189.5 34.4 %fusion.5 = bf16[16,20,128,128]{3,2,1,0:T(8,128)(2,1)} fusion(f32[20,16,128,128]{3,0,2,1:T(8,128)} %fusion.7, f32[128,16,20,128]{3,0,2,1:T(8,128)} %fusion.43, f32[128,16,20,128]{3,0,2,1:T(8,128)} %fusion.41, bf16[1,16,20,128,128]{4,3,2,1,0:T(8,128)(2,1)} %param.6, f32[20]{0:T(128)S(1)} %copy-done.6, f32[16,32,20,128]{3,1,2,0:T(8,128)} %copy-done.4, ...), kind=kOutput, calls=%fused_computation.6 | convolution fusion | flops 762871808 | bytes 94404688 | tf_op jit(solution)/shard_map/xkcz,ky->xcyz/dot_general | solution.py:55
  223.9 5.4 %fusion.110 = f32[64,16,20,128]{3,0,2,1:T(8,128)S(1)} fusion(bf16[16,20,128,128]{3,2,1,0:T(8,128)(2,1)} %fusion.5, f32[128,32]{0,1:T(8,128)S(1)} %get-tuple-element.30, f32[128,32]{0,1:T(8,128)S(1)} %get-tuple-element.29), kind=kOutput, calls=%fused_computation.162 | convolution fusion | flops 671129600 | bytes 21004288 | tf_op jit(solution)/shard_map/xcyz,yk->xckz/dot_general | solution.py:48
  231.0 4.9 fusion.116
  235.8 31.8 %fusion.9 = f32[16,20,64,32]{2,3,1,0:T(8,128)S(1)} fusion(f32[64,16,20,128]{3,0,2,1:T(8,128)} %fusion.116, f32[64,16,20,128]{3,0,2,1:T(8,128)S(1)} %fusion.110, f32[128,16]{0,1:T(8,128)S(1)} %get-tuple-element.31, f32[128,16]{0,1:T(8,128)S(1)} %get-tuple-element.32), kind=kOutput, calls=%fused_computation.13 | convolution fusion | flops 1009258496 | bytes 23609344 | tf_op jit(solution)/shard_map/xckz,zm->xckm/dot_general | solution.py:103
  269.5 3.0 copy.103
  272.5 5.1 %copy.104 = f32[16,32,640]{2,0,1:T(8,128)} copy(f32[16,32,640]{1,2,0:T(8,128)} %bitcast.233) | data formatting | bytes 2621440 | tf_op jit(solution)/shard_map/reshape | solution.py:109
  277.6 6.0 %all-to-all-start.2 = ((f32[16,32,640]{2,0,1:T(8,128)}), f32[16,32,640]{2,0,1:T(8,128)S(1)}, u32[]{:S(2)}, u32[]{:S(2)}) async-start(f32[16,32,640]{2,0,1:T(8,128)} %copy.104), calls=%async_computation.2 | async-start | bytes 2621440 | tf_op jit(solution)/shard_map/all_to_all | solution.py:110
  283.9 17.4 %all-to-all-done.2 = f32[16,32,640]{2,0,1:T(8,128)S(1)} async-done(((f32[16,32,640]{2,0,1:T(8,128)}), f32[16,32,640]{2,0,1:T(8,128)S(1)}, u32[]{:S(2)}, u32[]{:S(2)}) %all-to-all-start.2) | async-done | bytes 1310752 | tf_op jit(solution)/shard_map/all_to_all | solution.py:110
  302.3 2.1 fusion.30
  307.5 6.8 %add_bitcast_fusion = (f32[32,1,20,20,64]{4,0,3,2,1:T(8,128)}, f32[32,1,20,20,64]{4,0,3,2,1:T(8,128)}) fusion(f32[32,64,20]{1,0,2:T(8,128)S(1)} %copy.168, f32[32,64,20]{1,0,2:T(8,128)S(1)} %copy.113, f32[32,64,20]{1,0,2:T(8,128)S(1)} %copy.167, f32[32,64,20]{1,0,2:T(8,128)S(1)} %copy.111), kind=kLoop, calls=%fused_computation.30 | loop fusion | flops 4915200 | bytes 7208960 | tf_op jit(solution)/shard_map/stack | solution.py:83
  314.4 12.3 %pad_maximum_fusion = f32[32,2,20,20,64]{4,0,3,2,1:T(8,128)} fusion(f32[32,1,20,20,64]{4,0,3,2,1:T(8,128)} %get-tuple-element.24, f32[32,1,20,20,64]{4,0,3,2,1:T(8,128)} %get-tuple-element.23), kind=kLoop, calls=%fused_computation.9 | loop fusion | flops 1638400 | bytes 13107200 | tf_op jit(solution)/shard_map/stack | solution.py:83
  328.6 161.5 %all-reduce.3.cloned.1.call-done = f32[32,2,20,20,64]{4,0,3,2,1:T(8,128)} async-done(((f32[32,2,20,20,64]{4,0,3,2,1:T(8,128)}), f32[32,2,20,20,64]{4,0,3,2,1:T(8,128)}) %all-reduce.3.cloned.1.call-update) | async-done | bytes 6553616
  490.1 2.2 constant_dynamic-slice_fusion
  (76 shorter events, 21.8 us)
Async XLA Ops:
  6.5 124.0 %copy-start = (bf16[20,20]{1,0:T(8,128)(2,1)S(1)}, bf16[20,20]{1,0:T(8,128)(2,1)}, u32[]{:S(2)}) copy-start(bf16[20,20]{1,0:T(8,128)(2,1)} %param.8) | copy-start | bytes 2404
  6.5 90.8 %all-gather.2.cloned.1.call-start = ((), (), s32[]{:S(2)}) async-start(), calls=%async_computation.3 | async-start | bytes 6963200 | tf_op jit(solution)/shard_map/all_gather | solution.py:124
  6.5 10.5 %slice-start = ((s8[10485760]{0:T(1024)(128)(4,1)}), s8[2097152]{0:T(1024)(128)(4,1)S(1)}, s32[]{:S(2)}) async-start(s8[10485760]{0:T(1024)(128)(4,1)} %bitcast.230), calls=%async_computation.5 | async-start | bytes 4194304
  7.5 9.5 %slice-start.1 = ((s8[10485760]{0:T(1024)(128)(4,1)}), s8[4194304]{0:T(1024)(128)(4,1)S(1)}, s32[]{:S(2)}) async-start(s8[10485760]{0:T(1024)(128)(4,1)} %bitcast.230), calls=%async_computation.6 | async-start | bytes 8388608
  7.5 9.5 %slice-start.2 = ((s8[10485760]{0:T(1024)(128)(4,1)}), s8[4194304]{0:T(1024)(128)(4,1)S(1)}, s32[]{:S(2)}) async-start(s8[10485760]{0:T(1024)(128)(4,1)} %bitcast.230), calls=%async_computation.7 | async-start | bytes 8388608
  63.3 27.9 %all-to-all-start = ((f32[16,32,640]{2,0,1:T(8,128)}), f32[16,32,640]{2,0,1:T(8,128)S(1)}, u32[]{:S(2)}, u32[]{:S(2)}) async-start(f32[16,32,640]{2,0,1:T(8,128)} %copy.82), calls=%async_computation | async-start | bytes 2621440 | tf_op jit(solution)/shard_map/all_to_all | solution.py:110
  126.6 22.3 %all-to-all-start.1 = ((f32[128,4,640]{2,1,0:T(4,128)}), f32[128,4,640]{2,1,0:T(4,128)S(1)}, u32[]{:S(2)}, u32[]{:S(2)}) async-start(f32[128,4,640]{2,1,0:T(4,128)} %copy.95), calls=%async_computation.1 | async-start | bytes 2621440 | tf_op jit(solution)/shard_map/all_to_all | solution.py:134
  152.9 11.7 %copy-start.5 = (f32[16,32,20,32]{3,2,0,1:T(8,128)S(1)}, f32[16,32,20,32]{3,2,0,1:T(8,128)}, u32[]{:S(2)}) copy-start(f32[16,32,20,32]{3,2,0,1:T(8,128)} %reshape.183) | copy-start | bytes 3932164
  164.7 16.4 %copy-start.3 = (f32[16,32,20,128]{3,1,2,0:T(8,128)}, f32[16,32,20,128]{3,1,2,0:T(8,128)S(1)}, u32[]{:S(2)}) copy-start(f32[16,32,20,128]{3,1,2,0:T(8,128)S(1)} %fusion.22) | copy-start | bytes 15728644
  172.5 8.6 %copy-start.4 = (f32[16,32,20,128]{3,1,2,0:T(8,128)}, f32[16,32,20,128]{3,1,2,0:T(8,128)S(1)}, u32[]{:S(2)}) copy-start(f32[16,32,20,128]{3,1,2,0:T(8,128)S(1)} %fusion.20) | copy-start | bytes 15728644
  181.0 8.5 %copy-start.6 = (f32[20]{0:T(128)S(1)}, f32[20]{0:T(128)}, u32[]{:S(2)}) copy-start(f32[20]{0:T(128)} %param.9) | copy-start | bytes 244
  223.9 7.0 %copy-start.2 = (bf16[16,20,128,128]{3,2,1,0:T(8,128)(2,1)S(1)}, bf16[16,20,128,128]{3,2,1,0:T(8,128)(2,1)}, u32[]{:S(2)}) copy-start(bf16[16,20,128,128]{3,2,1,0:T(8,128)(2,1)} %fusion.5) | copy-start | bytes 31457284
  277.6 23.7 %all-to-all-start.2 = ((f32[16,32,640]{2,0,1:T(8,128)}), f32[16,32,640]{2,0,1:T(8,128)S(1)}, u32[]{:S(2)}, u32[]{:S(2)}) async-start(f32[16,32,640]{2,0,1:T(8,128)} %copy.104), calls=%async_computation.2 | async-start | bytes 2621440 | tf_op jit(solution)/shard_map/all_to_all | solution.py:110
  283.6 206.5 %all-reduce.3.cloned.1.call-start = ((), (), s32[]{:S(2)}) async-start(), calls=%async_computation.4 | async-start | bytes 26214400
  326.7 167.1 %copy-start.1 = (bf16[20,20]{1,0:T(8,128)(2,1)S(1)}, bf16[20,20]{1,0:T(8,128)(2,1)}, u32[]{:S(2)}) copy-start(bf16[20,20]{1,0:T(8,128)(2,1)} %param.8) | copy-start | bytes 2404
  326.7 0.7 copy-start.7
Sparse Core Ops, SparseCore 0:
  9.0 47.0 all-gather.1
  326.8 163.1 all-reduce.2
where the time goes:
time: 509 us; the launch traced here: 501 us
  waiting for transfers between devices  199 us (39%)
  matrix products  189 us (37%)
  local copies, waits for them, and re-layouts  47.6 us (9%)
  other arithmetic  31.3 us (6%)
  starting transfers between devices  18.8 us (4%)
  between operations  14.7 us (3%)
    unnamed x3, waiting for transfers between devices  162 us
    dot_general x2, matrix products, forward_modes(): along_yz = jnp.einsum('xckz,zm->xckm', along_y, table_z, precision=highest)  63.2 us
    all_to_all x2, waiting for transfers between devices, forward_modes(): lax.all_to_all(packed, 'mp', split_axis=1, concat_axis=0, tiled=True)  36.4 us
    dot_general x1, matrix products, three_pass(): jnp.einsum(form, data_lo, table_pair[0], preferred_element_type=jnp.float32)  34.4 us
    another operation x2, other arithmetic, grad_term(): return jnp.stack([grad_re, grad_im], axis=-4)  19.1 us
    dot_general x1, matrix products, shards(): jnp.einsum('xcyz,co->xoyz', volume, conv_weight, preferred_element_type=j...  17.7 us
    slice x1, local copies, waits for them, and re-layouts, mix_modes(): real_w = weights[..., 0, :, :, :]  15 us
    dot_general x2, matrix products, two_pass(): jnp.einsum(form, data_bf, table_pair[1], preferred_element_type=jnp.float32)  14.9 us
  transfers between devices with their start and end apart: 5, of which 4 were waited for; matrix products, arithmetic and copies ran while one was open for 16% of the time, Pallas kernels for 0%

commit v1 on v0

v1 whole, which is shorter than its diff:
```python
import functools

import jax
import jax.numpy as jnp
import ml_dtypes
import numpy as np
from jax import lax
from jax.experimental import pallas as pl
from jax.experimental.pallas import tpu as pltpu
from jax.sharding import PartitionSpec as P

X = 128
Y = 128
Z = 128
C = 20
KX = 32
KY = 32
KZ = 16
DP = 16
MP = 8
XP = 8
G = 5
GK = 20
GA = 10

bf16 = jnp.bfloat16
f32 = jnp.float32
np_bf16 = ml_dtypes.bfloat16

INV_ROOT_TWO = 0.7071067811865476
INV_ROOT_TWO_PI = 0.3989422804014327


def kept(count, length):
    return np.concatenate([np.arange(count // 2), np.arange(length - count // 2, length)])


def angles(modes, length):
    return 2.0 * np.pi / length * ((modes[:, None] * np.arange(length)[None, :]) % length)


def hi_lo(table):
    upper = table.astype(np_bf16)
    lower = (table - upper.astype(np.float64)).astype(np_bf16)
    return upper, lower


def z_scales():
    candidates = 1.0 + np.arange(512) / 512
    scales = []
    for row in angles(np.arange(KZ), Z):
        values = np.concatenate([np.cos(row), np.sin(row)])[None, :] * candidates[:, None]
        off = ((values.astype(np_bf16).astype(np.float64) - values) ** 2).sum(1) / (values**2).sum(1)
        scales.append(candidates[int(np.argmin(off))])
    return np.array(scales)


@functools.cache
def tables():
    scale = z_scales()
    weight = np.where(np.arange(KZ) == 0, 1.0, 2.0) / (X * Y * Z)
    phase_z = angles(np.arange(KZ), Z)
    cos_z, sin_z = np.cos(phase_z), np.sin(phase_z)
    forward_z = np.zeros((8, Z, 2, 8, KZ))
    inverse_z = np.zeros((4, 2, 8, KZ, 2, Z))
    for q in range(8):
        forward_z[q, :, 0, q, :] = (cos_z * scale[:, None]).T
        forward_z[q, :, 1, q, :] = (sin_z * scale[:, None]).T
        inverse_z[q // 2, 0, q, :, q % 2, :] = cos_z * scale[:, None]
        inverse_z[q // 2, 1, q, :, q % 2, :] = -sin_z * scale[:, None]
    unscale = np.tile(1.0 / scale, 16)[None, :]
    unscale_back = np.tile(weight / scale, 16)[None, :]
    unscale_inverse = np.tile(weight / scale, 8)[None, :]
    phase_y = angles(kept(KY, Y), Y)
    cos_y, sin_y = np.cos(phase_y), np.sin(phase_y)
    forward_y = np.zeros((KY, 2, 2, Y))
    forward_y[:, 0, 0], forward_y[:, 0, 1] = cos_y, -sin_y
    forward_y[:, 1, 0], forward_y[:, 1, 1] = -sin_y, -cos_y
    forward_y = np.concatenate(hi_lo(forward_y.reshape(64, 256)), axis=0)
    inverse_y = np.zeros((2, Y, KY, 2))
    inverse_y[0, :, :, 0], inverse_y[0, :, :, 1] = cos_y.T, -sin_y.T
    inverse_y[1, :, :, 0], inverse_y[1, :, :, 1] = sin_y.T, cos_y.T
    inverse_y = np.concatenate(hi_lo(inverse_y.reshape(256, 64)), axis=1)
    phase_x = angles(kept(KX, X), X).reshape(16, 2, 8, 8, 2)
    cos_x, sin_x = np.cos(phase_x), np.sin(phase_x)
    forward_x = np.zeros((2, 2, 2, 16, 8, 2, 8))
    inverse_x = np.zeros((2, 8, 2, 8, 2, 2, 16))
    cos_f = np.transpose(cos_x, (4, 1, 0, 2, 3))
    sin_f = np.transpose(sin_x, (4, 1, 0, 2, 3))
    forward_x[:, :, 0, :, :, 0, :] = cos_f
    forward_x[:, :, 0, :, :, 1, :] = sin_f
    forward_x[:, :, 1, :, :, 0, :] = -sin_f
    forward_x[:, :, 1, :, :, 1, :] = cos_f
    cos_i = np.transpose(cos_x, (4, 2, 3, 1, 0))
    sin_i = np.transpose(sin_x, (4, 2, 3, 1, 0))
    inverse_x[:, :, 0, :, :, 0, :] = cos_i
    inverse_x[:, :, 0, :, :, 1, :] = -sin_i
    inverse_x[:, :, 1, :, :, 0, :] = sin_i
    inverse_x[:, :, 1, :, :, 1, :] = cos_i
    forward_x = np.concatenate(hi_lo(forward_x.reshape(128, 128)), axis=1)
    inverse_x = np.concatenate(hi_lo(inverse_x.reshape(256, 64)), axis=1)
    spread = np.zeros((2, 4, KZ, 4, 2, 4, KZ))
    for channel in range(4):
        for place in range(4):
            for b in range(2):
                spread[b, channel, np.arange(KZ), channel, b, place, np.arange(KZ)] = 1.0
    spread = spread.reshape(128, 512)
    spread = np.concatenate([spread, spread], axis=0)
    place = np.zeros((4, 4, KZ, 2, 2, 4, KZ))
    for o in range(4):
        for kyl in range(4):
            place[o, kyl, np.arange(KZ), kyl // 2, kyl % 2, o, np.arange(KZ)] = 1.0
    return dict(
        forward_z=forward_z.reshape(4, 256, 256).astype(np_bf16),
        inverse_z=inverse_z.reshape(4, 256, 256).astype(np_bf16),
        unscale=unscale.astype(np.float32),
        unscale_back=unscale_back.astype(np.float32),
        unscale_inverse=unscale_inverse.astype(np.float32),
        forward_y=forward_y,
        inverse_y=inverse_y,
        forward_x=forward_x,
        inverse_x=inverse_x,
        spread=spread.astype(np_bf16),
        place=place.reshape(256, 256).astype(np_bf16),
    )


def mm(a, b):
    return jnp.dot(a, b, preferred_element_type=f32)


def analyse(lhs_of_pair, fz_ref, fy_ref, un_ref, modes_ref, step):
    total = mm(lhs_of_pair(0), fz_ref[0])
    for pair in range(1, 4):
        total = total + mm(lhs_of_pair(pair), fz_ref[pair])
    total = total * un_ref[...]
    for g in range(G):
        part = total[g * Y : (g + 1) * Y]
        both = jnp.concatenate([part[:, :128], part[:, 128:]], axis=0)
        upper = both.astype(bf16)
        lower = (both - upper.astype(f32)).astype(bf16)
        out = mm(fy_ref[...], jnp.concatenate([upper, lower], axis=1))
        modes = out[:64, :128] + out[64:, :128] + out[:64, 128:]
        for j in range(MP):
            modes_ref[pl.ds(j * 320 + g * 64 + step, 8, stride=8), :] = modes[j * 8 : (j + 1) * 8]


def analyse_kernel(field_ref, fz_ref, fy_ref, un_ref, out_ref, modes_ref):
    step = pl.program_id(0)

    def lhs(pair):
        xl, c4 = pair // 2, 2 * (pair % 2)
        rows = [
            jnp.concatenate(
                [field_ref[0, xl, 4 * g + c4], field_ref[0, xl, 4 * g + c4 + 1]], axis=1
            )
            for g in range(G)
        ]
        return jnp.concatenate(rows, axis=0)

    analyse(lhs, fz_ref, fy_ref, un_ref, modes_ref, step)

    @pl.when(step == XP - 1)
    def _():
        out_ref[...] = modes_ref[...].astype(bf16)


def full(shape):
    zeros = (0,) * len(shape)
    return pl.BlockSpec(shape, lambda *_: zeros, pipeline_mode=pl.Buffered(1))


def analyse_call(fields, t):
    return pl.pallas_call(
        analyse_kernel,
        out_shape=jax.ShapeDtypeStruct((2560, 128), bf16),
        grid=(XP,),
        in_specs=[
            pl.BlockSpec((1, 2, C, Y, Z), lambda i: (0, i, 0, 0, 0)),
            full((4, 256, 256)),
            full((128, 256)),
            full((1, 256)),
        ],
        out_specs=pl.BlockSpec((2560, 128), lambda i: (0, 0)),
        scratch_shapes=[pltpu.VMEM((2560, 128), f32)],
        compiler_params=pltpu.CompilerParams(
            dimension_semantics=("arbitrary",), vmem_limit_bytes=60 << 20
        ),
        name="analyse",
    )(fields, t["forward_z"], t["forward_y"], t["unscale"])


def gelu_slope(values):
    return (
        0.5 * (1.0 + lax.erf(values * INV_ROOT_TWO))
        + values * jnp.exp(-0.5 * values * values) * INV_ROOT_TWO_PI
    )


def slab_kernel(
    field_ref, cot_ref, mixed_ref, conv_ref, bias_ref, iy_ref, iz_ref, uni_ref, fz_ref, fy_ref, un_ref,
    out_ref, modes_ref, mixed_f32, conv_out, wave_ref, delta_ref,
):
    step = pl.program_id(0)

    @pl.when(step == 0)
    def _():
        mixed_f32[...] = mixed_ref[...].astype(f32)

    for g in range(G):
        rows = [mixed_f32[pl.ds(j * 320 + g * 64 + step, 8, stride=8), :] for j in range(MP)]
        part = jnp.concatenate(rows, axis=0).astype(bf16)
        wave = mm(iy_ref[...], jnp.concatenate([part, part], axis=0))
        wave = (wave * uni_ref[...]).astype(bf16)
        wave_ref[g * Y : (g + 1) * Y, :128] = wave[:Y]
        wave_ref[g * Y : (g + 1) * Y, 128:] = wave[Y:]

    for xl in range(2):
        for yp in range(4):
            right = jnp.concatenate(
                [
                    field_ref[0, xl, :, yp * 32 + h * 16 : yp * 32 + (h + 1) * 16, :].reshape(320, Z)
                    for h in range(2)
                ],
                axis=1,
            )
            out = mm(conv_ref[...], right)
            for h in range(2):
                conv_out[:, yp * 32 + h * 16 : yp * 32 + (h + 1) * 16, :] = out[
                    :, h * 128 : (h + 1) * 128
                ].reshape(C, 16, Z)
        for pair in (2 * xl, 2 * xl + 1):
            spectral = mm(wave_ref[...], iz_ref[pair])
            for g in range(G):
                for h in range(2):
                    channel = 4 * g + 2 * (pair % 2) + h
                    pre = (
                        spectral[g * Y : (g + 1) * Y, h * 128 : (h + 1) * 128]
                        + conv_out[channel]
                        + bias_ref[channel]
                    )
                    delta = cot_ref[0, xl, channel].astype(f32) * gelu_slope(pre)
                    delta_ref[pair, g * Y : (g + 1) * Y, h * 128 : (h + 1) * 128] = delta.astype(bf16)

    analyse(lambda pair: delta_ref[pair], fz_ref, fy_ref, un_ref, modes_ref, step)

    @pl.when(step == XP - 1)
    def _():
        out_ref[...] = modes_ref[...].astype(bf16)


def slab_call(fields, cotangent, mixed, conv, bias, t):
    return pl.pallas_call(
        slab_kernel,
        out_shape=jax.ShapeDtypeStruct((2560, 128), bf16),
        grid=(XP,),
        in_specs=[
            pl.BlockSpec((1, 2, C, Y, Z), lambda i: (0, i, 0, 0, 0)),
            pl.BlockSpec((1, 2, C, Y, Z), lambda i: (0, i, 0, 0, 0)),
            full((2560, 128)),
            full((320, 320)),
            pl.BlockSpec(memory_space=pltpu.SMEM),
            full((256, 128)),
            full((4, 256, 256)),
            full((1, 128)),
            full((4, 256, 256)),
            full((128, 256)),
            full((1, 256)),
        ],
        out_specs=pl.BlockSpec((2560, 128), lambda i: (0, 0)),
        scratch_shapes=[
            pltpu.VMEM((2560, 128), f32),
            pltpu.VMEM((2560, 128), f32),
            pltpu.VMEM((C, Y, Z), f32),
            pltpu.VMEM((640, 256), bf16),
            pltpu.VMEM((4, 640, 256), bf16),
        ],
        compiler_params=pltpu.CompilerParams(
            dimension_semantics=("arbitrary",), vmem_limit_bytes=60 << 20
        ),
        name="slab",
    )(
        fields, cotangent, mixed, conv, bias, t["inverse_y"], t["inverse_z"],
        t["unscale_inverse"], t["forward_z"], t["forward_y"], t["unscale_back"],
    )


def small_call(kernel, name, out_shape, scratch, *args):
    return pl.pallas_call(
        kernel,
        out_shape=out_shape,
        scratch_shapes=scratch,
        compiler_params=pltpu.CompilerParams(vmem_limit_bytes=60 << 20),
        name=name,
    )(*args)


def lower_half():
    return lax.broadcasted_iota(jnp.int32, (64, 128), 1) < 64


def forward_x_kernel(in_ref, fx_ref, out_ref):
    low = lower_half()
    for gk in range(GA):
        cols = []
        for b in range(2):
            row = (2 * gk + b) * 16
            cols.append(jnp.concatenate([in_ref[j * 320 + row : j * 320 + row + 16, :] for j in range(8)], axis=0))
        right = jnp.concatenate(cols, axis=1)
        out = mm(fx_ref[...], jnp.concatenate([right, right], axis=0))
        first = jnp.where(low, out[:64, :128], out[64:, 128:])
        second = jnp.where(low, out[:64, 128:], out[64:, :128])
        res = first + pltpu.roll(second, 64, 1)
        for r in range(4):
            out_ref[pl.ds(r * GA + gk, 16, stride=40), :] = res[r * 16 : (r + 1) * 16]


def inverse_x_kernel(in_ref, ix_ref, out_ref, wide_ref):
    wide_ref[...] = in_ref[...].astype(f32)
    low = lax.broadcasted_iota(jnp.int32, (128, 128), 1) < 64
    for gk in range(GA):
        rows = [wide_ref[pl.ds(r * GA + gk, 16, stride=40), :] for r in range(4)]
        part = jnp.concatenate(rows, axis=0).astype(bf16)
        out = mm(ix_ref[...], jnp.concatenate([part, part], axis=0))
        first = jnp.where(low, out[:128], pltpu.roll(out[128:], 64, 1)).astype(bf16)
        second = jnp.where(low, pltpu.roll(out[:128], 64, 1), out[128:]).astype(bf16)
        for b, value in enumerate((first, second)):
            row = (2 * gk + b) * 16
            for j in range(8):
                out_ref[j * 320 + row : j * 320 + row + 16, :] = value[j * 16 : (j + 1) * 16]


def weight_kernel(w_ref, place_ref, out_ref, wide_ref):
    wide_ref[...] = w_ref[...].astype(f32)
    cols = [wide_ref[pl.ds(o, 400, stride=4), :].astype(bf16) for o in range(4)]
    out = mm(jnp.concatenate(cols, axis=1), place_ref[...])
    out_ref[0] = out[:, :128]
    out_ref[1] = out[:, 128:]


def spread_channels(in_ref, spread_ref, wide_ref):
    for r in range(40):
        rows = in_ref[pl.ds(r, 16, stride=40), :]
        upper = rows.astype(bf16)
        lower = (rows - upper.astype(f32)).astype(bf16)
        wide_ref[r * 16 : (r + 1) * 16, :] = jnp.concatenate([upper, lower], axis=1)


def mix_kernel(in_ref, spread_ref, w_ref, out_ref, wide_ref, chan_ref, mixed_ref):
    spread_channels(in_ref, spread_ref, wide_ref)
    chan_ref[...] = mm(wide_ref[...], spread_ref[...])
    for kxl in range(2):
        for kya in range(2):
            real = [jnp.zeros((16, 128), f32) for _ in range(G)]
            imag = [jnp.zeros((16, 128), f32) for _ in range(G)]
            for c in range(C):
                row = (kxl * 20 + (c // 4) * 2 + kya) * 16
                lanes = (c % 4) * 128
                s_re = chan_ref[row : row + 16, lanes : lanes + 128]
                s_im = chan_ref[row + 160 : row + 176, lanes : lanes + 128]
                for go in range(G):
                    line = kxl * 200 + c * G + go
                    w_re = w_ref[kya, line : line + 1, :]
                    w_im = w_ref[kya, line + 100 : line + 101, :]
                    real[go] = real[go] + (s_re * w_re - s_im * w_im)
                    imag[go] = imag[go] + (s_re * w_im + s_im * w_re)
            for go in range(G):
                row = kxl * 20 + go * 2 + kya
                mixed_ref[pl.ds(row, 16, stride=40), :] = real[go]
                mixed_ref[pl.ds(row + 10, 16, stride=40), :] = imag[go]
    out_ref[...] = mixed_ref[...].astype(bf16)


def grad_kernel(s_ref, b_ref, spread_ref, out_ref, wide_ref, chan_ref):
    spread_channels(s_ref, spread_ref, wide_ref)
    chan_ref[...] = mm(wide_ref[...], spread_ref[...])
    for kxl in range(2):
        for kya in range(2):
            b_re = [b_ref[pl.ds(kxl * 20 + g * 2 + kya, 16, stride=40), :] for g in range(G)]
            b_im = [b_ref[pl.ds(kxl * 20 + g * 2 + kya + 10, 16, stride=40), :] for g in range(G)]
            for c in range(C):
                row = (kxl * 20 + (c // 4) * 2 + kya) * 16
                lanes = (c % 4) * 128
                s_re = chan_ref[row : row + 16, lanes : lanes + 128]
                s_im = chan_ref[row + 160 : row + 176, lanes : lanes + 128]
                for go in range(G):
                    line = kxl * 200 + c * G + go
                    real = s_re * b_re[go] + s_im * b_im[go]
                    imag = s_re * b_im[go] - s_im * b_re[go]
                    out_ref[kya, line : line + 1, :] = jnp.sum(real, axis=0, keepdims=True)
                    out_ref[kya, line + 100 : line + 101, :] = jnp.sum(imag, axis=0, keepdims=True)


def exchange(values, axis, count):
    blocks = values.reshape(count, -1, 128)
    return lax.all_to_all(blocks, axis, split_axis=0, concat_axis=0, tiled=True).reshape(-1, 128)


def shards(fields, cotangent, spectral_weight, conv_weight, conv_bias):
    t = {name: jnp.asarray(value) for name, value in tables().items()}
    conv = (
        conv_weight.T[:, None, :, None] * jnp.eye(16, dtype=bf16)[None, :, None, :]
    ).reshape(320, 320)

    def to_kx(modes):
        moved = exchange(modes, "mp", MP)
        part = small_call(
            forward_x_kernel, "forward_x", jax.ShapeDtypeStruct((640, 128), f32), [], moved, t["forward_x"]
        )
        return exchange(part, "dp", DP)

    weights = small_call(
        weight_kernel, "weights", jax.ShapeDtypeStruct((2, 400, 128), f32),
        [pltpu.VMEM((1600, 64), f32)], spectral_weight.reshape(1600, 64), t["place"],
    )
    spectra = to_kx(analyse_call(fields, t))
    mixed = small_call(
        mix_kernel, "mix", jax.ShapeDtypeStruct((640, 128), bf16),
        [pltpu.VMEM((640, 256), bf16), pltpu.VMEM((640, 512), f32), pltpu.VMEM((640, 128), f32)],
        spectra, t["spread"], weights,
    )
    slabs = small_call(
        inverse_x_kernel, "inverse_x", jax.ShapeDtypeStruct((2560, 128), bf16),
        [pltpu.VMEM((640, 128), f32)], exchange(mixed, "dp", DP), t["inverse_x"],
    )
    back_modes = slab_call(fields, cotangent, exchange(slabs, "mp", MP), conv, conv_bias, t)
    back = to_kx(back_modes)
    grad = small_call(
        grad_kernel, "grad", jax.ShapeDtypeStruct((2, 400, 128), f32),
        [pltpu.VMEM((640, 256), bf16), pltpu.VMEM((640, 512), f32)], spectra, back, t["spread"],
    )
    grad = grad.reshape(2, 2, 2, C, G, 2, 4, KZ)
    return jnp.transpose(grad, (1, 2, 3, 4, 6, 0, 5, 7)).reshape(2, 2, C, C, 64)


def solution(mesh):
    return jax.shard_map(
        shards,
        mesh=mesh,
        in_specs=(
            P("dp", "mp", None, None, None),
            P("dp", "mp", None, None, None),
            P("dp", None, None, None, "mp"),
            P(),
            P(),
        ),
        out_specs=P("dp", None, None, None, "mp"),
        check_vma=False,
    )
```

time: 509 us -> 154 us (0.30); the launches traced: 501 us -> 153 us
  matrix products: 189 us -> 0 us
  waiting for transfers between devices: 199 us -> 14.2 us
  blocking collectives: 0 us -> 61.1 us
  Pallas kernels: 0 us -> 49.9 us
  other arithmetic: 31.3 us -> 0.2 us
  local copies, waits for them, and re-layouts: 47.6 us -> 16.7 us
  between operations: 14.7 us -> 0.07 us
  starting transfers between devices: 18.8 us -> 10.5 us
    dot_general x18 -> x0, matrix products: 189 us -> none  [the longest x2 63.2 us: forward_modes(): along_yz = jnp.einsum('xckz,zm->xckm', along_y, table_z, precision=highest)]
    unnamed x3 -> x0, waiting for transfers between devices: 162 us -> none
    all_to_all x0 -> x4, blocking collectives: none -> 61.1 us  [exchange(): lax.all_to_all(blocks, axis, split_axis=0, concat_axis=0, tiled=True)]
    pallas_call x0 -> x8, Pallas kernels: none -> 49.9 us  [the longest x1 23.9 us: slab_call(): pl.pallas_call(slab_kernel, out_shape=jax.ShapeDtypeStruct((2560, 128), b...]
    another operation x9 -> x0, other arithmetic: 23 us -> none  [the longest x2 19.1 us: grad_term(): return jnp.stack([grad_re, grad_im], axis=-4)]
    all_to_all x3 -> x2, waiting for transfers between devices: 37 us -> 14.2 us  [exchange(): lax.all_to_all(blocks, axis, split_axis=0, concat_axis=0, tiled=True)]
    slice x1 -> x0, local copies, waits for them, and re-layouts: 15 us -> none  [mix_modes(): real_w = weights[..., 0, :, :, :]]
    all_to_all x3 -> x2, starting transfers between devices: 18.6 us -> 10.5 us  [exchange(): lax.all_to_all(blocks, axis, split_axis=0, concat_axis=0, tiled=True)]
  transfers between devices with their start and end apart: 5 -> 2, of which waited for: 4 -> 2; matrix products, arithmetic and copies ran while one was open for 16% -> 2% of each run, Pallas kernels for 0% -> 1%
where the time goes in v1:
time: 154 us; the launch traced here: 153 us
  blocking collectives  61.1 us (40%)
  Pallas kernels  49.9 us (32%)
  local copies, waits for them, and re-layouts  16.7 us (11%)
  waiting for transfers between devices  14.2 us (9%)
  starting transfers between devices  10.5 us (7%)
    all_to_all x4, blocking collectives, exchange(): lax.all_to_all(blocks, axis, split_axis=0, concat_axis=0, tiled=True)  61.1 us
    pallas_call x1, Pallas kernels, slab_call(): pl.pallas_call(slab_kernel, out_shape=jax.ShapeDtypeStruct((2560, 128), b...  23.9 us
    pallas_call x6, Pallas kernels, small_call(): pl.pallas_call(kernel, out_shape=out_shape, scratch_shapes=scratch, compi...  15.6 us
    all_to_all x2, waiting for transfers between devices, exchange(): lax.all_to_all(blocks, axis, split_axis=0, concat_axis=0, tiled=True)  14.2 us
    all_to_all x2, starting transfers between devices, exchange(): lax.all_to_all(blocks, axis, split_axis=0, concat_axis=0, tiled=True)  10.5 us
    pallas_call x1, Pallas kernels, analyse_call(): pl.pallas_call(analyse_kernel, out_shape=jax.ShapeDtypeStruct((2560, 128)...  10.4 us
    reshape x1, local copies, waits for them, and re-layouts, shards(): return jnp.transpose(grad, (1, 2, 3, 4, 6, 0, 5, 7)).reshape(2, 2, C, C, 64)  5.37 us
    transpose x1, local copies, waits for them, and re-layouts, shards(): return jnp.transpose(grad, (1, 2, 3, 4, 6, 0, 5, 7)).reshape(2, 2, C, C, 64)  3.5 us
  transfers between devices with their start and end apart: 2, of which 2 were waited for; matrix products, arithmetic and copies ran while one was open for 2% of the time, Pallas kernels for 1%

profile of v1, /device:TPU:1, one launch (start us, length us, event | category | flops | bytes accessed | tf_op | source)
XLA Modules:
  0.0 152.8 jit_solution(8885676288725693406)
XLA Ops:
  0.0 10.4 %analyse.1 = bf16[2560,128]{1,0:T(8,128)(2,1)} custom-call(bf16[1,16,20,128,128]{4,3,2,1,0:T(8,128)(2,1)} %field_ref.3, bf16[4,256,256]{2,1,0:T(8,128)(2,1)} %constant.22.clone.fz_ref, bf16[128,256]{1,0:T(8,128)(2,1)} %constant.27.clone.fy_ref, f32[1,256]{1,0:T(1,128)} %constant.24.clone.un_ref), custom_call_target="tpu_custom_call" | custom-call | tf_op jit(solution)/shard_map/analyse/pallas_call | solution.py:174
  10.4 0.0 copy-start.2
  10.4 20.1 %all_to_all.30 = bf16[8,320,128]{2,1,0:T(8,128)(2,1)} all-to-all(bf16[8,320,128]{2,1,0:T(8,128)(2,1)} %bitcast.19), channel_id=1, replica_groups=mesh['dp'=16,'mp'=8] {'mp'}, dimensions={0} | all-to-all | bytes 1310720 | tf_op jit(solution)/shard_map/all_to_all | solution.py:396
  30.5 2.2 %forward_x.2 = f32[640,128]{1,0:T(8,128)} custom-call(bf16[2560,128]{1,0:T(8,128)(2,1)} %bitcast.22, bf16[128,256]{1,0:T(8,128)(2,1)} %constant.29.clone.fx_ref), custom_call_target="tpu_custom_call" | custom-call | tf_op jit(solution)/shard_map/forward_x/pallas_call | solution.py:289
  32.7 7.0 %all-to-all-start.1 = ((f32[16,40,128]{2,1,0:T(8,128)}), f32[16,40,128]{2,1,0:T(8,128)S(1)}, u32[]{:S(2)}, u32[]{:S(2)}) async-start(f32[16,40,128]{2,1,0:T(8,128)} %bitcast.25), calls=%async_computation.1 | async-start | bytes 655360 | tf_op jit(solution)/shard_map/all_to_all | solution.py:396
  39.7 0.0 copy-done.2
  39.7 0.0 copy-start.3
  39.7 0.1 copy.20
  39.8 0.9 reshape.62.w_ref
  40.7 2.0 %weights.1.w_ref = f32[2,400,128]{2,1,0:T(8,128)} custom-call(bf16[1600,64]{1,0:T(8,128)(2,1)} %reshape.62.w_ref, bf16[256,256]{1,0:T(8,128)(2,1)} %constant.32.clone.place_ref), custom_call_target="tpu_custom_call" | custom-call | tf_op jit(solution)/shard_map/weights/pallas_call | solution.py:289
  42.8 4.6 %all-to-all-done.1 = f32[16,40,128]{2,1,0:T(8,128)S(1)} async-done(((f32[16,40,128]{2,1,0:T(8,128)}), f32[16,40,128]{2,1,0:T(8,128)S(1)}, u32[]{:S(2)}, u32[]{:S(2)}) %all-to-all-start.1) | async-done | bytes 327712 | tf_op jit(solution)/shard_map/all_to_all | solution.py:396
  47.4 0.0 copy-start
  47.4 0.7 copy-done
  48.1 3.2 %mix.1 = bf16[640,128]{1,0:T(8,128)(2,1)} custom-call(f32[640,128]{1,0:T(8,128)} %bitcast.17, bf16[256,512]{1,0:T(8,128)(2,1)} %constant.31.clone.spread_ref, f32[2,400,128]{2,1,0:T(8,128)} %weights.1.w_ref), custom_call_target="tpu_custom_call" | custom-call | tf_op jit(solution)/shard_map/mix/pallas_call | solution.py:289
  51.3 11.3 %all_to_all.31 = bf16[16,40,128]{2,1,0:T(8,128)(2,1)} all-to-all(bf16[16,40,128]{2,1,0:T(8,128)(2,1)} %bitcast.29), channel_id=1, replica_groups=mesh['dp'=16,'mp'=8] {'dp'}, dimensions={0} | all-to-all | bytes 327680 | tf_op jit(solution)/shard_map/all_to_all | solution.py:396
  62.6 2.2 %inverse_x.1 = bf16[2560,128]{1,0:T(8,128)(2,1)} custom-call(bf16[640,128]{1,0:T(8,128)(2,1)} %bitcast.28, bf16[256,128]{1,0:T(8,128)(2,1)} %constant.30.clone.ix_ref), custom_call_target="tpu_custom_call" | custom-call | tf_op jit(solution)/shard_map/inverse_x/pallas_call | solution.py:289
  64.8 3.5 %all-to-all-start.3 = ((bf16[8,320,128]{2,1,0:T(8,128)(2,1)}), bf16[8,320,128]{2,1,0:T(8,128)(2,1)S(1)}, u32[]{:S(2)}, u32[]{:S(2)}) async-start(bf16[8,320,128]{2,1,0:T(8,128)(2,1)} %bitcast.20), calls=%async_computation.3 | async-start | bytes 1310720 | tf_op jit(solution)/shard_map/all_to_all | solution.py:396
  68.4 0.0 copy-done.3
  68.4 0.1 copy.21
  68.5 0.2 broadcast_multiply_fusion
  68.7 1.8 %mul.20.conv_ref = bf16[320,320]{1,0:T(8,128)(2,1)} reshape(bf16[20,16,20,16]{3,2,1,0:T(8,128)(2,1)S(1)} %broadcast_multiply_fusion) | data formatting | bytes 409600 | tf_op jit(solution)/shard_map/mul | solution.py:402
  70.5 9.6 %all-to-all-done.3 = bf16[8,320,128]{2,1,0:T(8,128)(2,1)S(1)} async-done(((bf16[8,320,128]{2,1,0:T(8,128)(2,1)}), bf16[8,320,128]{2,1,0:T(8,128)(2,1)S(1)}, u32[]{:S(2)}, u32[]{:S(2)}) %all-to-all-start.3) | async-done | bytes 655392 | tf_op jit(solution)/shard_map/all_to_all | solution.py:396
  80.1 0.0 copy-start.1
  80.1 0.8 copy-done.1
  81.0 23.9 %slab.1 = bf16[2560,128]{1,0:T(8,128)(2,1)} custom-call(bf16[1,16,20,128,128]{4,3,2,1,0:T(8,128)(2,1)} %field_ref.3, bf16[1,16,20,128,128]{4,3,2,1,0:T(8,128)(2,1)} %cot_ref.1, bf16[2560,128]{1,0:T(8,128)(2,1)} %bitcast.23, bf16[320,320]{1,0:T(8,128)(2,1)} %mul.20.conv_ref, f32[20]{0:T(128)} %bias_ref.1, bf16[256,128]{1,0:T(8,128)(2,1)} %constant.28.clone.iy_ref, ...), custom_call_target="tpu_custom_call" | custom-call | tf_op jit(solution)/shard_map/slab/pallas_call | solution.py:253
  104.8 15.6 %all_to_all.32 = bf16[8,320,128]{2,1,0:T(8,128)(2,1)} all-to-all(bf16[8,320,128]{2,1,0:T(8,128)(2,1)} %bitcast.24), channel_id=1, replica_groups=mesh['dp'=16,'mp'=8] {'mp'}, dimensions={0} | all-to-all | bytes 1310720 | tf_op jit(solution)/shard_map/all_to_all | solution.py:396
  120.4 2.2 %forward_x.3 = f32[640,128]{1,0:T(8,128)} custom-call(bf16[2560,128]{1,0:T(8,128)(2,1)} %bitcast.21, bf16[128,256]{1,0:T(8,128)(2,1)} %constant.29.clone.fx_ref), custom_call_target="tpu_custom_call" | custom-call | tf_op jit(solution)/shard_map/forward_x/pallas_call | solution.py:289
  122.7 14.1 %all_to_all.33 = f32[16,40,128]{2,1,0:T(8,128)} all-to-all(f32[16,40,128]{2,1,0:T(8,128)} %bitcast.26), channel_id=1, replica_groups=mesh['dp'=16,'mp'=8] {'dp'}, dimensions={0} | all-to-all | bytes 655360 | tf_op jit(solution)/shard_map/all_to_all | solution.py:396
  136.8 3.7 %grad.1 = f32[2,400,128]{2,1,0:T(8,128)} custom-call(f32[640,128]{1,0:T(8,128)} %bitcast.18, f32[640,128]{1,0:T(8,128)} %bitcast.27, bf16[256,512]{1,0:T(8,128)(2,1)} %constant.31.clone.spread_ref), custom_call_target="tpu_custom_call" | custom-call | tf_op jit(solution)/shard_map/grad/pallas_call | solution.py:289
  140.5 3.4 %reshape.71 = f32[2,2,2,20,5,2,4,16]{7,6,5,4,3,2,1,0:T(4,128)S(1)} reshape(f32[2,400,128]{2,1,0:T(8,128)} %grad.1) | data formatting | bytes 819200 | tf_op jit(solution)/shard_map/reshape | solution.py:432
  143.9 3.5 %copy.22 = f32[2,2,20,5,4,2,2,16]{7,6,5,1,4,3,2,0:T(2,128)} copy(f32[2,2,20,5,4,2,2,16]{7,4,6,3,2,1,0,5:T(4,128)S(1)} %bitcast.16) | data formatting | bytes 819200 | tf_op jit(solution)/shard_map/transpose | solution.py:433
  147.4 5.4 %reshape.72 = f32[2,2,20,20,64]{4,1,3,2,0:T(2,128)} reshape(f32[2,2,20,5,4,2,2,16]{7,6,5,1,4,3,2,0:T(2,128)} %copy.22) | data formatting | bytes 819200 | tf_op jit(solution)/shard_map/reshape | solution.py:433
  (1 shorter events, 0.0 us)
Async XLA Ops:
  10.4 29.3 %copy-start.2 = (bf16[2,2,20,20,64]{4,1,3,2,0:T(2,128)(2,1)S(1)}, bf16[2,2,20,20,64]{4,1,3,2,0:T(2,128)(2,1)}, u32[]{:S(2)}) copy-start(bf16[2,2,20,20,64]{4,1,3,2,0:T(2,128)(2,1)} %param.18) | copy-start | bytes 614404
  32.7 14.7 %all-to-all-start.1 = ((f32[16,40,128]{2,1,0:T(8,128)}), f32[16,40,128]{2,1,0:T(8,128)S(1)}, u32[]{:S(2)}, u32[]{:S(2)}) async-start(f32[16,40,128]{2,1,0:T(8,128)} %bitcast.25), calls=%async_computation.1 | async-start | bytes 655360 | tf_op jit(solution)/shard_map/all_to_all | solution.py:396
  39.7 28.6 %copy-start.3 = (bf16[20,20]{1,0:T(8,128)(2,1)S(1)}, bf16[20,20]{1,0:T(8,128)(2,1)}, u32[]{:S(2)}) copy-start(bf16[20,20]{1,0:T(8,128)(2,1)} %param.19) | copy-start | bytes 2404
  47.4 0.7 copy-start
  64.8 15.3 %all-to-all-start.3 = ((bf16[8,320,128]{2,1,0:T(8,128)(2,1)}), bf16[8,320,128]{2,1,0:T(8,128)(2,1)S(1)}, u32[]{:S(2)}, u32[]{:S(2)}) async-start(bf16[8,320,128]{2,1,0:T(8,128)(2,1)} %bitcast.20), calls=%async_computation.3 | async-start | bytes 1310720 | tf_op jit(solution)/shard_map/all_to_all | solution.py:396
  80.1 0.8 copy-start.1

commit v2 on v1

v2 whole, which is shorter than its diff:
```python
import functools

import jax
import jax.numpy as jnp
import ml_dtypes
import numpy as np
from jax import lax
from jax.experimental import pallas as pl
from jax.experimental.pallas import tpu as pltpu
from jax.sharding import PartitionSpec as P

X = 128
Y = 128
Z = 128
C = 20
KX = 32
KY = 32
KZ = 16
DP = 16
MP = 8
XP = 8
G = 5
GK = 20
GA = 10
SUB = 2

bf16 = jnp.bfloat16
f32 = jnp.float32
np_bf16 = ml_dtypes.bfloat16

INV_ROOT_TWO = 0.7071067811865476
TWO_OVER_ROOT_PI = 1.1283791670955126
LOG2_E = 1.4426950408889634


def kept(count, length):
    return np.concatenate([np.arange(count // 2), np.arange(length - count // 2, length)])


def angles(modes, length):
    return 2.0 * np.pi / length * ((modes[:, None] * np.arange(length)[None, :]) % length)


def hi_lo(table):
    upper = table.astype(np_bf16)
    lower = (table - upper.astype(np.float64)).astype(np_bf16)
    return upper, lower


def z_scales():
    candidates = 1.0 + np.arange(512) / 512
    scales = []
    for row in angles(np.arange(KZ), Z):
        values = np.concatenate([np.cos(row), np.sin(row)])[None, :] * candidates[:, None]
        off = ((values.astype(np_bf16).astype(np.float64) - values) ** 2).sum(1) / (values**2).sum(1)
        scales.append(candidates[int(np.argmin(off))])
    return np.array(scales)


@functools.cache
def tables():
    scale = z_scales()
    weight = np.where(np.arange(KZ) == 0, 1.0, 2.0) / (X * Y * Z)
    phase_z = angles(np.arange(KZ), Z)
    cos_z, sin_z = np.cos(phase_z), np.sin(phase_z)
    forward_z = np.zeros((8, Z, 2, 8, KZ))
    inverse_z = np.zeros((4, 2, 8, KZ, 2, Z))
    for q in range(8):
        forward_z[q, :, 0, q, :] = (cos_z * scale[:, None]).T
        forward_z[q, :, 1, q, :] = (sin_z * scale[:, None]).T
        inverse_z[q // 2, 0, q, :, q % 2, :] = cos_z * scale[:, None]
        inverse_z[q // 2, 1, q, :, q % 2, :] = -sin_z * scale[:, None]
    unscale = np.tile(1.0 / scale, 16)[None, :]
    unscale_back = np.tile(0.5 * weight / scale, 16)[None, :]
    unscale_inverse = np.tile(INV_ROOT_TWO * weight / scale, 8)[None, :]
    phase_y = angles(kept(KY, Y), Y)
    cos_y, sin_y = np.cos(phase_y), np.sin(phase_y)
    forward_y = np.zeros((KY, 2, 2, Y))
    forward_y[:, 0, 0], forward_y[:, 0, 1] = cos_y, -sin_y
    forward_y[:, 1, 0], forward_y[:, 1, 1] = -sin_y, -cos_y
    forward_y = np.concatenate(hi_lo(forward_y.reshape(64, 256)), axis=0)
    inverse_y = np.zeros((2, Y, KY, 2))
    inverse_y[0, :, :, 0], inverse_y[0, :, :, 1] = cos_y.T, -sin_y.T
    inverse_y[1, :, :, 0], inverse_y[1, :, :, 1] = sin_y.T, cos_y.T
    inverse_y = np.concatenate(hi_lo(inverse_y.reshape(256, 64)), axis=1)
    phase_x = angles(kept(KX, X), X).reshape(16, 2, 8, 8, 2)
    cos_x, sin_x = np.cos(phase_x), np.sin(phase_x)
    forward_x = np.zeros((2, 2, 2, 16, 8, 2, 8))
    inverse_x = np.zeros((2, 8, 2, 8, 2, 2, 16))
    cos_f = np.transpose(cos_x, (4, 1, 0, 2, 3))
    sin_f = np.transpose(sin_x, (4, 1, 0, 2, 3))
    forward_x[:, :, 0, :, :, 0, :] = cos_f
    forward_x[:, :, 0, :, :, 1, :] = sin_f
    forward_x[:, :, 1, :, :, 0, :] = -sin_f
    forward_x[:, :, 1, :, :, 1, :] = cos_f
    cos_i = np.transpose(cos_x, (4, 2, 3, 1, 0))
    sin_i = np.transpose(sin_x, (4, 2, 3, 1, 0))
    inverse_x[:, :, 0, :, :, 0, :] = cos_i
    inverse_x[:, :, 0, :, :, 1, :] = -sin_i
    inverse_x[:, :, 1, :, :, 0, :] = sin_i
    inverse_x[:, :, 1, :, :, 1, :] = cos_i
    forward_x = np.concatenate(hi_lo(forward_x.reshape(128, 128)), axis=1)
    inverse_x = np.concatenate(hi_lo(inverse_x.reshape(256, 64)), axis=1)
    spread = np.zeros((2, 4, KZ, 4, 2, 4, KZ))
    for channel in range(4):
        for place in range(4):
            for b in range(2):
                spread[b, channel, np.arange(KZ), channel, b, place, np.arange(KZ)] = 1.0
    spread = spread.reshape(128, 512)
    place = np.zeros((4, 4, KZ, 2, 2, 4, KZ))
    for o in range(4):
        for kyl in range(4):
            place[o, kyl, np.arange(KZ), kyl // 2, kyl % 2, o, np.arange(KZ)] = 1.0
    gather = np.zeros((2, 2, 4, KZ, 4, 2, 2, 2, KZ))
    for o in range(4):
        for a in range(2):
            for b in range(2):
                gather[a, b, o, np.arange(KZ), o, 0, a, b, np.arange(KZ)] = 1.0
    gather = gather.reshape(256, 512)
    return dict(
        gather=np.concatenate([gather, gather], axis=0).astype(np_bf16),
        forward_z=forward_z.reshape(4, 256, 256).astype(np_bf16),
        inverse_z=inverse_z.reshape(4, 256, 256).astype(np_bf16),
        unscale=unscale.astype(np.float32),
        unscale_back=unscale_back.astype(np.float32),
        unscale_inverse=unscale_inverse.astype(np.float32),
        forward_y=forward_y,
        inverse_y=inverse_y,
        forward_x=forward_x,
        inverse_x=inverse_x,
        spread=spread.astype(np_bf16),
        place=place.reshape(256, 256).astype(np_bf16),
    )


def mm(a, b):
    return jnp.dot(a, b, preferred_element_type=f32)


def z_transform(lhs_of, fz_ref, un_ref, groups):
    total = mm(lhs_of(0, groups), fz_ref[0])
    for pair in range(1, 4):
        total = total + mm(lhs_of(pair, groups), fz_ref[pair])
    return total * un_ref[...]


def y_transform(part, fy_ref, modes_ref, g, at):
    both = jnp.concatenate([part[:, :128], part[:, 128:]], axis=0)
    upper = both.astype(bf16)
    lower = (both - upper.astype(f32)).astype(bf16)
    out = mm(fy_ref[...], jnp.concatenate([upper, lower], axis=1))
    modes = out[:64, :128] + out[64:, :128] + out[:64, 128:]
    for j in range(MP):
        modes_ref[pl.ds(j * 320 + g * 64 + at, 8, stride=8), :] = modes[j * 8 : (j + 1) * 8]


def analyse(lhs_of, fz_ref, fy_ref, un_ref, modes_ref, at, groups):
    total = z_transform(lhs_of, fz_ref, un_ref, groups)
    for k, g in enumerate(groups):
        y_transform(total[k * Y : (k + 1) * Y], fy_ref, modes_ref, g, at)


HALVES = ((0, 1, 2), (3, 4))


def analyse_kernel(*refs):
    field_refs, (fz_ref, fy_ref, un_ref, out_ref, modes_ref) = refs[: 2 * SUB], refs[2 * SUB :]
    step = pl.program_id(0)

    for sub in range(SUB):

        def lhs(pair, groups, sub=sub):
            xl, c4 = 2 * sub + pair // 2, 2 * (pair % 2)
            rows = [
                jnp.concatenate(
                    [field_refs[xl][0, 0, 4 * g + c4], field_refs[xl][0, 0, 4 * g + c4 + 1]], axis=1
                )
                for g in groups
            ]
            return jnp.concatenate(rows, axis=0)

        totals = [z_transform(lhs, fz_ref, un_ref, groups) for groups in HALVES]
        for total, groups in zip(totals, HALVES):
            for k, g in enumerate(groups):
                y_transform(total[k * Y : (k + 1) * Y], fy_ref, modes_ref, g, step * SUB + sub)

    @pl.when(step == XP // SUB - 1)
    def _():
        out_ref[...] = modes_ref[...].astype(bf16)


def x_streams():
    return [
        pl.BlockSpec((1, 1, C, Y, Z), lambda i, k=k: (0, 2 * SUB * i + k, 0, 0, 0))
        for k in range(2 * SUB)
    ]


def full(shape):
    zeros = (0,) * len(shape)
    return pl.BlockSpec(shape, lambda *_: zeros, pipeline_mode=pl.Buffered(1))


def analyse_call(fields, t):
    return pl.pallas_call(
        analyse_kernel,
        out_shape=jax.ShapeDtypeStruct((2560, 128), bf16),
        grid=(XP // SUB,),
        in_specs=[
            *x_streams(),
            full((4, 256, 256)),
            full((128, 256)),
            full((1, 256)),
        ],
        out_specs=pl.BlockSpec((2560, 128), lambda i: (0, 0)),
        scratch_shapes=[pltpu.VMEM((2560, 128), f32)],
        compiler_params=pltpu.CompilerParams(
            dimension_semantics=("arbitrary",), vmem_limit_bytes=54 << 20
        ),
        name="analyse",
    )(*[fields] * (2 * SUB), t["forward_z"], t["forward_y"], t["unscale"])


def conv_kernel(*refs):
    field_refs, (conv_ref, bias_ref), out_refs = refs[: 2 * SUB], refs[2 * SUB : -2 * SUB], refs[-2 * SUB :]
    bias = jnp.concatenate([bias_ref[...], bias_ref[...]], axis=1)
    for xl in range(2 * SUB):
        for yp in range(4):
            right = jnp.concatenate(
                [
                    field_refs[xl][0, 0, :, yp * 32 + h * 16 : yp * 32 + (h + 1) * 16, :].reshape(320, Z)
                    for h in range(2)
                ],
                axis=1,
            )
            out = ((mm(conv_ref[...], right) + bias) * INV_ROOT_TWO).astype(bf16)
            for h in range(2):
                out_refs[xl][0, :, yp * 32 + h * 16 : yp * 32 + (h + 1) * 16, :] = out[
                    :, h * 128 : (h + 1) * 128
                ].reshape(C, 16, Z)


def conv_call(fields, conv, bias):
    return pl.pallas_call(
        conv_kernel,
        out_shape=[jax.ShapeDtypeStruct((XP // SUB, C, Y, Z), bf16)] * (2 * SUB),
        grid=(XP // SUB,),
        in_specs=[
            *x_streams(),
            full((320, 320)),
            full((320, 128)),
        ],
        out_specs=[pl.BlockSpec((1, C, Y, Z), lambda i: (i, 0, 0, 0))] * (2 * SUB),
        compiler_params=pltpu.CompilerParams(
            dimension_semantics=("arbitrary",), vmem_limit_bytes=54 << 20
        ),
        cost_estimate=pl.CostEstimate(
            flops=2 * 16 * Y * Z * 320 * C, bytes_accessed=4 * 16 * C * Y * Z, transcendentals=0
        ),
        name="conv",
    )(*[fields] * (2 * SUB), conv, bias)


def slab_kernel(*refs):
    conv_refs, cot_refs = refs[: 2 * SUB], refs[2 * SUB : 4 * SUB]
    mixed_ref, iy_ref, iz_ref, uni_ref, fz_ref, fy_ref, un_ref, out_ref = refs[4 * SUB : 4 * SUB + 8]
    modes_ref, mixed_f32, wave_ref, delta_ref = refs[4 * SUB + 8 :]
    step = pl.program_id(0)

    def wave(at, slot, g):
        rows = [mixed_f32[pl.ds(j * 320 + g * 64 + at, 8, stride=8), :] for j in range(MP)]
        part = jnp.concatenate(rows, axis=0).astype(bf16)
        out = mm(iy_ref[...], jnp.concatenate([part, part], axis=0))
        out = (out * uni_ref[...]).astype(bf16)
        wave_ref[slot, g * Y : (g + 1) * Y, :128] = out[:Y]
        wave_ref[slot, g * Y : (g + 1) * Y, 128:] = out[Y:]

    def delta(sub, pair, spectral):
        xl = 2 * sub + pair // 2
        for g in range(G):
            for h in range(2):
                channel = 4 * g + 2 * (pair % 2) + h
                u = spectral[g * Y : (g + 1) * Y, h * 128 : (h + 1) * 128] + conv_refs[xl][
                    0, channel
                ].astype(f32)
                bell = jnp.exp2(u * u * -LOG2_E)
                slope = 1.0 + (lax.erf(u) + (u * TWO_OVER_ROOT_PI) * bell)
                value = cot_refs[xl][0, 0, channel].astype(f32) * slope
                delta_ref[sub % 2, pair, g * Y : (g + 1) * Y, h * 128 : (h + 1) * 128] = value.astype(bf16)

    def lhs_of(slot):
        return lambda pair, groups: delta_ref[slot, pair, groups[0] * Y : (groups[-1] + 1) * Y, :]

    @pl.when(step == 0)
    def _():
        mixed_f32[...] = mixed_ref[...].astype(f32)
        for g in range(G):
            wave(0, 0, g)

    for sub in range(SUB):
        at = step * SUB + sub
        before = jnp.maximum(at - 1, 0)
        after = jnp.minimum(at + 1, XP - 1)
        slot = sub % 2
        lhs = lhs_of(1 - slot)
        spectral = [mm(wave_ref[slot], iz_ref[0])]
        totals = []
        for pair in range(4):
            if pair < 3:
                spectral.append(mm(wave_ref[slot], iz_ref[pair + 1]))
            delta(sub, pair, spectral[pair])
            if pair < 2:
                totals.append(z_transform(lhs, fz_ref, un_ref, HALVES[pair]))
            else:
                for k, g in enumerate(HALVES[pair - 2]):
                    y_transform(totals[pair - 2][k * Y : (k + 1) * Y], fy_ref, modes_ref, g, before)
            for g in ((0, 1), (2,), (3,), (4,))[pair]:
                wave(after, 1 - slot, g)

    @pl.when(step == XP // SUB - 1)
    def _():
        lhs = lhs_of((SUB - 1) % 2)
        for groups in HALVES:
            analyse(lhs, fz_ref, fy_ref, un_ref, modes_ref, XP - 1, groups)
        out_ref[...] = modes_ref[...].astype(bf16)


def slab_call(conv, cotangent, mixed, t):
    return pl.pallas_call(
        slab_kernel,
        out_shape=jax.ShapeDtypeStruct((2560, 128), bf16),
        grid=(XP // SUB,),
        in_specs=[
            *[pl.BlockSpec((1, C, Y, Z), lambda i: (i, 0, 0, 0))] * (2 * SUB),
            *x_streams(),
            full((2560, 128)),
            full((256, 128)),
            full((4, 256, 256)),
            full((1, 128)),
            full((4, 256, 256)),
            full((128, 256)),
            full((1, 256)),
        ],
        out_specs=pl.BlockSpec((2560, 128), lambda i: (0, 0)),
        scratch_shapes=[
            pltpu.VMEM((2560, 128), f32),
            pltpu.VMEM((2560, 128), f32),
            pltpu.VMEM((SUB, 640, 256), bf16),
            pltpu.VMEM((SUB, 4, 640, 256), bf16),
        ],
        compiler_params=pltpu.CompilerParams(
            dimension_semantics=("arbitrary",), vmem_limit_bytes=54 << 20
        ),
        name="slab",
    )(
        *conv, *[cotangent] * (2 * SUB), mixed, t["inverse_y"], t["inverse_z"],
        t["unscale_inverse"], t["forward_z"], t["forward_y"], t["unscale_back"],
    )


def small_call(kernel, name, out_shape, scratch, *args):
    return pl.pallas_call(
        kernel,
        out_shape=out_shape,
        scratch_shapes=scratch,
        compiler_params=pltpu.CompilerParams(vmem_limit_bytes=10 << 20),
        name=name,
    )(*args)


def lower_half():
    return lax.broadcasted_iota(jnp.int32, (64, 128), 1) < 64


def forward_x_kernel(in_ref, fx_ref, out_ref, wide_ref):
    low = lower_half()
    for gk in range(GA):
        cols = []
        for b in range(2):
            row = (2 * gk + b) * 16
            cols.append(jnp.concatenate([in_ref[j * 320 + row : j * 320 + row + 16, :] for j in range(8)], axis=0))
        right = jnp.concatenate(cols, axis=1)
        out = mm(fx_ref[...], jnp.concatenate([right, right], axis=0))
        first = jnp.where(low, out[:64, :128], out[64:, 128:])
        second = jnp.where(low, out[:64, 128:], out[64:, :128])
        res = first + pltpu.roll(second, 64, 1)
        for r in range(4):
            wide_ref[pl.ds(r * GA + gk, 16, stride=40), :] = res[r * 16 : (r + 1) * 16]
    out_ref[...] = wide_ref[...].astype(bf16)


def inverse_x_kernel(in_ref, ix_ref, out_ref, wide_ref):
    wide_ref[...] = in_ref[...].astype(f32)
    low = lax.broadcasted_iota(jnp.int32, (128, 128), 1) < 64
    for gk in range(GA):
        rows = [wide_ref[pl.ds(r * GA + gk, 16, stride=40), :] for r in range(4)]
        part = jnp.concatenate(rows, axis=0).astype(bf16)
        out = mm(ix_ref[...], jnp.concatenate([part, part], axis=0))
        first = jnp.where(low, out[:128], pltpu.roll(out[128:], 64, 1)).astype(bf16)
        second = jnp.where(low, pltpu.roll(out[:128], 64, 1), out[128:]).astype(bf16)
        for b, value in enumerate((first, second)):
            row = (2 * gk + b) * 16
            for j in range(8):
                out_ref[j * 320 + row : j * 320 + row + 16, :] = value[j * 16 : (j + 1) * 16]


def weight_kernel(w_ref, place_ref, out_ref, wide_ref):
    wide_ref[...] = w_ref[...].astype(f32)
    cols = [wide_ref[pl.ds(o, 400, stride=4), :].astype(bf16) for o in range(4)]
    out = mm(jnp.concatenate(cols, axis=1), place_ref[...])
    out_ref[0] = out[:, :128]
    out_ref[1] = out[:, 128:]


def spread_channels(in_ref, spread_ref, wide_ref, rows_ref, chan_ref):
    wide_ref[...] = in_ref[...].astype(f32)
    for r in range(40):
        rows_ref[r * 16 : (r + 1) * 16, :] = wide_ref[pl.ds(r, 16, stride=40), :].astype(bf16)
    chan_ref[...] = mm(rows_ref[...], spread_ref[...])


def channel_parts(chan_ref, kxl, kya, c):
    row = (kxl * 20 + (c // 4) * 2 + kya) * 16
    lanes = (c % 4) * 128
    return (
        chan_ref[row : row + 16, lanes : lanes + 128],
        chan_ref[row + 160 : row + 176, lanes : lanes + 128],
    )


SPREAD_SCRATCH = (
    pltpu.VMEM((640, 128), f32), pltpu.VMEM((640, 128), bf16), pltpu.VMEM((640, 512), f32)
)


def mix_kernel(in_ref, spread_ref, w_ref, out_ref, wide_ref, rows_ref, chan_ref):
    spread_channels(in_ref, spread_ref, wide_ref, rows_ref, chan_ref)
    for kxl in range(2):
        for kya in range(2):
            real = [jnp.zeros((16, 128), f32) for _ in range(G)]
            imag = [jnp.zeros((16, 128), f32) for _ in range(G)]
            for c in range(C):
                s_re, s_im = channel_parts(chan_ref, kxl, kya, c)
                for go in range(G):
                    line = kxl * 200 + c * G + go
                    w_re = w_ref[kya, line : line + 1, :]
                    w_im = w_ref[kya, line + 100 : line + 101, :]
                    real[go] = real[go] + (s_re * w_re - s_im * w_im)
                    imag[go] = imag[go] + (s_re * w_im + s_im * w_re)
            for go in range(G):
                row = kxl * 20 + go * 2 + kya
                wide_ref[pl.ds(row, 16, stride=40), :] = real[go]
                wide_ref[pl.ds(row + 10, 16, stride=40), :] = imag[go]
    out_ref[...] = wide_ref[...].astype(bf16)


def grad_kernel(s_ref, b_ref, spread_ref, gather_ref, out_ref, wide_ref, rows_ref, chan_ref, sum_ref):
    spread_channels(s_ref, spread_ref, wide_ref, rows_ref, chan_ref)
    wide_ref[...] = b_ref[...].astype(f32)
    for kxl in range(2):
        for kya in range(2):
            b_re = [wide_ref[pl.ds(kxl * 20 + g * 2 + kya, 16, stride=40), :] for g in range(G)]
            b_im = [wide_ref[pl.ds(kxl * 20 + g * 2 + kya + 10, 16, stride=40), :] for g in range(G)]
            for c in range(C):
                s_re, s_im = channel_parts(chan_ref, kxl, kya, c)
                for go in range(G):
                    line = kxl * 100 + c * G + go
                    real = s_re * b_re[go] + s_im * b_im[go]
                    imag = s_re * b_im[go] - s_im * b_re[go]
                    lanes = slice(kya * 128, kya * 128 + 128)
                    sum_ref[line : line + 1, lanes] = jnp.sum(real, axis=0, keepdims=True)
                    sum_ref[200 + line : 201 + line, lanes] = jnp.sum(imag, axis=0, keepdims=True)
    sums = sum_ref[...]
    upper = sums.astype(bf16)
    lower = (sums - upper.astype(f32)).astype(bf16)
    placed = mm(jnp.concatenate([upper, lower], axis=1), gather_ref[...])
    for o in range(4):
        for part in range(2):
            out_ref[pl.ds(o * 2 + part, 200, stride=8), :] = placed[
                part * 200 : (part + 1) * 200, o * 128 : o * 128 + 128
            ]


def exchange(values, axis, count):
    blocks = values.reshape(count, -1, 128)
    return lax.all_to_all(blocks, axis, split_axis=0, concat_axis=0, tiled=True).reshape(-1, 128)


def shards(fields, cotangent, spectral_weight, conv_weight, conv_bias):
    t = {name: jnp.asarray(value) for name, value in tables().items()}
    conv = (
        conv_weight.T[:, None, :, None] * jnp.eye(16, dtype=bf16)[None, :, None, :]
    ).reshape(320, 320)

    bias = jnp.broadcast_to(conv_bias[:, None, None], (C, 16, 128)).reshape(320, 128)

    def to_kx(modes):
        moved = exchange(modes, "mp", MP)
        part = small_call(
            forward_x_kernel, "forward_x", jax.ShapeDtypeStruct((640, 128), bf16),
            [pltpu.VMEM((640, 128), f32)], moved, t["forward_x"],
        )
        return exchange(part, "dp", DP)

    weights = small_call(
        weight_kernel, "weights", jax.ShapeDtypeStruct((2, 400, 128), f32),
        [pltpu.VMEM((1600, 64), f32)], spectral_weight.reshape(1600, 64), t["place"],
    )
    spectra = to_kx(analyse_call(fields, t))
    mixed = small_call(
        mix_kernel, "mix", jax.ShapeDtypeStruct((640, 128), bf16), SPREAD_SCRATCH,
        spectra, t["spread"], weights,
    )
    slabs = small_call(
        inverse_x_kernel, "inverse_x", jax.ShapeDtypeStruct((2560, 128), bf16),
        [pltpu.VMEM((640, 128), f32)], exchange(mixed, "dp", DP), t["inverse_x"],
    )
    slabs, conv = lax.optimization_barrier((slabs, conv))
    conv_term = conv_call(fields, conv, bias)
    back = to_kx(slab_call(conv_term, cotangent, exchange(slabs, "mp", MP), t))
    grad = small_call(
        grad_kernel, "grad", jax.ShapeDtypeStruct((1600, 128), f32),
        (*SPREAD_SCRATCH, pltpu.VMEM((400, 256), f32)), spectra, back, t["spread"], t["gather"],
    )
    return jnp.transpose(grad.reshape(2, C, C, 2, 128)[..., :64], (0, 3, 1, 2, 4))


def solution(mesh):
    return jax.shard_map(
        shards,
        mesh=mesh,
        in_specs=(
            P("dp", "mp", None, None, None),
            P("dp", "mp", None, None, None),
            P("dp", None, None, None, "mp"),
            P(),
            P(),
        ),
        out_specs=P("dp", None, None, None, "mp"),
        check_vma=False,
    )
```

time: 154 us -> 125 us (0.81)
  blocking collectives: 61.1 us -> 49 us
  local copies, waits for them, and re-layouts: 16.7 us -> 4.93 us
  Pallas kernels: 49.9 us -> 45.1 us
  starting transfers between devices: 10.5 us -> 14.3 us
  waiting for transfers between devices: 14.2 us -> 10.5 us
    all_to_all x4 -> x3, blocking collectives: 61.1 us -> 49 us  [exchange(): lax.all_to_all(blocks, axis, split_axis=0, concat_axis=0, tiled=True)]
    pallas_call x0 -> x1, Pallas kernels: none -> 10.4 us  [conv_call(): pl.pallas_call(conv_kernel, out_shape=[jax.ShapeDtypeStruct((XP // SUB, C...]
    reshape x2 -> x0, local copies, waits for them, and re-layouts: 8.72 us -> none  [the longest x1 5.37 us: shards(): return jnp.transpose(grad, (1, 2, 3, 4, 6, 0, 5, 7)).reshape(2, 2, C, C, 64)]
    pallas_call x6, Pallas kernels: 15.6 us -> 7.27 us  [small_call(): pl.pallas_call(kernel, out_shape=out_shape, scratch_shapes=scratch, compi...]
    pallas_call x1, Pallas kernels: 23.9 us -> 18.4 us  [slab_call(): pl.pallas_call(slab_kernel, out_shape=jax.ShapeDtypeStruct((2560, 128), b...]
    all_to_all x2 -> x3, starting transfers between devices: 10.5 us -> 14.3 us  [exchange(): lax.all_to_all(blocks, axis, split_axis=0, concat_axis=0, tiled=True)]
    all_to_all x2 -> x3, waiting for transfers between devices: 14.2 us -> 10.5 us  [exchange(): lax.all_to_all(blocks, axis, split_axis=0, concat_axis=0, tiled=True)]
    transpose x1, local copies, waits for them, and re-layouts: 3.5 us -> 0.94 us  [shards(): jnp.transpose(grad.reshape(2, C, C, 2, 128)[..., :64], (0, 3, 1, 2, 4))]
  transfers between devices with their start and end apart: 2 -> 3, of which waited for: 2 -> 3; matrix products, arithmetic and copies ran while one was open for 2% -> 3% of each run, Pallas kernels for 1% -> 9%
where the time goes in v2:
time: 125 us; the launch traced here: 124 us
  blocking collectives  49 us (39%)
  Pallas kernels  45.1 us (36%)
  starting transfers between devices  14.3 us (11%)
  waiting for transfers between devices  10.5 us (8%)
  local copies, waits for them, and re-layouts  4.93 us (4%)
    all_to_all x3, blocking collectives, exchange(): lax.all_to_all(blocks, axis, split_axis=0, concat_axis=0, tiled=True)  49 us
    pallas_call x1, Pallas kernels, slab_call(): pl.pallas_call(slab_kernel, out_shape=jax.ShapeDtypeStruct((2560, 128), b...  18.4 us
    all_to_all x3, starting transfers between devices, exchange(): lax.all_to_all(blocks, axis, split_axis=0, concat_axis=0, tiled=True)  14.3 us
    all_to_all x3, waiting for transfers between devices, exchange(): lax.all_to_all(blocks, axis, split_axis=0, concat_axis=0, tiled=True)  10.5 us
    pallas_call x1, Pallas kernels, conv_call(): pl.pallas_call(conv_kernel, out_shape=[jax.ShapeDtypeStruct((XP // SUB, C...  10.4 us
    pallas_call x1, Pallas kernels, analyse_call(): pl.pallas_call(analyse_kernel, out_shape=jax.ShapeDtypeStruct((2560, 128)...  9.06 us
    pallas_call x6, Pallas kernels, small_call(): pl.pallas_call(kernel, out_shape=out_shape, scratch_shapes=scratch, compi...  7.27 us
  transfers between devices with their start and end apart: 3, of which 3 were waited for; matrix products, arithmetic and copies ran while one was open for 3% of the time, Pallas kernels for 9%

profile of v2, /device:TPU:1, one launch (start us, length us, event | category | flops | bytes accessed | tf_op | source)
XLA Modules:
  0.0 124.2 jit_solution(17884023037096246014)
XLA Ops:
  0.0 9.1 %analyse.1 = bf16[2560,128]{1,0:T(8,128)(2,1)} custom-call(bf16[1,16,20,128,128]{4,3,2,1,0:T(8,128)(2,1)} %refs_3_.3, bf16[1,16,20,128,128]{4,3,2,1,0:T(8,128)(2,1)} %refs_3_.3, bf16[1,16,20,128,128]{4,3,2,1,0:T(8,128)(2,1)} %refs_3_.3, bf16[1,16,20,128,128]{4,3,2,1,0:T(8,128)(2,1)} %refs_3_.3, bf16[4,256,256]{2,1,0:T(8,128)(2,1)} %constant.25.clone.refs_4_.refs_12_, ...), custom_call_target="tpu_custom_call" | custom-call | tf_op jit(solution)/shard_map/analyse/pallas_call | solution.py:205
  9.1 0.0 copy-start.1
  9.1 20.0 %all_to_all.30 = bf16[8,320,128]{2,1,0:T(8,128)(2,1)S(1)} all-to-all(bf16[8,320,128]{2,1,0:T(8,128)(2,1)} %bitcast.26), channel_id=1, replica_groups=mesh['dp'=16,'mp'=8] {'mp'}, dimensions={0} | all-to-all | bytes 1310720 | tf_op jit(solution)/shard_map/all_to_all | solution.py:486
  29.1 0.0 copy-done.2
  29.1 1.1 forward_x.2
  30.2 7.0 %all-to-all-start.1 = ((bf16[16,40,128]{2,1,0:T(8,128)(2,1)}), bf16[16,40,128]{2,1,0:T(8,128)(2,1)S(1)}, u32[]{:S(2)}, u32[]{:S(2)}) async-start(bf16[16,40,128]{2,1,0:T(8,128)(2,1)} %bitcast.2), calls=%async_computation.1 | async-start | bytes 327680 | tf_op jit(solution)/shard_map/all_to_all | solution.py:486
  37.2 0.1 copy.21
  37.3 0.1 copy.20
  37.4 0.2 reshape.62.w_ref
  37.5 0.3 weights.1.w_ref
  37.8 5.7 %all-to-all-done.1 = bf16[16,40,128]{2,1,0:T(8,128)(2,1)S(1)} async-done(((bf16[16,40,128]{2,1,0:T(8,128)(2,1)}), bf16[16,40,128]{2,1,0:T(8,128)(2,1)S(1)}, u32[]{:S(2)}, u32[]{:S(2)}) %all-to-all-start.1) | async-done | bytes 163872 | tf_op jit(solution)/shard_map/all_to_all | solution.py:486
  43.5 2.0 %mix.1 = bf16[640,128]{1,0:T(8,128)(2,1)} custom-call(bf16[640,128]{1,0:T(8,128)(2,1)S(1)} %bitcast.19, bf16[128,512]{1,0:T(8,128)(2,1)S(1)} %copy-done.1, f32[2,400,128]{2,1,0:T(8,128)S(1)} %weights.1.w_ref), custom_call_target="tpu_custom_call" | custom-call | tf_op jit(solution)/shard_map/mix/pallas_call | solution.py:362
  45.5 3.8 %all-to-all-start.2 = ((bf16[16,40,128]{2,1,0:T(8,128)(2,1)}), bf16[16,40,128]{2,1,0:T(8,128)(2,1)S(1)}, u32[]{:S(2)}, u32[]{:S(2)}) async-start(bf16[16,40,128]{2,1,0:T(8,128)(2,1)} %bitcast.4), calls=%async_computation.2 | async-start | bytes 327680 | tf_op jit(solution)/shard_map/all_to_all | solution.py:486
  49.3 0.2 broadcast_multiply_fusion
  49.5 0.0 copy-start.8
  49.6 1.8 %mul.20.refs_4_ = bf16[320,320]{1,0:T(8,128)(2,1)} reshape(bf16[20,16,20,16]{3,2,1,0:T(8,128)(2,1)S(1)} %broadcast_multiply_fusion) | data formatting | bytes 409600 | tf_op jit(solution)/shard_map/mul | solution.py:492
  51.4 4.4 %all-to-all-done.2 = bf16[16,40,128]{2,1,0:T(8,128)(2,1)S(1)} async-done(((bf16[16,40,128]{2,1,0:T(8,128)(2,1)}), bf16[16,40,128]{2,1,0:T(8,128)(2,1)S(1)}, u32[]{:S(2)}, u32[]{:S(2)}) %all-to-all-start.2) | async-done | bytes 163872 | tf_op jit(solution)/shard_map/all_to_all | solution.py:486
  55.8 1.3 %inverse_x.1 = bf16[2560,128]{1,0:T(8,128)(2,1)} custom-call(bf16[640,128]{1,0:T(8,128)(2,1)S(1)} %bitcast.21, bf16[256,128]{1,0:T(8,128)(2,1)S(1)} %copy-done.4), custom_call_target="tpu_custom_call" | custom-call | tf_op jit(solution)/shard_map/inverse_x/pallas_call | solution.py:362
  57.0 3.5 %all-to-all-start.3 = ((bf16[8,320,128]{2,1,0:T(8,128)(2,1)}), bf16[8,320,128]{2,1,0:T(8,128)(2,1)S(1)}, u32[]{:S(2)}, u32[]{:S(2)}) async-start(bf16[8,320,128]{2,1,0:T(8,128)(2,1)} %bitcast.7), calls=%async_computation.3 | async-start | bytes 1310720 | tf_op jit(solution)/shard_map/all_to_all | solution.py:486
  60.6 0.0 copy-done.8
  60.6 0.1 broadcast_in_dim.12
  60.6 0.1 broadcast_in_dim.13
  60.7 0.8 broadcast_in_dim.14.refs_5_
  61.5 10.4 %conv.1 = (bf16[4,20,128,128]{3,2,1,0:T(8,128)(2,1)}, bf16[4,20,128,128]{3,2,1,0:T(8,128)(2,1)}, bf16[4,20,128,128]{3,2,1,0:T(8,128)(2,1)}, bf16[4,20,128,128]{3,2,1,0:T(8,128)(2,1)}) custom-call(bf16[1,16,20,128,128]{4,3,2,1,0:T(8,128)(2,1)} %refs_3_.3, bf16[1,16,20,128,128]{4,3,2,1,0:T(8,128)(2,1)} %refs_3_.3, bf16[1,16,20,128,128]{4,3,2,1,0:T(8,128)(2,1)} %refs_3_.3, ...), custom_call_target="tpu_custom_call" | custom-call | flops 3355443200 | bytes 20971520 | tf_op jit(solution)/shard_map/conv/pallas_call | solution.py:244
  71.9 0.5 all-to-all-done.3
  72.3 0.8 copy-done.5
  73.2 18.4 %slab.1 = bf16[2560,128]{1,0:T(8,128)(2,1)} custom-call(bf16[4,20,128,128]{3,2,1,0:T(8,128)(2,1)} %get-tuple-element.12.refs_0_, bf16[4,20,128,128]{3,2,1,0:T(8,128)(2,1)} %get-tuple-element.13.refs_1_, bf16[4,20,128,128]{3,2,1,0:T(8,128)(2,1)} %get-tuple-element.14.refs_2_, bf16[4,20,128,128]{3,2,1,0:T(8,128)(2,1)} %get-tuple-element.15.refs_3_, ...), custom_call_target="tpu_custom_call" | custom-call | tf_op jit(solution)/shard_map/slab/pallas_call | solution.py:329
  91.6 17.7 %all_to_all.31 = bf16[8,320,128]{2,1,0:T(8,128)(2,1)S(1)} all-to-all(bf16[8,320,128]{2,1,0:T(8,128)(2,1)} %bitcast.25), channel_id=1, replica_groups=mesh['dp'=16,'mp'=8] {'mp'}, dimensions={0} | all-to-all | bytes 1310720 | tf_op jit(solution)/shard_map/all_to_all | solution.py:486
  109.2 0.4 forward_x.3
  109.7 11.3 %all_to_all.32 = bf16[16,40,128]{2,1,0:T(8,128)(2,1)S(1)} all-to-all(bf16[16,40,128]{2,1,0:T(8,128)(2,1)S(1)} %bitcast.23), channel_id=1, replica_groups=mesh['dp'=16,'mp'=8] {'dp'}, dimensions={0} | all-to-all | bytes 327680 | tf_op jit(solution)/shard_map/all_to_all | solution.py:486
  121.0 2.2 %grad.1 = f32[1600,128]{1,0:T(8,128)S(1)} custom-call(bf16[640,128]{1,0:T(8,128)(2,1)S(1)} %bitcast.20, bf16[640,128]{1,0:T(8,128)(2,1)S(1)} %bitcast.22, bf16[128,512]{1,0:T(8,128)(2,1)S(1)} %copy-done.1, bf16[512,512]{1,0:T(8,128)(2,1)S(1)} %copy-done), custom_call_target="tpu_custom_call" | custom-call | tf_op jit(solution)/shard_map/grad/pallas_call | solution.py:362
  123.2 0.9 slice_bitcast_fusion
  (14 shorter events, 0.0 us)
Async XLA Ops:
  0.0 29.1 %copy-start.2 = (bf16[128,256]{1,0:T(8,128)(2,1)S(1)}, bf16[128,256]{1,0:T(8,128)(2,1)}, u32[]{:S(2)}) copy-start(bf16[128,256]{1,0:T(8,128)(2,1)} %constant.32.clone.fx_ref) | copy-start | bytes 196612
  0.0 37.2 %copy-start.7 = (bf16[20,20]{1,0:T(8,128)(2,1)S(1)}, bf16[20,20]{1,0:T(8,128)(2,1)}, u32[]{:S(2)}) copy-start(bf16[20,20]{1,0:T(8,128)(2,1)} %param.20) | copy-start | bytes 2404
  9.1 28.2 %copy-start.6 = (bf16[2,2,20,20,64]{4,1,3,2,0:T(2,128)(2,1)S(1)}, bf16[2,2,20,20,64]{4,1,3,2,0:T(2,128)(2,1)}, u32[]{:S(2)}) copy-start(bf16[2,2,20,20,64]{4,1,3,2,0:T(2,128)(2,1)} %param.19) | copy-start | bytes 614404
  9.1 28.5 %copy-start.3 = (bf16[256,256]{1,0:T(8,128)(2,1)S(1)}, bf16[256,256]{1,0:T(8,128)(2,1)}, u32[]{:S(2)}) copy-start(bf16[256,256]{1,0:T(8,128)(2,1)} %constant.35.clone.place_ref) | copy-start | bytes 393220
  9.1 34.4 %copy-start.1 = (bf16[128,512]{1,0:T(8,128)(2,1)S(1)}, bf16[128,512]{1,0:T(8,128)(2,1)}, u32[]{:S(2)}) copy-start(bf16[128,512]{1,0:T(8,128)(2,1)} %constant.34.clone.spread_ref) | copy-start | bytes 393220
  30.2 13.3 %all-to-all-start.1 = ((bf16[16,40,128]{2,1,0:T(8,128)(2,1)}), bf16[16,40,128]{2,1,0:T(8,128)(2,1)S(1)}, u32[]{:S(2)}, u32[]{:S(2)}) async-start(bf16[16,40,128]{2,1,0:T(8,128)(2,1)} %bitcast.2), calls=%async_computation.1 | async-start | bytes 327680 | tf_op jit(solution)/shard_map/all_to_all | solution.py:486
  43.5 12.2 %copy-start.4 = (bf16[256,128]{1,0:T(8,128)(2,1)S(1)}, bf16[256,128]{1,0:T(8,128)(2,1)}, u32[]{:S(2)}) copy-start(bf16[256,128]{1,0:T(8,128)(2,1)} %constant.33.clone.ix_ref) | copy-start | bytes 196612
  45.5 10.2 %all-to-all-start.2 = ((bf16[16,40,128]{2,1,0:T(8,128)(2,1)}), bf16[16,40,128]{2,1,0:T(8,128)(2,1)S(1)}, u32[]{:S(2)}, u32[]{:S(2)}) async-start(bf16[16,40,128]{2,1,0:T(8,128)(2,1)} %bitcast.4), calls=%async_computation.2 | async-start | bytes 327680 | tf_op jit(solution)/shard_map/all_to_all | solution.py:486
  49.5 11.0 %copy-start.8 = (f32[20]{0:T(128)S(1)}, f32[20]{0:T(128)}, u32[]{:S(2)}) copy-start(f32[20]{0:T(128)} %param.21) | copy-start | bytes 244
  57.0 15.3 %all-to-all-start.3 = ((bf16[8,320,128]{2,1,0:T(8,128)(2,1)}), bf16[8,320,128]{2,1,0:T(8,128)(2,1)S(1)}, u32[]{:S(2)}, u32[]{:S(2)}) async-start(bf16[8,320,128]{2,1,0:T(8,128)(2,1)} %bitcast.7), calls=%async_computation.3 | async-start | bytes 1310720 | tf_op jit(solution)/shard_map/all_to_all | solution.py:486
  72.3 0.8 copy-start.5
  91.6 29.4 %copy-start = (bf16[512,512]{1,0:T(8,128)(2,1)S(1)}, bf16[512,512]{1,0:T(8,128)(2,1)}, u32[]{:S(2)}) copy-start(bf16[512,512]{1,0:T(8,128)(2,1)} %constant.24.clone.gather_ref) | copy-start | bytes 1572868

commit v3 on v2

--- a/solution.py
+++ b/solution.py
@@ -167,9 +167,8 @@
     field_refs, (fz_ref, fy_ref, un_ref, out_ref, modes_ref) = refs[: 2 * SUB], refs[2 * SUB :]
     step = pl.program_id(0)
 
-    for sub in range(SUB):
-
-        def lhs(pair, groups, sub=sub):
+    def lhs_of(sub):
+        def lhs(pair, groups):
             xl, c4 = 2 * sub + pair // 2, 2 * (pair % 2)
             rows = [
                 jnp.concatenate(
@@ -179,10 +178,12 @@
             ]
             return jnp.concatenate(rows, axis=0)
 
-        totals = [z_transform(lhs, fz_ref, un_ref, groups) for groups in HALVES]
-        for total, groups in zip(totals, HALVES):
-            for k, g in enumerate(groups):
-                y_transform(total[k * Y : (k + 1) * Y], fy_ref, modes_ref, g, step * SUB + sub)
+        return lhs
+
+    totals = [z_transform(lhs_of(sub), fz_ref, un_ref, range(G)) for sub in range(SUB)]
+    for g in range(G):
+        for sub in range(SUB):
+            y_transform(totals[sub][g * Y : (g + 1) * Y], fy_ref, modes_ref, g, step * SUB + sub)
 
     @pl.when(step == XP // SUB - 1)
     def _():
@@ -194,6 +195,10 @@
         pl.BlockSpec((1, 1, C, Y, Z), lambda i, k=k: (0, 2 * SUB * i + k, 0, 0, 0))
         for k in range(2 * SUB)
     ]
+
+
+def in_hbm(array):
+    return pltpu.with_memory_space_constraint(array, pltpu.HBM)
 
 
 def full(shape):
@@ -215,10 +220,10 @@
         out_specs=pl.BlockSpec((2560, 128), lambda i: (0, 0)),
         scratch_shapes=[pltpu.VMEM((2560, 128), f32)],
         compiler_params=pltpu.CompilerParams(
-            dimension_semantics=("arbitrary",), vmem_limit_bytes=54 << 20
+            dimension_semantics=("arbitrary",), vmem_limit_bytes=44 << 20
         ),
         name="analyse",
-    )(*[fields] * (2 * SUB), t["forward_z"], t["forward_y"], t["unscale"])
+    )(*map(in_hbm, [*[fields] * (2 * SUB), t["forward_z"], t["forward_y"], t["unscale"]]))
 
 
 def conv_kernel(*refs):
@@ -243,7 +248,7 @@
 def conv_call(fields, conv, bias):
     return pl.pallas_call(
         conv_kernel,
-        out_shape=[jax.ShapeDtypeStruct((XP // SUB, C, Y, Z), bf16)] * (2 * SUB),
+        out_shape=[pltpu.HBM((XP // SUB, C, Y, Z), bf16)] * (2 * SUB),
         grid=(XP // SUB,),
         in_specs=[
             *x_streams(),
@@ -252,13 +257,13 @@
         ],
         out_specs=[pl.BlockSpec((1, C, Y, Z), lambda i: (i, 0, 0, 0))] * (2 * SUB),
         compiler_params=pltpu.CompilerParams(
-            dimension_semantics=("arbitrary",), vmem_limit_bytes=54 << 20
+            dimension_semantics=("arbitrary",), vmem_limit_bytes=44 << 20
         ),
         cost_estimate=pl.CostEstimate(
             flops=2 * 16 * Y * Z * 320 * C, bytes_accessed=4 * 16 * C * Y * Z, transcendentals=0
         ),
         name="conv",
-    )(*[fields] * (2 * SUB), conv, bias)
+    )(*map(in_hbm, [fields] * (2 * SUB)), conv, bias)
 
 
 def slab_kernel(*refs):
@@ -320,8 +325,7 @@
     @pl.when(step == XP // SUB - 1)
     def _():
         lhs = lhs_of((SUB - 1) % 2)
-        for groups in HALVES:
-            analyse(lhs, fz_ref, fy_ref, un_ref, modes_ref, XP - 1, groups)
+        analyse(lhs, fz_ref, fy_ref, un_ref, modes_ref, XP - 1, range(G))
         out_ref[...] = modes_ref[...].astype(bf16)
 
 
@@ -349,11 +353,11 @@
             pltpu.VMEM((SUB, 4, 640, 256), bf16),
         ],
         compiler_params=pltpu.CompilerParams(
-            dimension_semantics=("arbitrary",), vmem_limit_bytes=54 << 20
+            dimension_semantics=("arbitrary",), vmem_limit_bytes=44 << 20
         ),
         name="slab",
     )(
-        *conv, *[cotangent] * (2 * SUB), mixed, t["inverse_y"], t["inverse_z"],
+        *map(in_hbm, [*conv, *[cotangent] * (2 * SUB)]), mixed, t["inverse_y"], t["inverse_z"],
         t["unscale_inverse"], t["forward_z"], t["forward_y"], t["unscale_back"],
     )
 

time: 125 us -> 118 us (0.944)
  Pallas kernels: 45.1 us -> 40.6 us
  local copies, waits for them, and re-layouts: 4.93 us -> 2.82 us
  waiting for transfers between devices: 10.5 us -> 11.9 us
    pallas_call x1, Pallas kernels: 18.4 us -> 16 us  [slab_call(): pl.pallas_call(slab_kernel, out_shape=jax.ShapeDtypeStruct((2560, 128), b...]
    pallas_call x1, Pallas kernels: 9.06 us -> 7.19 us  [analyse_call(): pl.pallas_call(analyse_kernel, out_shape=jax.ShapeDtypeStruct((2560, 128)...]
    all_to_all x3, waiting for transfers between devices: 10.5 us -> 11.9 us  [exchange(): lax.all_to_all(blocks, axis, split_axis=0, concat_axis=0, tiled=True)]
  transfers between devices with their start and end apart: 3 -> 3, of which waited for: 3 -> 3; matrix products, arithmetic and copies ran while one was open for 3% -> 2% of each run, Pallas kernels for 9% -> 9%
where the time goes in v3:
time: 118 us
  blocking collectives  47.8 us (41%)
  Pallas kernels  40.6 us (34%)
  starting transfers between devices  14.3 us (12%)
  waiting for transfers between devices  11.9 us (10%)
  local copies, waits for them, and re-layouts  2.82 us (2%)
    all_to_all x3, blocking collectives, exchange(): lax.all_to_all(blocks, axis, split_axis=0, concat_axis=0, tiled=True)  47.8 us
    pallas_call x1, Pallas kernels, slab_call(): pl.pallas_call(slab_kernel, out_shape=jax.ShapeDtypeStruct((2560, 128), b...  16 us
    all_to_all x3, starting transfers between devices, exchange(): lax.all_to_all(blocks, axis, split_axis=0, concat_axis=0, tiled=True)  14.3 us
    all_to_all x3, waiting for transfers between devices, exchange(): lax.all_to_all(blocks, axis, split_axis=0, concat_axis=0, tiled=True)  11.9 us
    pallas_call x1, Pallas kernels, conv_call(): pl.pallas_call(conv_kernel, out_shape=[pltpu.HBM((XP // SUB, C, Y, Z), bf...  10.2 us
    pallas_call x6, Pallas kernels, small_call(): pl.pallas_call(kernel, out_shape=out_shape, scratch_shapes=scratch, compi...  7.27 us
    pallas_call x1, Pallas kernels, analyse_call(): pl.pallas_call(analyse_kernel, out_shape=jax.ShapeDtypeStruct((2560, 128)...  7.19 us
  transfers between devices with their start and end apart: 3, of which 3 were waited for; matrix products, arithmetic and copies ran while one was open for 2% of the time, Pallas kernels for 9%

profile of v3, /device:TPU:1, one launch (start us, length us, event | category | flops | bytes accessed | tf_op | source)
XLA Modules:
  0.0 117.9 jit_solution(1252776298502641819)
XLA Ops:
  0.0 7.2 %analyse.1 = bf16[2560,128]{1,0:T(8,128)(2,1)S(1)} custom-call(bf16[1,16,20,128,128]{4,3,2,1,0:T(8,128)(2,1)} %refs_3_.3, bf16[1,16,20,128,128]{4,3,2,1,0:T(8,128)(2,1)} %refs_3_.3, bf16[1,16,20,128,128]{4,3,2,1,0:T(8,128)(2,1)} %refs_3_.3, bf16[1,16,20,128,128]{4,3,2,1,0:T(8,128)(2,1)} %refs_3_.3, bf16[4,256,256]{2,1,0:T(8,128)(2,1)} %constant.25.clone.refs_4_.refs_12_, ...), custom_call_target="tpu_custom_call" | custom-call | tf_op jit(solution)/shard_map/analyse/pallas_call | solution.py:210
  7.2 0.0 copy-start.6
  7.2 0.0 copy-start.3
  7.2 19.8 %all_to_all.30 = bf16[8,320,128]{2,1,0:T(8,128)(2,1)S(1)} all-to-all(bf16[8,320,128]{2,1,0:T(8,128)(2,1)S(1)} %bitcast.21), channel_id=1, replica_groups=mesh['dp'=16,'mp'=8] {'mp'}, dimensions={0} | all-to-all | bytes 1310720 | tf_op jit(solution)/shard_map/all_to_all | solution.py:490
  27.0 1.1 forward_x.2
  28.1 7.0 %all-to-all-start.1 = ((bf16[16,40,128]{2,1,0:T(8,128)(2,1)}), bf16[16,40,128]{2,1,0:T(8,128)(2,1)S(1)}, u32[]{:S(2)}, u32[]{:S(2)}) async-start(bf16[16,40,128]{2,1,0:T(8,128)(2,1)} %bitcast.2), calls=%async_computation.1 | async-start | bytes 327680 | tf_op jit(solution)/shard_map/all_to_all | solution.py:490
  35.1 0.1 copy.21
  35.2 0.1 copy.20
  35.3 0.2 reshape.62.w_ref
  35.5 0.3 weights.1.w_ref
  35.8 5.7 %all-to-all-done.1 = bf16[16,40,128]{2,1,0:T(8,128)(2,1)S(1)} async-done(((bf16[16,40,128]{2,1,0:T(8,128)(2,1)}), bf16[16,40,128]{2,1,0:T(8,128)(2,1)S(1)}, u32[]{:S(2)}, u32[]{:S(2)}) %all-to-all-start.1) | async-done | bytes 163872 | tf_op jit(solution)/shard_map/all_to_all | solution.py:490
  41.5 2.0 %mix.1 = bf16[640,128]{1,0:T(8,128)(2,1)} custom-call(bf16[640,128]{1,0:T(8,128)(2,1)S(1)} %bitcast.22, bf16[128,512]{1,0:T(8,128)(2,1)S(1)} %copy-done.3, f32[2,400,128]{2,1,0:T(8,128)S(1)} %weights.1.w_ref), custom_call_target="tpu_custom_call" | custom-call | tf_op jit(solution)/shard_map/mix/pallas_call | solution.py:366
  43.5 3.8 %all-to-all-start.2 = ((bf16[16,40,128]{2,1,0:T(8,128)(2,1)}), bf16[16,40,128]{2,1,0:T(8,128)(2,1)S(1)}, u32[]{:S(2)}, u32[]{:S(2)}) async-start(bf16[16,40,128]{2,1,0:T(8,128)(2,1)} %bitcast.4), calls=%async_computation.2 | async-start | bytes 327680 | tf_op jit(solution)/shard_map/all_to_all | solution.py:490
  47.3 0.2 broadcast_multiply_fusion
  47.5 1.2 %mul.20.refs_4_ = bf16[320,320]{1,0:T(8,128)(2,1)S(1)} reshape(bf16[20,16,20,16]{3,2,1,0:T(8,128)(2,1)S(1)} %broadcast_multiply_fusion) | data formatting | bytes 409600 | tf_op jit(solution)/shard_map/mul | solution.py:496
  48.7 5.0 %all-to-all-done.2 = bf16[16,40,128]{2,1,0:T(8,128)(2,1)S(1)} async-done(((bf16[16,40,128]{2,1,0:T(8,128)(2,1)}), bf16[16,40,128]{2,1,0:T(8,128)(2,1)S(1)}, u32[]{:S(2)}, u32[]{:S(2)}) %all-to-all-start.2) | async-done | bytes 163872 | tf_op jit(solution)/shard_map/all_to_all | solution.py:490
  53.7 1.3 %inverse_x.1 = bf16[2560,128]{1,0:T(8,128)(2,1)} custom-call(bf16[640,128]{1,0:T(8,128)(2,1)S(1)} %bitcast.24, bf16[256,128]{1,0:T(8,128)(2,1)S(1)} %copy-done.8), custom_call_target="tpu_custom_call" | custom-call | tf_op jit(solution)/shard_map/inverse_x/pallas_call | solution.py:366
  55.0 3.5 %all-to-all-start.3 = ((bf16[8,320,128]{2,1,0:T(8,128)(2,1)}), bf16[8,320,128]{2,1,0:T(8,128)(2,1)S(1)}, u32[]{:S(2)}, u32[]{:S(2)}) async-start(bf16[8,320,128]{2,1,0:T(8,128)(2,1)} %bitcast.7), calls=%async_computation.3 | async-start | bytes 1310720 | tf_op jit(solution)/shard_map/all_to_all | solution.py:490
  58.5 0.1 broadcast_in_dim.12
  58.6 0.1 broadcast_in_dim.13
  58.7 0.1 broadcast_in_dim.14.refs_5_
  58.8 0.0 copy-start
  58.8 0.0 copy-start.4
  58.8 0.0 copy-start.7
  58.9 10.2 %conv.1 = (bf16[4,20,128,128]{3,2,1,0:T(8,128)(2,1)}, bf16[4,20,128,128]{3,2,1,0:T(8,128)(2,1)}, bf16[4,20,128,128]{3,2,1,0:T(8,128)(2,1)}, bf16[4,20,128,128]{3,2,1,0:T(8,128)(2,1)}) custom-call(bf16[1,16,20,128,128]{4,3,2,1,0:T(8,128)(2,1)} %refs_3_.3, bf16[1,16,20,128,128]{4,3,2,1,0:T(8,128)(2,1)} %refs_3_.3, bf16[1,16,20,128,128]{4,3,2,1,0:T(8,128)(2,1)} %refs_3_.3, ...), custom_call_target="tpu_custom_call" | custom-call | flops 3355443200 | bytes 20971520 | tf_op jit(solution)/shard_map/conv/pallas_call | solution.py:249
  69.0 1.3 %all-to-all-done.3 = bf16[8,320,128]{2,1,0:T(8,128)(2,1)S(1)} async-done(((bf16[8,320,128]{2,1,0:T(8,128)(2,1)}), bf16[8,320,128]{2,1,0:T(8,128)(2,1)S(1)}, u32[]{:S(2)}, u32[]{:S(2)}) %all-to-all-start.3) | async-done | bytes 655392 | tf_op jit(solution)/shard_map/all_to_all | solution.py:490
  70.3 16.0 %slab.1 = bf16[2560,128]{1,0:T(8,128)(2,1)S(1)} custom-call(bf16[4,20,128,128]{3,2,1,0:T(8,128)(2,1)} %get-tuple-element.12.refs_0_, bf16[4,20,128,128]{3,2,1,0:T(8,128)(2,1)} %get-tuple-element.13.refs_1_, bf16[4,20,128,128]{3,2,1,0:T(8,128)(2,1)} %get-tuple-element.14.refs_2_, bf16[4,20,128,128]{3,2,1,0:T(8,128)(2,1)} %get-tuple-element.15.refs_3_, ...), custom_call_target="tpu_custom_call" | custom-call | tf_op jit(solution)/shard_map/slab/pallas_call | solution.py:333
  86.4 16.7 %all_to_all.31 = bf16[8,320,128]{2,1,0:T(8,128)(2,1)S(1)} all-to-all(bf16[8,320,128]{2,1,0:T(8,128)(2,1)S(1)} %bitcast.20), channel_id=1, replica_groups=mesh['dp'=16,'mp'=8] {'mp'}, dimensions={0} | all-to-all | bytes 1310720 | tf_op jit(solution)/shard_map/all_to_all | solution.py:490
  103.0 0.4 forward_x.3
  103.5 11.3 %all_to_all.32 = bf16[16,40,128]{2,1,0:T(8,128)(2,1)S(1)} all-to-all(bf16[16,40,128]{2,1,0:T(8,128)(2,1)S(1)} %bitcast.26), channel_id=1, replica_groups=mesh['dp'=16,'mp'=8] {'dp'}, dimensions={0} | all-to-all | bytes 327680 | tf_op jit(solution)/shard_map/all_to_all | solution.py:490
  114.8 2.2 %grad.1 = f32[1600,128]{1,0:T(8,128)S(1)} custom-call(bf16[640,128]{1,0:T(8,128)(2,1)S(1)} %bitcast.23, bf16[640,128]{1,0:T(8,128)(2,1)S(1)} %bitcast.25, bf16[128,512]{1,0:T(8,128)(2,1)S(1)} %copy-done.3, bf16[512,512]{1,0:T(8,128)(2,1)S(1)} %copy-done.2), custom_call_target="tpu_custom_call" | custom-call | tf_op jit(solution)/shard_map/grad/pallas_call | solution.py:366
  117.0 0.9 slice_bitcast_fusion
  (24 shorter events, 0.1 us)
Async XLA Ops:
  0.0 27.0 %copy-start.5 = (bf16[128,256]{1,0:T(8,128)(2,1)S(1)}, bf16[128,256]{1,0:T(8,128)(2,1)}, u32[]{:S(2)}) copy-start(bf16[128,256]{1,0:T(8,128)(2,1)} %constant.32.clone.fx_ref) | copy-start | bytes 196612
  0.0 35.1 %copy-start.12 = (bf16[20,20]{1,0:T(8,128)(2,1)S(1)}, bf16[20,20]{1,0:T(8,128)(2,1)}, u32[]{:S(2)}) copy-start(bf16[20,20]{1,0:T(8,128)(2,1)} %param.20) | copy-start | bytes 2404
  7.2 28.0 %copy-start.11 = (bf16[2,2,20,20,64]{4,1,3,2,0:T(2,128)(2,1)S(1)}, bf16[2,2,20,20,64]{4,1,3,2,0:T(2,128)(2,1)}, u32[]{:S(2)}) copy-start(bf16[2,2,20,20,64]{4,1,3,2,0:T(2,128)(2,1)} %param.19) | copy-start | bytes 614404
  7.2 28.3 %copy-start.6 = (bf16[256,256]{1,0:T(8,128)(2,1)S(1)}, bf16[256,256]{1,0:T(8,128)(2,1)}, u32[]{:S(2)}) copy-start(bf16[256,256]{1,0:T(8,128)(2,1)} %constant.35.clone.place_ref) | copy-start | bytes 393220
  7.2 34.2 %copy-start.3 = (bf16[128,512]{1,0:T(8,128)(2,1)S(1)}, bf16[128,512]{1,0:T(8,128)(2,1)}, u32[]{:S(2)}) copy-start(bf16[128,512]{1,0:T(8,128)(2,1)} %constant.34.clone.spread_ref) | copy-start | bytes 393220
  28.1 13.3 %all-to-all-start.1 = ((bf16[16,40,128]{2,1,0:T(8,128)(2,1)}), bf16[16,40,128]{2,1,0:T(8,128)(2,1)S(1)}, u32[]{:S(2)}, u32[]{:S(2)}) async-start(bf16[16,40,128]{2,1,0:T(8,128)(2,1)} %bitcast.2), calls=%async_computation.1 | async-start | bytes 327680 | tf_op jit(solution)/shard_map/all_to_all | solution.py:490
  41.5 12.2 %copy-start.8 = (bf16[256,128]{1,0:T(8,128)(2,1)S(1)}, bf16[256,128]{1,0:T(8,128)(2,1)}, u32[]{:S(2)}) copy-start(bf16[256,128]{1,0:T(8,128)(2,1)} %constant.33.clone.ix_ref) | copy-start | bytes 196612
  43.5 10.2 %all-to-all-start.2 = ((bf16[16,40,128]{2,1,0:T(8,128)(2,1)}), bf16[16,40,128]{2,1,0:T(8,128)(2,1)S(1)}, u32[]{:S(2)}, u32[]{:S(2)}) async-start(bf16[16,40,128]{2,1,0:T(8,128)(2,1)} %bitcast.4), calls=%async_computation.2 | async-start | bytes 327680 | tf_op jit(solution)/shard_map/all_to_all | solution.py:490
  47.5 11.0 %copy-start.13 = (f32[20]{0:T(128)S(1)}, f32[20]{0:T(128)}, u32[]{:S(2)}) copy-start(f32[20]{0:T(128)} %param.21) | copy-start | bytes 244
  55.0 15.3 %all-to-all-start.3 = ((bf16[8,320,128]{2,1,0:T(8,128)(2,1)}), bf16[8,320,128]{2,1,0:T(8,128)(2,1)S(1)}, u32[]{:S(2)}, u32[]{:S(2)}) async-start(bf16[8,320,128]{2,1,0:T(8,128)(2,1)} %bitcast.7), calls=%async_computation.3 | async-start | bytes 1310720 | tf_op jit(solution)/shard_map/all_to_all | solution.py:490
  58.8 11.5 %copy-start = (bf16[4,256,256]{2,1,0:T(8,128)(2,1)S(1)}, bf16[4,256,256]{2,1,0:T(8,128)(2,1)}, u32[]{:S(2)}) copy-start(bf16[4,256,256]{2,1,0:T(8,128)(2,1)} %constant.25.clone.refs_4_.refs_12_) | copy-start | bytes 1572868
  58.8 11.5 %copy-start.1 = (bf16[4,256,256]{2,1,0:T(8,128)(2,1)S(1)}, bf16[4,256,256]{2,1,0:T(8,128)(2,1)}, u32[]{:S(2)}) copy-start(bf16[4,256,256]{2,1,0:T(8,128)(2,1)} %constant.26.clone.refs_10_) | copy-start | bytes 1572868
  58.8 11.5 %copy-start.4 = (bf16[128,256]{1,0:T(8,128)(2,1)S(1)}, bf16[128,256]{1,0:T(8,128)(2,1)}, u32[]{:S(2)}) copy-start(bf16[128,256]{1,0:T(8,128)(2,1)} %constant.30.clone.refs_5_.refs_13_) | copy-start | bytes 196612
  58.8 11.5 %copy-start.7 = (bf16[256,128]{1,0:T(8,128)(2,1)S(1)}, bf16[256,128]{1,0:T(8,128)(2,1)}, u32[]{:S(2)}) copy-start(bf16[256,128]{1,0:T(8,128)(2,1)} %constant.31.clone.refs_9_) | copy-start | bytes 196612
  58.8 11.5 %copy-start.9 = (f32[1,256]{1,0:T(1,128)S(1)}, f32[1,256]{1,0:T(1,128)}, u32[]{:S(2)}) copy-start(f32[1,256]{1,0:T(1,128)} %constant.28.clone.refs_14_) | copy-start | bytes 3076
  58.8 11.5 %copy-start.10 = (f32[1,128]{1,0:T(1,128)S(1)}, f32[1,128]{1,0:T(1,128)}, u32[]{:S(2)}) copy-start(f32[1,128]{1,0:T(1,128)} %constant.29.clone.refs_11_) | copy-start | bytes 1540
  86.4 28.4 %copy-start.2 = (bf16[512,512]{1,0:T(8,128)(2,1)S(1)}, bf16[512,512]{1,0:T(8,128)(2,1)}, u32[]{:S(2)}) copy-start(bf16[512,512]{1,0:T(8,128)(2,1)} %constant.24.clone.gather_ref) | copy-start | bytes 1572868

commit v4 on v3

--- a/solution.py
+++ b/solution.py
@@ -70,8 +70,8 @@
         forward_z[q, :, 1, q, :] = (sin_z * scale[:, None]).T
         inverse_z[q // 2, 0, q, :, q % 2, :] = cos_z * scale[:, None]
         inverse_z[q // 2, 1, q, :, q % 2, :] = -sin_z * scale[:, None]
-    unscale = np.tile(1.0 / scale, 16)[None, :]
-    unscale_back = np.tile(0.5 * weight / scale, 16)[None, :]
+    unscale = np.tile(1.0 / scale, 8)[None, :]
+    unscale_back = np.tile(0.5 * weight / scale, 8)[None, :]
     unscale_inverse = np.tile(INV_ROOT_TWO * weight / scale, 8)[None, :]
     phase_y = angles(kept(KY, Y), Y)
     cos_y, sin_y = np.cos(phase_y), np.sin(phase_y)
@@ -137,11 +137,11 @@
     return jnp.dot(a, b, preferred_element_type=f32)
 
 
-def z_transform(lhs_of, fz_ref, un_ref, groups):
+def z_transform(lhs_of, fz_ref, groups):
     total = mm(lhs_of(0, groups), fz_ref[0])
     for pair in range(1, 4):
         total = total + mm(lhs_of(pair, groups), fz_ref[pair])
-    return total * un_ref[...]
+    return total
 
 
 def y_transform(part, fy_ref, modes_ref, g, at):
@@ -154,8 +154,8 @@
         modes_ref[pl.ds(j * 320 + g * 64 + at, 8, stride=8), :] = modes[j * 8 : (j + 1) * 8]
 
 
-def analyse(lhs_of, fz_ref, fy_ref, un_ref, modes_ref, at, groups):
-    total = z_transform(lhs_of, fz_ref, un_ref, groups)
+def analyse(lhs_of, fz_ref, fy_ref, modes_ref, at, groups):
+    total = z_transform(lhs_of, fz_ref, groups)
     for k, g in enumerate(groups):
         y_transform(total[k * Y : (k + 1) * Y], fy_ref, modes_ref, g, at)
 
@@ -164,7 +164,7 @@
 
 
 def analyse_kernel(*refs):
-    field_refs, (fz_ref, fy_ref, un_ref, out_ref, modes_ref) = refs[: 2 * SUB], refs[2 * SUB :]
+    field_refs, (fz_ref, fy_ref, out_ref, modes_ref) = refs[: 2 * SUB], refs[2 * SUB :]
     step = pl.program_id(0)
 
     def lhs_of(sub):
@@ -180,7 +180,7 @@
 
         return lhs
 
-    totals = [z_transform(lhs_of(sub), fz_ref, un_ref, range(G)) for sub in range(SUB)]
+    totals = [z_transform(lhs_of(sub), fz_ref, range(G)) for sub in range(SUB)]
     for g in range(G):
         for sub in range(SUB):
             y_transform(totals[sub][g * Y : (g + 1) * Y], fy_ref, modes_ref, g, step * SUB + sub)
@@ -215,7 +215,6 @@
             *x_streams(),
             full((4, 256, 256)),
             full((128, 256)),
-            full((1, 256)),
         ],
         out_specs=pl.BlockSpec((2560, 128), lambda i: (0, 0)),
         scratch_shapes=[pltpu.VMEM((2560, 128), f32)],
@@ -223,7 +222,7 @@
             dimension_semantics=("arbitrary",), vmem_limit_bytes=44 << 20
         ),
         name="analyse",
-    )(*map(in_hbm, [*[fields] * (2 * SUB), t["forward_z"], t["forward_y"], t["unscale"]]))
+    )(*map(in_hbm, [*[fields] * (2 * SUB), t["forward_z"], t["forward_y"]]))
 
 
 def conv_kernel(*refs):
@@ -268,15 +267,15 @@
 
 def slab_kernel(*refs):
     conv_refs, cot_refs = refs[: 2 * SUB], refs[2 * SUB : 4 * SUB]
-    mixed_ref, iy_ref, iz_ref, uni_ref, fz_ref, fy_ref, un_ref, out_ref = refs[4 * SUB : 4 * SUB + 8]
-    modes_ref, mixed_f32, wave_ref, delta_ref = refs[4 * SUB + 8 :]
+    mixed_ref, iy_ref, iz_ref, fz_ref, fy_ref, out_ref = refs[4 * SUB : 4 * SUB + 6]
+    modes_ref, mixed_f32, wave_ref, delta_ref = refs[4 * SUB + 6 :]
     step = pl.program_id(0)
 
     def wave(at, slot, g):
         rows = [mixed_f32[pl.ds(j * 320 + g * 64 + at, 8, stride=8), :] for j in range(MP)]
         part = jnp.concatenate(rows, axis=0).astype(bf16)
         out = mm(iy_ref[...], jnp.concatenate([part, part], axis=0))
-        out = (out * uni_ref[...]).astype(bf16)
+        out = out.astype(bf16)
         wave_ref[slot, g * Y : (g + 1) * Y, :128] = out[:Y]
         wave_ref[slot, g * Y : (g + 1) * Y, 128:] = out[Y:]
 
@@ -315,7 +314,7 @@
                 spectral.append(mm(wave_ref[slot], iz_ref[pair + 1]))
             delta(sub, pair, spectral[pair])
             if pair < 2:
-                totals.append(z_transform(lhs, fz_ref, un_ref, HALVES[pair]))
+                totals.append(z_transform(lhs, fz_ref, HALVES[pair]))
             else:
                 for k, g in enumerate(HALVES[pair - 2]):
                     y_transform(totals[pair - 2][k * Y : (k + 1) * Y], fy_ref, modes_ref, g, before)
@@ -325,7 +324,8 @@
     @pl.when(step == XP // SUB - 1)
     def _():
         lhs = lhs_of((SUB - 1) % 2)
-        analyse(lhs, fz_ref, fy_ref, un_ref, modes_ref, XP - 1, range(G))
+        for groups in HALVES:
+            analyse(lhs, fz_ref, fy_ref, modes_ref, XP - 1, groups)
         out_ref[...] = modes_ref[...].astype(bf16)
 
 
@@ -340,10 +340,8 @@
             full((2560, 128)),
             full((256, 128)),
             full((4, 256, 256)),
-            full((1, 128)),
             full((4, 256, 256)),
             full((128, 256)),
-            full((1, 256)),
         ],
         out_specs=pl.BlockSpec((2560, 128), lambda i: (0, 0)),
         scratch_shapes=[
@@ -358,7 +356,7 @@
         name="slab",
     )(
         *map(in_hbm, [*conv, *[cotangent] * (2 * SUB)]), mixed, t["inverse_y"], t["inverse_z"],
-        t["unscale_inverse"], t["forward_z"], t["forward_y"], t["unscale_back"],
+        t["forward_z"], t["forward_y"],
     )
 
 
@@ -376,7 +374,7 @@
     return lax.broadcasted_iota(jnp.int32, (64, 128), 1) < 64
 
 
-def forward_x_kernel(in_ref, fx_ref, out_ref, wide_ref):
+def forward_x_kernel(in_ref, fx_ref, un_ref, out_ref, wide_ref):
     low = lower_half()
     for gk in range(GA):
         cols = []
@@ -387,19 +385,19 @@
         out = mm(fx_ref[...], jnp.concatenate([right, right], axis=0))
         first = jnp.where(low, out[:64, :128], out[64:, 128:])
         second = jnp.where(low, out[:64, 128:], out[64:, :128])
-        res = first + pltpu.roll(second, 64, 1)
+        res = (first + pltpu.roll(second, 64, 1)) * un_ref[...]
         for r in range(4):
             wide_ref[pl.ds(r * GA + gk, 16, stride=40), :] = res[r * 16 : (r + 1) * 16]
     out_ref[...] = wide_ref[...].astype(bf16)
 
 
-def inverse_x_kernel(in_ref, ix_ref, out_ref, wide_ref):
+def inverse_x_kernel(in_ref, ix_ref, un_ref, out_ref, wide_ref):
     wide_ref[...] = in_ref[...].astype(f32)
     low = lax.broadcasted_iota(jnp.int32, (128, 128), 1) < 64
     for gk in range(GA):
         rows = [wide_ref[pl.ds(r * GA + gk, 16, stride=40), :] for r in range(4)]
         part = jnp.concatenate(rows, axis=0).astype(bf16)
-        out = mm(ix_ref[...], jnp.concatenate([part, part], axis=0))
+        out = mm(ix_ref[...], jnp.concatenate([part, part], axis=0)) * un_ref[...]
         first = jnp.where(low, out[:128], pltpu.roll(out[128:], 64, 1)).astype(bf16)
         second = jnp.where(low, pltpu.roll(out[:128], 64, 1), out[128:]).astype(bf16)
         for b, value in enumerate((first, second)):
@@ -458,31 +456,45 @@
     out_ref[...] = wide_ref[...].astype(bf16)
 
 
-def grad_kernel(s_ref, b_ref, spread_ref, gather_ref, out_ref, wide_ref, rows_ref, chan_ref, sum_ref):
+def grad_kernel(
+    s_ref, b_ref, spread_ref, gather_ref, out_ref, wide_ref, rows_ref, chan_ref, line_ref, sum_ref
+):
     spread_channels(s_ref, spread_ref, wide_ref, rows_ref, chan_ref)
+    for r in range(40):
+        for c4 in range(4):
+            kxl, part, g, kya = r // 20, r // 10 % 2, r // 2 % 5, r % 2
+            first = ((kxl * 2 + part) * 2 + kya) * 384 + 4 * g + c4
+            line_ref[pl.ds(first, 16, stride=24), :] = chan_ref[
+                r * 16 : (r + 1) * 16, c4 * 128 : (c4 + 1) * 128
+            ]
     wide_ref[...] = b_ref[...].astype(f32)
     for kxl in range(2):
         for kya in range(2):
-            b_re = [wide_ref[pl.ds(kxl * 20 + g * 2 + kya, 16, stride=40), :] for g in range(G)]
-            b_im = [wide_ref[pl.ds(kxl * 20 + g * 2 + kya + 10, 16, stride=40), :] for g in range(G)]
-            for c in range(C):
-                s_re, s_im = channel_parts(chan_ref, kxl, kya, c)
-                for go in range(G):
-                    line = kxl * 100 + c * G + go
-                    real = s_re * b_re[go] + s_im * b_im[go]
-                    imag = s_re * b_im[go] - s_im * b_re[go]
-                    lanes = slice(kya * 128, kya * 128 + 128)
-                    sum_ref[line : line + 1, lanes] = jnp.sum(real, axis=0, keepdims=True)
-                    sum_ref[200 + line : 201 + line, lanes] = jnp.sum(imag, axis=0, keepdims=True)
-    sums = sum_ref[...]
+            base = (kxl * 4 + kya) * 384
+            for go in range(G):
+                real = jnp.zeros((24, 128), f32)
+                imag = jnp.zeros((24, 128), f32)
+                for s in range(DP):
+                    row = s * 40 + kxl * 20 + go * 2 + kya
+                    b_re = wide_ref[row : row + 1, :]
+                    b_im = wide_ref[row + 10 : row + 11, :]
+                    s_re = line_ref[base + s * 24 : base + s * 24 + 24, :]
+                    s_im = line_ref[base + 768 + s * 24 : base + 768 + s * 24 + 24, :]
+                    real = real + (s_re * b_re + s_im * b_im)
+                    imag = imag + (s_re * b_im - s_im * b_re)
+                first = kya * 400 + kxl * 100 + go
+                sum_ref[pl.ds(first, C, stride=G), :] = real[:C]
+                sum_ref[pl.ds(first + 200, C, stride=G), :] = imag[:C]
+    sums = jnp.concatenate([sum_ref[:400, :], sum_ref[400:, :]], axis=1)
     upper = sums.astype(bf16)
     lower = (sums - upper.astype(f32)).astype(bf16)
     placed = mm(jnp.concatenate([upper, lower], axis=1), gather_ref[...])
     for o in range(4):
         for part in range(2):
-            out_ref[pl.ds(o * 2 + part, 200, stride=8), :] = placed[
+            line_ref[pl.ds(o * 2 + part, 200, stride=8), :] = placed[
                 part * 200 : (part + 1) * 200, o * 128 : o * 128 + 128
             ]
+    out_ref[...] = line_ref[:1600, :64]
 
 
 def exchange(values, axis, count):
@@ -498,11 +510,11 @@
 
     bias = jnp.broadcast_to(conv_bias[:, None, None], (C, 16, 128)).reshape(320, 128)
 
-    def to_kx(modes):
+    def to_kx(modes, unscale):
         moved = exchange(modes, "mp", MP)
         part = small_call(
             forward_x_kernel, "forward_x", jax.ShapeDtypeStruct((640, 128), bf16),
-            [pltpu.VMEM((640, 128), f32)], moved, t["forward_x"],
+            [pltpu.VMEM((640, 128), f32)], moved, t["forward_x"], unscale,
         )
         return exchange(part, "dp", DP)
 
@@ -510,23 +522,24 @@
         weight_kernel, "weights", jax.ShapeDtypeStruct((2, 400, 128), f32),
         [pltpu.VMEM((1600, 64), f32)], spectral_weight.reshape(1600, 64), t["place"],
     )
-    spectra = to_kx(analyse_call(fields, t))
+    weights, conv, bias = lax.optimization_barrier((weights, conv, bias))
+    spectra = to_kx(analyse_call(fields, t), t["unscale"])
     mixed = small_call(
         mix_kernel, "mix", jax.ShapeDtypeStruct((640, 128), bf16), SPREAD_SCRATCH,
         spectra, t["spread"], weights,
     )
     slabs = small_call(
         inverse_x_kernel, "inverse_x", jax.ShapeDtypeStruct((2560, 128), bf16),
-        [pltpu.VMEM((640, 128), f32)], exchange(mixed, "dp", DP), t["inverse_x"],
+        [pltpu.VMEM((640, 128), f32)], exchange(mixed, "dp", DP), t["inverse_x"], t["unscale_inverse"],
     )
     slabs, conv = lax.optimization_barrier((slabs, conv))
     conv_term = conv_call(fields, conv, bias)
-    back = to_kx(slab_call(conv_term, cotangent, exchange(slabs, "mp", MP), t))
+    back = to_kx(slab_call(conv_term, cotangent, exchange(slabs, "mp", MP), t), t["unscale_back"])
     grad = small_call(
-        grad_kernel, "grad", jax.ShapeDtypeStruct((1600, 128), f32),
-        (*SPREAD_SCRATCH, pltpu.VMEM((400, 256), f32)), spectra, back, t["spread"], t["gather"],
-    )
-    return jnp.transpose(grad.reshape(2, C, C, 2, 128)[..., :64], (0, 3, 1, 2, 4))
+        grad_kernel, "grad", jax.ShapeDtypeStruct((1600, 64), f32),
+        (*SPREAD_SCRATCH, pltpu.VMEM((3072, 128), f32), pltpu.VMEM((800, 128), f32)), spectra, back, t["spread"], t["gather"],
+    )
+    return jnp.transpose(grad.reshape(2, C, C, 2, 64), (0, 3, 1, 2, 4))
 
 
 def solution(mesh):

time: 118 us -> 118 us (level)
  blocking collectives: 47.8 us -> 37.7 us
  starting transfers between devices: 14.3 us -> 18.4 us
  waiting for transfers between devices: 11.9 us -> 14.6 us
  Pallas kernels: 40.6 us -> 42 us
  other arithmetic: 0.2 us -> 1.49 us
    all_to_all x3, blocking collectives: 47.8 us -> 37.7 us  [exchange(): lax.all_to_all(blocks, axis, split_axis=0, concat_axis=0, tiled=True)]
    all_to_all x3, starting transfers between devices: 14.3 us -> 18.4 us  [exchange(): lax.all_to_all(blocks, axis, split_axis=0, concat_axis=0, tiled=True)]
    all_to_all x3, waiting for transfers between devices: 11.9 us -> 14.6 us  [exchange(): lax.all_to_all(blocks, axis, split_axis=0, concat_axis=0, tiled=True)]
    mul x1, local copies, waits for them, and re-layouts: 1.2 us -> 2.86 us  [shards(): conv_weight.T[:, None, :, None] * jnp.eye(16, dtype=bf16)[None, :, None, :]]
    mul x1, other arithmetic: 0.19 us -> 1.49 us  [shards(): conv_weight.T[:, None, :, None] * jnp.eye(16, dtype=bf16)[None, :, None, :]]
  transfers between devices with their start and end apart: 3 -> 3, of which waited for: 3 -> 3; matrix products, arithmetic and copies ran while one was open for 2% -> 4% of each run, Pallas kernels for 9% -> 9%
where the time goes in v4:
time: 118 us
  Pallas kernels  42 us (36%)
  blocking collectives  37.7 us (32%)
  starting transfers between devices  18.4 us (16%)
  waiting for transfers between devices  14.6 us (12%)
  local copies, waits for them, and re-layouts  3.52 us (3%)
  other arithmetic  1.49 us (1%)
    all_to_all x3, blocking collectives, exchange(): lax.all_to_all(blocks, axis, split_axis=0, concat_axis=0, tiled=True)  37.7 us
    all_to_all x3, starting transfers between devices, exchange(): lax.all_to_all(blocks, axis, split_axis=0, concat_axis=0, tiled=True)  18.4 us
    pallas_call x1, Pallas kernels, slab_call(): pl.pallas_call(slab_kernel, out_shape=jax.ShapeDtypeStruct((2560, 128), b...  16.3 us
    all_to_all x3, waiting for transfers between devices, exchange(): lax.all_to_all(blocks, axis, split_axis=0, concat_axis=0, tiled=True)  14.6 us
    pallas_call x1, Pallas kernels, conv_call(): pl.pallas_call(conv_kernel, out_shape=[pltpu.HBM((XP // SUB, C, Y, Z), bf...  10.2 us
    pallas_call x1, Pallas kernels, analyse_call(): pl.pallas_call(analyse_kernel, out_shape=jax.ShapeDtypeStruct((2560, 128)...  7.95 us
    pallas_call x6, Pallas kernels, small_call(): pl.pallas_call(kernel, out_shape=out_shape, scratch_shapes=scratch, compi...  7.55 us
    mul x1, local copies, waits for them, and re-layouts, shards(): conv_weight.T[:, None, :, None] * jnp.eye(16, dtype=bf16)[None, :, None, :]  2.86 us
  transfers between devices with their start and end apart: 3, of which 3 were waited for; matrix products, arithmetic and copies ran while one was open for 4% of the time, Pallas kernels for 9%

profile of v4, /device:TPU:1, one launch (start us, length us, event | category | flops | bytes accessed | tf_op | source)
XLA Modules:
  0.0 117.8 jit_solution(12027178250108530099)
XLA Ops:
  0.0 7.9 %analyse.1 = bf16[2560,128]{1,0:T(8,128)(2,1)} custom-call(bf16[1,16,20,128,128]{4,3,2,1,0:T(8,128)(2,1)} %refs_3_.3, bf16[1,16,20,128,128]{4,3,2,1,0:T(8,128)(2,1)} %refs_3_.3, bf16[1,16,20,128,128]{4,3,2,1,0:T(8,128)(2,1)} %refs_3_.3, bf16[1,16,20,128,128]{4,3,2,1,0:T(8,128)(2,1)} %refs_3_.3, bf16[4,256,256]{2,1,0:T(8,128)(2,1)} %constant.25.clone.refs_4_.refs_11_, ...), custom_call_target="tpu_custom_call" | custom-call | tf_op jit(solution)/shard_map/analyse/pallas_call | solution.py:210
  8.0 8.5 %all-to-all-start = ((bf16[8,320,128]{2,1,0:T(8,128)(2,1)}), bf16[8,320,128]{2,1,0:T(8,128)(2,1)S(1)}, u32[]{:S(2)}, u32[]{:S(2)}) async-start(bf16[8,320,128]{2,1,0:T(8,128)(2,1)} %bitcast), calls=%async_computation | async-start | bytes 1310720 | tf_op jit(solution)/shard_map/all_to_all | solution.py:502
  16.4 0.0 copy-done.13
  16.4 0.1 copy.21
  16.5 0.1 broadcast_in_dim.12
  16.6 0.1 broadcast_in_dim.13
  16.7 0.1 copy.20
  16.8 0.2 reshape.62.w_ref
  17.0 11.3 %all-to-all-done = bf16[8,320,128]{2,1,0:T(8,128)(2,1)S(1)} async-done(((bf16[8,320,128]{2,1,0:T(8,128)(2,1)}), bf16[8,320,128]{2,1,0:T(8,128)(2,1)S(1)}, u32[]{:S(2)}, u32[]{:S(2)}) %all-to-all-start) | async-done | bytes 655392 | tf_op jit(solution)/shard_map/all_to_all | solution.py:502
  28.3 1.1 forward_x.2
  29.4 6.0 %all-to-all-start.1 = ((bf16[16,40,128]{2,1,0:T(8,128)(2,1)}), bf16[16,40,128]{2,1,0:T(8,128)(2,1)S(1)}, u32[]{:S(2)}, u32[]{:S(2)}) async-start(bf16[16,40,128]{2,1,0:T(8,128)(2,1)} %bitcast.2), calls=%async_computation.1 | async-start | bytes 327680 | tf_op jit(solution)/shard_map/all_to_all | solution.py:502
  35.4 1.5 %broadcast_multiply_fusion = bf16[20,16,20,16]{3,2,1,0:T(8,128)(2,1)} fusion(bf16[16,16]{1,0:T(8,128)(2,1)S(1)} %fusion, bf16[20,20]{1,0:T(8,128)(2,1)S(1)} %copy.21), kind=kLoop, calls=%fused_computation | loop fusion | flops 102400 | bytes 206112 | tf_op jit(solution)/shard_map/mul | solution.py:508
  36.9 2.9 %mul.20.refs_4_ = bf16[320,320]{1,0:T(8,128)(2,1)S(1)} reshape(bf16[20,16,20,16]{3,2,1,0:T(8,128)(2,1)} %broadcast_multiply_fusion) | data formatting | bytes 409600 | tf_op jit(solution)/shard_map/mul | solution.py:508
  39.7 0.3 weights.1.w_ref
  40.0 0.1 broadcast_in_dim.14.refs_5_
  40.1 1.6 %all-to-all-done.1 = bf16[16,40,128]{2,1,0:T(8,128)(2,1)S(1)} async-done(((bf16[16,40,128]{2,1,0:T(8,128)(2,1)}), bf16[16,40,128]{2,1,0:T(8,128)(2,1)S(1)}, u32[]{:S(2)}, u32[]{:S(2)}) %all-to-all-start.1) | async-done | bytes 163872 | tf_op jit(solution)/shard_map/all_to_all | solution.py:502
  41.7 1.4 %mix.1 = bf16[640,128]{1,0:T(8,128)(2,1)S(1)} custom-call(bf16[640,128]{1,0:T(8,128)(2,1)S(1)} %bitcast.20, bf16[128,512]{1,0:T(8,128)(2,1)S(1)} %copy-done.2, f32[2,400,128]{2,1,0:T(8,128)S(1)} %weights.1.w_ref), custom_call_target="tpu_custom_call" | custom-call | tf_op jit(solution)/shard_map/mix/pallas_call | solution.py:364
  43.1 10.3 %all_to_all.30 = bf16[16,40,128]{2,1,0:T(8,128)(2,1)S(1)} all-to-all(bf16[16,40,128]{2,1,0:T(8,128)(2,1)S(1)} %bitcast.25), channel_id=1, replica_groups=mesh['dp'=16,'mp'=8] {'dp'}, dimensions={0} | all-to-all | bytes 327680 | tf_op jit(solution)/shard_map/all_to_all | solution.py:502
  53.4 1.3 %inverse_x.1 = bf16[2560,128]{1,0:T(8,128)(2,1)} custom-call(bf16[640,128]{1,0:T(8,128)(2,1)S(1)} %bitcast.23, bf16[256,128]{1,0:T(8,128)(2,1)S(1)} %copy-done.8, f32[1,128]{1,0:T(1,128)S(1)} %copy-done.10), custom_call_target="tpu_custom_call" | custom-call | tf_op jit(solution)/shard_map/inverse_x/pallas_call | solution.py:364
  54.7 3.9 %all-to-all-start.3 = ((bf16[8,320,128]{2,1,0:T(8,128)(2,1)}), bf16[8,320,128]{2,1,0:T(8,128)(2,1)S(1)}, u32[]{:S(2)}, u32[]{:S(2)}) async-start(bf16[8,320,128]{2,1,0:T(8,128)(2,1)} %bitcast.7), calls=%async_computation.3 | async-start | bytes 1310720 | tf_op jit(solution)/shard_map/all_to_all | solution.py:502
  58.6 0.0 copy-start.3
  58.7 0.0 copy-start.4
  58.7 0.0 copy-start.7
  58.7 10.2 %conv.1 = (bf16[4,20,128,128]{3,2,1,0:T(8,128)(2,1)}, bf16[4,20,128,128]{3,2,1,0:T(8,128)(2,1)}, bf16[4,20,128,128]{3,2,1,0:T(8,128)(2,1)}, bf16[4,20,128,128]{3,2,1,0:T(8,128)(2,1)}) custom-call(bf16[1,16,20,128,128]{4,3,2,1,0:T(8,128)(2,1)} %refs_3_.3, bf16[1,16,20,128,128]{4,3,2,1,0:T(8,128)(2,1)} %refs_3_.3, bf16[1,16,20,128,128]{4,3,2,1,0:T(8,128)(2,1)} %refs_3_.3, ...), custom_call_target="tpu_custom_call" | custom-call | flops 3355443200 | bytes 20971520 | tf_op jit(solution)/shard_map/conv/pallas_call | solution.py:248
  68.8 1.8 %all-to-all-done.3 = bf16[8,320,128]{2,1,0:T(8,128)(2,1)S(1)} async-done(((bf16[8,320,128]{2,1,0:T(8,128)(2,1)}), bf16[8,320,128]{2,1,0:T(8,128)(2,1)S(1)}, u32[]{:S(2)}, u32[]{:S(2)}) %all-to-all-start.3) | async-done | bytes 655392 | tf_op jit(solution)/shard_map/all_to_all | solution.py:502
  70.6 0.0 copy-start.9
  70.6 16.3 %slab.1 = bf16[2560,128]{1,0:T(8,128)(2,1)S(1)} custom-call(bf16[4,20,128,128]{3,2,1,0:T(8,128)(2,1)} %get-tuple-element.18.refs_0_, bf16[4,20,128,128]{3,2,1,0:T(8,128)(2,1)} %get-tuple-element.19.refs_1_, bf16[4,20,128,128]{3,2,1,0:T(8,128)(2,1)} %get-tuple-element.20.refs_2_, bf16[4,20,128,128]{3,2,1,0:T(8,128)(2,1)} %get-tuple-element.21.refs_3_, ...), custom_call_target="tpu_custom_call" | custom-call | tf_op jit(solution)/shard_map/slab/pallas_call | solution.py:333
  86.9 0.0 copy-start.1
  86.9 15.7 %all_to_all.31 = bf16[8,320,128]{2,1,0:T(8,128)(2,1)S(1)} all-to-all(bf16[8,320,128]{2,1,0:T(8,128)(2,1)S(1)} %bitcast.19), channel_id=1, replica_groups=mesh['dp'=16,'mp'=8] {'mp'}, dimensions={0} | all-to-all | bytes 1310720 | tf_op jit(solution)/shard_map/all_to_all | solution.py:502
  102.7 0.4 forward_x.3
  103.1 11.6 %all_to_all.32 = bf16[16,40,128]{2,1,0:T(8,128)(2,1)S(1)} all-to-all(bf16[16,40,128]{2,1,0:T(8,128)(2,1)S(1)} %bitcast.24), channel_id=1, replica_groups=mesh['dp'=16,'mp'=8] {'dp'}, dimensions={0} | all-to-all | bytes 327680 | tf_op jit(solution)/shard_map/all_to_all | solution.py:502
  114.8 3.1 %grad.1 = f32[1600,64]{1,0:T(8,128)} custom-call(bf16[640,128]{1,0:T(8,128)(2,1)S(1)} %bitcast.21, bf16[640,128]{1,0:T(8,128)(2,1)S(1)} %bitcast.22, bf16[128,512]{1,0:T(8,128)(2,1)S(1)} %copy-done.2, bf16[512,512]{1,0:T(8,128)(2,1)S(1)} %copy-done.1), custom_call_target="tpu_custom_call" | custom-call | tf_op jit(solution)/shard_map/grad/pallas_call | solution.py:364
  (25 shorter events, 0.1 us)
Async XLA Ops:
  0.0 16.4 %copy-start.13 = (bf16[20,20]{1,0:T(8,128)(2,1)S(1)}, bf16[20,20]{1,0:T(8,128)(2,1)}, u32[]{:S(2)}) copy-start(bf16[20,20]{1,0:T(8,128)(2,1)} %param.20) | copy-start | bytes 2404
  0.0 16.5 %copy-start.14 = (f32[20]{0:T(128)S(1)}, f32[20]{0:T(128)}, u32[]{:S(2)}) copy-start(f32[20]{0:T(128)} %param.21) | copy-start | bytes 244
  0.0 16.7 %copy-start.12 = (bf16[2,2,20,20,64]{4,1,3,2,0:T(2,128)(2,1)S(1)}, bf16[2,2,20,20,64]{4,1,3,2,0:T(2,128)(2,1)}, u32[]{:S(2)}) copy-start(bf16[2,2,20,20,64]{4,1,3,2,0:T(2,128)(2,1)} %param.19) | copy-start | bytes 614404
  8.0 20.3 %copy-start.5 = (bf16[128,256]{1,0:T(8,128)(2,1)S(1)}, bf16[128,256]{1,0:T(8,128)(2,1)}, u32[]{:S(2)}) copy-start(bf16[128,256]{1,0:T(8,128)(2,1)} %constant.32.clone.fx_ref) | copy-start | bytes 196612
  8.0 20.3 %copy-start.11 = (f32[1,128]{1,0:T(1,128)S(1)}, f32[1,128]{1,0:T(1,128)}, u32[]{:S(2)}) copy-start(f32[1,128]{1,0:T(1,128)} %constant.27.clone.un_ref) | copy-start | bytes 1540
  8.0 20.3 %all-to-all-start = ((bf16[8,320,128]{2,1,0:T(8,128)(2,1)}), bf16[8,320,128]{2,1,0:T(8,128)(2,1)S(1)}, u32[]{:S(2)}, u32[]{:S(2)}) async-start(bf16[8,320,128]{2,1,0:T(8,128)(2,1)} %bitcast), calls=%async_computation | async-start | bytes 1310720 | tf_op jit(solution)/shard_map/all_to_all | solution.py:502
  28.3 11.5 %copy-start.6 = (bf16[256,256]{1,0:T(8,128)(2,1)S(1)}, bf16[256,256]{1,0:T(8,128)(2,1)}, u32[]{:S(2)}) copy-start(bf16[256,256]{1,0:T(8,128)(2,1)} %constant.35.clone.place_ref) | copy-start | bytes 393220
  29.4 12.3 %all-to-all-start.1 = ((bf16[16,40,128]{2,1,0:T(8,128)(2,1)}), bf16[16,40,128]{2,1,0:T(8,128)(2,1)S(1)}, u32[]{:S(2)}, u32[]{:S(2)}) async-start(bf16[16,40,128]{2,1,0:T(8,128)(2,1)} %bitcast.2), calls=%async_computation.1 | async-start | bytes 327680 | tf_op jit(solution)/shard_map/all_to_all | solution.py:502
  35.4 6.3 %copy-start.2 = (bf16[128,512]{1,0:T(8,128)(2,1)S(1)}, bf16[128,512]{1,0:T(8,128)(2,1)}, u32[]{:S(2)}) copy-start(bf16[128,512]{1,0:T(8,128)(2,1)} %constant.34.clone.spread_ref) | copy-start | bytes 393220
  36.9 16.6 %copy-start.8 = (bf16[256,128]{1,0:T(8,128)(2,1)S(1)}, bf16[256,128]{1,0:T(8,128)(2,1)}, u32[]{:S(2)}) copy-start(bf16[256,128]{1,0:T(8,128)(2,1)} %constant.33.clone.ix_ref) | copy-start | bytes 196612
  36.9 16.6 %copy-start.10 = (f32[1,128]{1,0:T(1,128)S(1)}, f32[1,128]{1,0:T(1,128)}, u32[]{:S(2)}) copy-start(f32[1,128]{1,0:T(1,128)} %constant.29.clone.un_ref) | copy-start | bytes 1540
  54.7 15.9 %all-to-all-start.3 = ((bf16[8,320,128]{2,1,0:T(8,128)(2,1)}), bf16[8,320,128]{2,1,0:T(8,128)(2,1)S(1)}, u32[]{:S(2)}, u32[]{:S(2)}) async-start(bf16[8,320,128]{2,1,0:T(8,128)(2,1)} %bitcast.7), calls=%async_computation.3 | async-start | bytes 1310720 | tf_op jit(solution)/shard_map/all_to_all | solution.py:502
  58.6 12.0 %copy-start = (bf16[4,256,256]{2,1,0:T(8,128)(2,1)S(1)}, bf16[4,256,256]{2,1,0:T(8,128)(2,1)}, u32[]{:S(2)}) copy-start(bf16[4,256,256]{2,1,0:T(8,128)(2,1)} %constant.25.clone.refs_4_.refs_11_) | copy-start | bytes 1572868
  58.6 12.0 %copy-start.3 = (bf16[4,256,256]{2,1,0:T(8,128)(2,1)S(1)}, bf16[4,256,256]{2,1,0:T(8,128)(2,1)}, u32[]{:S(2)}) copy-start(bf16[4,256,256]{2,1,0:T(8,128)(2,1)} %constant.26.clone.refs_10_) | copy-start | bytes 1572868
  58.7 11.9 %copy-start.4 = (bf16[128,256]{1,0:T(8,128)(2,1)S(1)}, bf16[128,256]{1,0:T(8,128)(2,1)}, u32[]{:S(2)}) copy-start(bf16[128,256]{1,0:T(8,128)(2,1)} %constant.30.clone.refs_5_.refs_12_) | copy-start | bytes 196612
  58.7 11.9 %copy-start.7 = (bf16[256,128]{1,0:T(8,128)(2,1)S(1)}, bf16[256,128]{1,0:T(8,128)(2,1)}, u32[]{:S(2)}) copy-start(bf16[256,128]{1,0:T(8,128)(2,1)} %constant.31.clone.refs_9_) | copy-start | bytes 196612
  70.6 32.1 %copy-start.9 = (f32[1,128]{1,0:T(1,128)S(1)}, f32[1,128]{1,0:T(1,128)}, u32[]{:S(2)}) copy-start(f32[1,128]{1,0:T(1,128)} %constant.28.clone.un_ref) | copy-start | bytes 1540
  86.9 27.8 %copy-start.1 = (bf16[512,512]{1,0:T(8,128)(2,1)S(1)}, bf16[512,512]{1,0:T(8,128)(2,1)}, u32[]{:S(2)}) copy-start(bf16[512,512]{1,0:T(8,128)(2,1)} %constant.24.clone.gather_ref) | copy-start | bytes 1572868

commit v5 on v4

--- a/solution.py
+++ b/solution.py
@@ -226,8 +226,26 @@
 
 
 def conv_kernel(*refs):
-    field_refs, (conv_ref, bias_ref), out_refs = refs[: 2 * SUB], refs[2 * SUB : -2 * SUB], refs[-2 * SUB :]
-    bias = jnp.concatenate([bias_ref[...], bias_ref[...]], axis=1)
+    field_refs, (w_ref, bias_ref) = refs[: 2 * SUB], refs[2 * SUB : 2 * SUB + 2]
+    out_refs, (conv_ref, lines_ref) = refs[2 * SUB + 2 : 4 * SUB + 2], refs[4 * SUB + 2 :]
+
+    @pl.when(pl.program_id(0) == 0)
+    def _():
+        def picks(shape, along):
+            long = lax.broadcasted_iota(jnp.int32, shape, along) >> 4
+            return jnp.where(long == lax.broadcasted_iota(jnp.int32, shape, 1 - along), 1.0, 0.0).astype(bf16)
+
+        by_row = lax.dot_general(
+            picks((320, C), 0), w_ref[...], (((1,), (1,)), ((), ())), preferred_element_type=f32
+        ).astype(bf16)
+        spread = mm(by_row, picks((C, 320), 1))
+        row = lax.broadcasted_iota(jnp.int32, (320, 320), 0) & 15
+        column = lax.broadcasted_iota(jnp.int32, (320, 320), 1) & 15
+        conv_ref[...] = jnp.where(row == column, spread, 0.0).astype(bf16)
+        for o in range(C):
+            lines_ref[o * 16 : (o + 1) * 16, :] = jnp.full((16, 256), bias_ref[o], f32)
+
+    bias = lines_ref[...]
     for xl in range(2 * SUB):
         for yp in range(4):
             right = jnp.concatenate(
@@ -251,10 +269,11 @@
         grid=(XP // SUB,),
         in_specs=[
             *x_streams(),
-            full((320, 320)),
-            full((320, 128)),
+            full((C, C)),
+            pl.BlockSpec(memory_space=pltpu.SMEM),
         ],
         out_specs=[pl.BlockSpec((1, C, Y, Z), lambda i: (i, 0, 0, 0))] * (2 * SUB),
+        scratch_shapes=[pltpu.VMEM((320, 320), bf16), pltpu.VMEM((320, 256), f32)],
         compiler_params=pltpu.CompilerParams(
             dimension_semantics=("arbitrary",), vmem_limit_bytes=44 << 20
         ),
@@ -485,7 +504,7 @@
                 first = kya * 400 + kxl * 100 + go
                 sum_ref[pl.ds(first, C, stride=G), :] = real[:C]
                 sum_ref[pl.ds(first + 200, C, stride=G), :] = imag[:C]
-    sums = jnp.concatenate([sum_ref[:400, :], sum_ref[400:, :]], axis=1)
+    sums = jnp.concatenate([sum_ref[:400, :], sum_ref[400:800, :]], axis=1)
     upper = sums.astype(bf16)
     lower = (sums - upper.astype(f32)).astype(bf16)
     placed = mm(jnp.concatenate([upper, lower], axis=1), gather_ref[...])
@@ -504,26 +523,19 @@
 
 def shards(fields, cotangent, spectral_weight, conv_weight, conv_bias):
     t = {name: jnp.asarray(value) for name, value in tables().items()}
-    conv = (
-        conv_weight.T[:, None, :, None] * jnp.eye(16, dtype=bf16)[None, :, None, :]
-    ).reshape(320, 320)
-
-    bias = jnp.broadcast_to(conv_bias[:, None, None], (C, 16, 128)).reshape(320, 128)
-
-    def to_kx(modes, unscale):
-        moved = exchange(modes, "mp", MP)
-        part = small_call(
+    def to_kx(moved, unscale):
+        return small_call(
             forward_x_kernel, "forward_x", jax.ShapeDtypeStruct((640, 128), bf16),
             [pltpu.VMEM((640, 128), f32)], moved, t["forward_x"], unscale,
         )
-        return exchange(part, "dp", DP)
-
+
+    moved = exchange(analyse_call(fields, t), "mp", MP)
+    moved, spectral_weight = lax.optimization_barrier((moved, spectral_weight))
+    spectra = exchange(to_kx(moved, t["unscale"]), "dp", DP)
     weights = small_call(
         weight_kernel, "weights", jax.ShapeDtypeStruct((2, 400, 128), f32),
         [pltpu.VMEM((1600, 64), f32)], spectral_weight.reshape(1600, 64), t["place"],
     )
-    weights, conv, bias = lax.optimization_barrier((weights, conv, bias))
-    spectra = to_kx(analyse_call(fields, t), t["unscale"])
     mixed = small_call(
         mix_kernel, "mix", jax.ShapeDtypeStruct((640, 128), bf16), SPREAD_SCRATCH,
         spectra, t["spread"], weights,
@@ -532,12 +544,13 @@
         inverse_x_kernel, "inverse_x", jax.ShapeDtypeStruct((2560, 128), bf16),
         [pltpu.VMEM((640, 128), f32)], exchange(mixed, "dp", DP), t["inverse_x"], t["unscale_inverse"],
     )
-    slabs, conv = lax.optimization_barrier((slabs, conv))
-    conv_term = conv_call(fields, conv, bias)
-    back = to_kx(slab_call(conv_term, cotangent, exchange(slabs, "mp", MP), t), t["unscale_back"])
+    slabs, conv_weight = lax.optimization_barrier((slabs, conv_weight))
+    conv_term = conv_call(fields, conv_weight, conv_bias)
+    back_modes = slab_call(conv_term, cotangent, exchange(slabs, "mp", MP), t)
+    back = exchange(to_kx(exchange(back_modes, "mp", MP), t["unscale_back"]), "dp", DP)
     grad = small_call(
         grad_kernel, "grad", jax.ShapeDtypeStruct((1600, 64), f32),
-        (*SPREAD_SCRATCH, pltpu.VMEM((3072, 128), f32), pltpu.VMEM((800, 128), f32)), spectra, back, t["spread"], t["gather"],
+        (*SPREAD_SCRATCH, pltpu.VMEM((3072, 128), f32), pltpu.VMEM((840, 128), f32)), spectra, back, t["spread"], t["gather"],
     )
     return jnp.transpose(grad.reshape(2, C, C, 2, 64), (0, 3, 1, 2, 4))
 

time: 118 us -> 116 us (0.983)
  blocking collectives: 37.7 us -> 56.5 us
  starting transfers between devices: 18.4 us -> 10.5 us
  waiting for transfers between devices: 14.6 us -> 7.65 us
  local copies, waits for them, and re-layouts: 3.52 us -> 0.32 us
  other arithmetic: 1.49 us -> 0 us
  Pallas kernels: 42 us -> 40.7 us
    all_to_all x3 -> x4, blocking collectives: 37.7 us -> 56.5 us  [exchange(): lax.all_to_all(blocks, axis, split_axis=0, concat_axis=0, tiled=True)]
    all_to_all x3 -> x2, starting transfers between devices: 18.4 us -> 10.5 us  [exchange(): lax.all_to_all(blocks, axis, split_axis=0, concat_axis=0, tiled=True)]
    all_to_all x3 -> x2, waiting for transfers between devices: 14.6 us -> 7.65 us  [exchange(): lax.all_to_all(blocks, axis, split_axis=0, concat_axis=0, tiled=True)]
    mul x1 -> x0, local copies, waits for them, and re-layouts: 2.86 us -> none  [shards(): conv_weight.T[:, None, :, None] * jnp.eye(16, dtype=bf16)[None, :, None, :]]
    mul x1 -> x0, other arithmetic: 1.49 us -> none  [shards(): conv_weight.T[:, None, :, None] * jnp.eye(16, dtype=bf16)[None, :, None, :]]
  transfers between devices with their start and end apart: 3 -> 2, of which waited for: 3 -> 2; matrix products, arithmetic and copies ran while one was open for 4% -> 0% of each run, Pallas kernels for 9% -> 9%
where the time goes in v5:
time: 116 us
  blocking collectives  56.5 us (49%)
  Pallas kernels  40.7 us (35%)
  starting transfers between devices  10.5 us (9%)
  waiting for transfers between devices  7.65 us (7%)
    all_to_all x4, blocking collectives, exchange(): lax.all_to_all(blocks, axis, split_axis=0, concat_axis=0, tiled=True)  56.5 us
    pallas_call x1, Pallas kernels, slab_call(): pl.pallas_call(slab_kernel, out_shape=jax.ShapeDtypeStruct((2560, 128), b...  16.3 us
    all_to_all x2, starting transfers between devices, exchange(): lax.all_to_all(blocks, axis, split_axis=0, concat_axis=0, tiled=True)  10.5 us
    pallas_call x1, Pallas kernels, conv_call(): pl.pallas_call(conv_kernel, out_shape=[pltpu.HBM((XP // SUB, C, Y, Z), bf...  9.81 us
    all_to_all x2, waiting for transfers between devices, exchange(): lax.all_to_all(blocks, axis, split_axis=0, concat_axis=0, tiled=True)  7.65 us
    pallas_call x6, Pallas kernels, small_call(): pl.pallas_call(kernel, out_shape=out_shape, scratch_shapes=scratch, compi...  7.45 us
    pallas_call x1, Pallas kernels, analyse_call(): pl.pallas_call(analyse_kernel, out_shape=jax.ShapeDtypeStruct((2560, 128)...  7.11 us
  transfers between devices with their start and end apart: 2, of which 2 were waited for; matrix products, arithmetic and copies ran while one was open for 0% of the time, Pallas kernels for 9%

profile of v5, /device:TPU:1, one launch (start us, length us, event | category | flops | bytes accessed | tf_op | source)
XLA Modules:
  0.0 115.9 jit_solution(10687563012116330156)
XLA Ops:
  0.0 7.1 %analyse.1 = bf16[2560,128]{1,0:T(8,128)(2,1)S(1)} custom-call(bf16[1,16,20,128,128]{4,3,2,1,0:T(8,128)(2,1)} %refs_3_.3, bf16[1,16,20,128,128]{4,3,2,1,0:T(8,128)(2,1)} %refs_3_.3, bf16[1,16,20,128,128]{4,3,2,1,0:T(8,128)(2,1)} %refs_3_.3, bf16[1,16,20,128,128]{4,3,2,1,0:T(8,128)(2,1)} %refs_3_.3, bf16[4,256,256]{2,1,0:T(8,128)(2,1)} %constant.25.clone.refs_4_.refs_11_, ...), custom_call_target="tpu_custom_call" | custom-call | tf_op jit(solution)/shard_map/analyse/pallas_call | solution.py:210
  7.1 0.0 copy-start.14
  7.1 0.0 copy-start.6
  7.1 0.0 copy-start.2
  7.2 19.8 %all_to_all.30 = bf16[8,320,128]{2,1,0:T(8,128)(2,1)S(1)} all-to-all(bf16[8,320,128]{2,1,0:T(8,128)(2,1)S(1)} %bitcast.17), channel_id=1, replica_groups=mesh['dp'=16,'mp'=8] {'mp'}, dimensions={0} | all-to-all | bytes 1310720 | tf_op jit(solution)/shard_map/all_to_all | solution.py:521
  27.0 0.0 copy-done.5
  27.0 1.1 forward_x.2
  28.1 7.0 %all-to-all-start.1 = ((bf16[16,40,128]{2,1,0:T(8,128)(2,1)}), bf16[16,40,128]{2,1,0:T(8,128)(2,1)S(1)}, u32[]{:S(2)}, u32[]{:S(2)}) async-start(bf16[16,40,128]{2,1,0:T(8,128)(2,1)} %bitcast.2), calls=%async_computation.1 | async-start | bytes 327680 | tf_op jit(solution)/shard_map/all_to_all | solution.py:521
  35.1 0.1 copy.19
  35.1 0.0 copy-start.9
  35.1 0.0 copy-start.10
  35.2 0.2 reshape.46.w_ref
  35.3 0.3 weights.1.w_ref
  35.6 5.8 %all-to-all-done.1 = bf16[16,40,128]{2,1,0:T(8,128)(2,1)S(1)} async-done(((bf16[16,40,128]{2,1,0:T(8,128)(2,1)}), bf16[16,40,128]{2,1,0:T(8,128)(2,1)S(1)}, u32[]{:S(2)}, u32[]{:S(2)}) %all-to-all-start.1) | async-done | bytes 163872 | tf_op jit(solution)/shard_map/all_to_all | solution.py:521
  41.4 1.3 %mix.1 = bf16[640,128]{1,0:T(8,128)(2,1)S(1)} custom-call(bf16[640,128]{1,0:T(8,128)(2,1)S(1)} %bitcast.20, bf16[128,512]{1,0:T(8,128)(2,1)S(1)} %copy-done.2, f32[2,400,128]{2,1,0:T(8,128)S(1)} %weights.1.w_ref), custom_call_target="tpu_custom_call" | custom-call | tf_op jit(solution)/shard_map/mix/pallas_call | solution.py:383
  42.7 9.3 %all_to_all.31 = bf16[16,40,128]{2,1,0:T(8,128)(2,1)S(1)} all-to-all(bf16[16,40,128]{2,1,0:T(8,128)(2,1)S(1)} %bitcast.25), channel_id=1, replica_groups=mesh['dp'=16,'mp'=8] {'dp'}, dimensions={0} | all-to-all | bytes 327680 | tf_op jit(solution)/shard_map/all_to_all | solution.py:521
  52.1 1.3 %inverse_x.1 = bf16[2560,128]{1,0:T(8,128)(2,1)} custom-call(bf16[640,128]{1,0:T(8,128)(2,1)S(1)} %bitcast.23, bf16[256,128]{1,0:T(8,128)(2,1)S(1)} %copy-done.8, f32[1,128]{1,0:T(1,128)S(1)} %copy-done.12), custom_call_target="tpu_custom_call" | custom-call | tf_op jit(solution)/shard_map/inverse_x/pallas_call | solution.py:383
  53.3 3.5 %all-to-all-start.3 = ((bf16[8,320,128]{2,1,0:T(8,128)(2,1)}), bf16[8,320,128]{2,1,0:T(8,128)(2,1)S(1)}, u32[]{:S(2)}, u32[]{:S(2)}) async-start(bf16[8,320,128]{2,1,0:T(8,128)(2,1)} %bitcast.6), calls=%async_computation.3 | async-start | bytes 1310720 | tf_op jit(solution)/shard_map/all_to_all | solution.py:521
  56.9 0.0 copy-start
  56.9 0.0 copy-start.3
  56.9 0.0 copy-start.4
  56.9 0.0 copy-start.7
  56.9 9.8 %conv.1 = (bf16[4,20,128,128]{3,2,1,0:T(8,128)(2,1)}, bf16[4,20,128,128]{3,2,1,0:T(8,128)(2,1)}, bf16[4,20,128,128]{3,2,1,0:T(8,128)(2,1)}, bf16[4,20,128,128]{3,2,1,0:T(8,128)(2,1)}) custom-call(bf16[1,16,20,128,128]{4,3,2,1,0:T(8,128)(2,1)} %refs_3_.3, bf16[1,16,20,128,128]{4,3,2,1,0:T(8,128)(2,1)} %refs_3_.3, bf16[1,16,20,128,128]{4,3,2,1,0:T(8,128)(2,1)} %refs_3_.3, ...), custom_call_target="tpu_custom_call" | custom-call | flops 3355443200 | bytes 20971520 | tf_op jit(solution)/shard_map/conv/pallas_call | solution.py:266
  66.8 1.9 %all-to-all-done.3 = bf16[8,320,128]{2,1,0:T(8,128)(2,1)S(1)} async-done(((bf16[8,320,128]{2,1,0:T(8,128)(2,1)}), bf16[8,320,128]{2,1,0:T(8,128)(2,1)S(1)}, u32[]{:S(2)}, u32[]{:S(2)}) %all-to-all-start.3) | async-done | bytes 655392 | tf_op jit(solution)/shard_map/all_to_all | solution.py:521
  68.6 0.0 copy-done
  68.7 0.0 copy-start.11
  68.7 16.3 %slab.1 = bf16[2560,128]{1,0:T(8,128)(2,1)S(1)} custom-call(bf16[4,20,128,128]{3,2,1,0:T(8,128)(2,1)} %get-tuple-element.16.refs_0_, bf16[4,20,128,128]{3,2,1,0:T(8,128)(2,1)} %get-tuple-element.17.refs_1_, bf16[4,20,128,128]{3,2,1,0:T(8,128)(2,1)} %get-tuple-element.18.refs_2_, bf16[4,20,128,128]{3,2,1,0:T(8,128)(2,1)} %get-tuple-element.19.refs_3_, ...), custom_call_target="tpu_custom_call" | custom-call | tf_op jit(solution)/shard_map/slab/pallas_call | solution.py:352
  85.0 0.0 copy-start.1
  85.0 16.1 %all_to_all.32 = bf16[8,320,128]{2,1,0:T(8,128)(2,1)S(1)} all-to-all(bf16[8,320,128]{2,1,0:T(8,128)(2,1)S(1)} %bitcast.19), channel_id=1, replica_groups=mesh['dp'=16,'mp'=8] {'mp'}, dimensions={0} | all-to-all | bytes 1310720 | tf_op jit(solution)/shard_map/all_to_all | solution.py:521
  101.1 0.4 forward_x.3
  101.5 11.3 %all_to_all.33 = bf16[16,40,128]{2,1,0:T(8,128)(2,1)S(1)} all-to-all(bf16[16,40,128]{2,1,0:T(8,128)(2,1)S(1)} %bitcast.24), channel_id=1, replica_groups=mesh['dp'=16,'mp'=8] {'dp'}, dimensions={0} | all-to-all | bytes 327680 | tf_op jit(solution)/shard_map/all_to_all | solution.py:521
  112.8 3.1 %grad.1 = f32[1600,64]{1,0:T(8,128)} custom-call(bf16[640,128]{1,0:T(8,128)(2,1)S(1)} %bitcast.21, bf16[640,128]{1,0:T(8,128)(2,1)S(1)} %bitcast.22, bf16[128,512]{1,0:T(8,128)(2,1)S(1)} %copy-done.2, bf16[512,512]{1,0:T(8,128)(2,1)S(1)} %copy-done.1), custom_call_target="tpu_custom_call" | custom-call | tf_op jit(solution)/shard_map/grad/pallas_call | solution.py:383
  (17 shorter events, 0.0 us)
Async XLA Ops:
  0.0 27.0 %copy-start.5 = (bf16[128,256]{1,0:T(8,128)(2,1)S(1)}, bf16[128,256]{1,0:T(8,128)(2,1)}, u32[]{:S(2)}) copy-start(bf16[128,256]{1,0:T(8,128)(2,1)} %constant.32.clone.fx_ref) | copy-start | bytes 196612
  0.0 27.0 %copy-start.13 = (f32[1,128]{1,0:T(1,128)S(1)}, f32[1,128]{1,0:T(1,128)}, u32[]{:S(2)}) copy-start(f32[1,128]{1,0:T(1,128)} %constant.27.clone.un_ref) | copy-start | bytes 1540
  7.1 27.9 %copy-start.14 = (bf16[2,2,20,20,64]{4,1,3,2,0:T(2,128)(2,1)S(1)}, bf16[2,2,20,20,64]{4,1,3,2,0:T(2,128)(2,1)}, u32[]{:S(2)}) copy-start(bf16[2,2,20,20,64]{4,1,3,2,0:T(2,128)(2,1)} %param.19) | copy-start | bytes 614404
  7.1 28.2 %copy-start.6 = (bf16[256,256]{1,0:T(8,128)(2,1)S(1)}, bf16[256,256]{1,0:T(8,128)(2,1)}, u32[]{:S(2)}) copy-start(bf16[256,256]{1,0:T(8,128)(2,1)} %constant.35.clone.place_ref) | copy-start | bytes 393220
  7.1 34.2 %copy-start.2 = (bf16[128,512]{1,0:T(8,128)(2,1)S(1)}, bf16[128,512]{1,0:T(8,128)(2,1)}, u32[]{:S(2)}) copy-start(bf16[128,512]{1,0:T(8,128)(2,1)} %constant.34.clone.spread_ref) | copy-start | bytes 393220
  27.0 25.1 %copy-start.8 = (bf16[256,128]{1,0:T(8,128)(2,1)S(1)}, bf16[256,128]{1,0:T(8,128)(2,1)}, u32[]{:S(2)}) copy-start(bf16[256,128]{1,0:T(8,128)(2,1)} %constant.33.clone.ix_ref) | copy-start | bytes 196612
  27.0 25.1 %copy-start.12 = (f32[1,128]{1,0:T(1,128)S(1)}, f32[1,128]{1,0:T(1,128)}, u32[]{:S(2)}) copy-start(f32[1,128]{1,0:T(1,128)} %constant.29.clone.un_ref) | copy-start | bytes 1540
  28.1 13.3 %all-to-all-start.1 = ((bf16[16,40,128]{2,1,0:T(8,128)(2,1)}), bf16[16,40,128]{2,1,0:T(8,128)(2,1)S(1)}, u32[]{:S(2)}, u32[]{:S(2)}) async-start(bf16[16,40,128]{2,1,0:T(8,128)(2,1)} %bitcast.2), calls=%async_computation.1 | async-start | bytes 327680 | tf_op jit(solution)/shard_map/all_to_all | solution.py:521
  35.1 21.7 %copy-start.9 = (bf16[20,20]{1,0:T(8,128)(2,1)S(1)}, bf16[20,20]{1,0:T(8,128)(2,1)}, u32[]{:S(2)}) copy-start(bf16[20,20]{1,0:T(8,128)(2,1)} %refs_4_.2) | copy-start | bytes 2404
  35.1 21.7 %copy-start.10 = (f32[20]{0:T(128)S(1)}, f32[20]{0:T(128)}, u32[]{:S(2)}) copy-start(f32[20]{0:T(128)} %refs_5_.3) | copy-start | bytes 244
  53.3 15.3 %all-to-all-start.3 = ((bf16[8,320,128]{2,1,0:T(8,128)(2,1)}), bf16[8,320,128]{2,1,0:T(8,128)(2,1)S(1)}, u32[]{:S(2)}, u32[]{:S(2)}) async-start(bf16[8,320,128]{2,1,0:T(8,128)(2,1)} %bitcast.6), calls=%async_computation.3 | async-start | bytes 1310720 | tf_op jit(solution)/shard_map/all_to_all | solution.py:521
  56.9 11.7 %copy-start = (bf16[4,256,256]{2,1,0:T(8,128)(2,1)S(1)}, bf16[4,256,256]{2,1,0:T(8,128)(2,1)}, u32[]{:S(2)}) copy-start(bf16[4,256,256]{2,1,0:T(8,128)(2,1)} %constant.25.clone.refs_4_.refs_11_) | copy-start | bytes 1572868
  56.9 11.7 %copy-start.3 = (bf16[4,256,256]{2,1,0:T(8,128)(2,1)S(1)}, bf16[4,256,256]{2,1,0:T(8,128)(2,1)}, u32[]{:S(2)}) copy-start(bf16[4,256,256]{2,1,0:T(8,128)(2,1)} %constant.26.clone.refs_10_) | copy-start | bytes 1572868
  56.9 11.7 %copy-start.4 = (bf16[128,256]{1,0:T(8,128)(2,1)S(1)}, bf16[128,256]{1,0:T(8,128)(2,1)}, u32[]{:S(2)}) copy-start(bf16[128,256]{1,0:T(8,128)(2,1)} %constant.30.clone.refs_5_.refs_12_) | copy-start | bytes 196612
  56.9 11.7 %copy-start.7 = (bf16[256,128]{1,0:T(8,128)(2,1)S(1)}, bf16[256,128]{1,0:T(8,128)(2,1)}, u32[]{:S(2)}) copy-start(bf16[256,128]{1,0:T(8,128)(2,1)} %constant.31.clone.refs_9_) | copy-start | bytes 196612
  68.7 32.4 %copy-start.11 = (f32[1,128]{1,0:T(1,128)S(1)}, f32[1,128]{1,0:T(1,128)}, u32[]{:S(2)}) copy-start(f32[1,128]{1,0:T(1,128)} %constant.28.clone.un_ref) | copy-start | bytes 1540
  85.0 27.8 %copy-start.1 = (bf16[512,512]{1,0:T(8,128)(2,1)S(1)}, bf16[512,512]{1,0:T(8,128)(2,1)}, u32[]{:S(2)}) copy-start(bf16[512,512]{1,0:T(8,128)(2,1)} %constant.24.clone.gather_ref) | copy-start | bytes 1572868

commit v6 on v5

--- a/solution.py
+++ b/solution.py
@@ -490,20 +490,21 @@
     for kxl in range(2):
         for kya in range(2):
             base = (kxl * 4 + kya) * 384
-            for go in range(G):
-                real = jnp.zeros((24, 128), f32)
-                imag = jnp.zeros((24, 128), f32)
-                for s in range(DP):
+            real = [jnp.zeros((24, 128), f32) for _ in range(G)]
+            imag = [jnp.zeros((24, 128), f32) for _ in range(G)]
+            for s in range(DP):
+                s_re = line_ref[base + s * 24 : base + s * 24 + 24, :]
+                s_im = line_ref[base + 768 + s * 24 : base + 768 + s * 24 + 24, :]
+                for go in range(G):
                     row = s * 40 + kxl * 20 + go * 2 + kya
                     b_re = wide_ref[row : row + 1, :]
                     b_im = wide_ref[row + 10 : row + 11, :]
-                    s_re = line_ref[base + s * 24 : base + s * 24 + 24, :]
-                    s_im = line_ref[base + 768 + s * 24 : base + 768 + s * 24 + 24, :]
-                    real = real + (s_re * b_re + s_im * b_im)
-                    imag = imag + (s_re * b_im - s_im * b_re)
+                    real[go] = real[go] + (s_re * b_re + s_im * b_im)
+                    imag[go] = imag[go] + (s_re * b_im - s_im * b_re)
+            for go in range(G):
                 first = kya * 400 + kxl * 100 + go
-                sum_ref[pl.ds(first, C, stride=G), :] = real[:C]
-                sum_ref[pl.ds(first + 200, C, stride=G), :] = imag[:C]
+                sum_ref[pl.ds(first, C, stride=G), :] = real[go][:C]
+                sum_ref[pl.ds(first + 200, C, stride=G), :] = imag[go][:C]
     sums = jnp.concatenate([sum_ref[:400, :], sum_ref[400:800, :]], axis=1)
     upper = sums.astype(bf16)
     lower = (sums - upper.astype(f32)).astype(bf16)
@@ -530,12 +531,12 @@
         )
 
     moved = exchange(analyse_call(fields, t), "mp", MP)
-    moved, spectral_weight = lax.optimization_barrier((moved, spectral_weight))
-    spectra = exchange(to_kx(moved, t["unscale"]), "dp", DP)
     weights = small_call(
         weight_kernel, "weights", jax.ShapeDtypeStruct((2, 400, 128), f32),
         [pltpu.VMEM((1600, 64), f32)], spectral_weight.reshape(1600, 64), t["place"],
     )
+    moved, weights = lax.optimization_barrier((moved, weights))
+    spectra = exchange(to_kx(moved, t["unscale"]), "dp", DP)
     mixed = small_call(
         mix_kernel, "mix", jax.ShapeDtypeStruct((640, 128), bf16), SPREAD_SCRATCH,
         spectra, t["spread"], weights,

time: 116 us -> 116 us (level)
  blocking collectives: 56.5 us -> 48.6 us
  waiting for transfers between devices: 7.65 us -> 13.3 us
  starting transfers between devices: 10.5 us -> 12.4 us
    all_to_all x4, blocking collectives: 56.5 us -> 48.6 us  [exchange(): lax.all_to_all(blocks, axis, split_axis=0, concat_axis=0, tiled=True)]
    all_to_all x2, waiting for transfers between devices: 7.65 us -> 13.3 us  [exchange(): lax.all_to_all(blocks, axis, split_axis=0, concat_axis=0, tiled=True)]
    all_to_all x2, starting transfers between devices: 10.5 us -> 12.4 us  [exchange(): lax.all_to_all(blocks, axis, split_axis=0, concat_axis=0, tiled=True)]
where the time goes in v6:
time: 116 us; the launch traced here: 115 us
  blocking collectives  48.6 us (42%)
  Pallas kernels  40.6 us (35%)
  waiting for transfers between devices  13.3 us (11%)
  starting transfers between devices  12.4 us (11%)
    all_to_all x4, blocking collectives, exchange(): lax.all_to_all(blocks, axis, split_axis=0, concat_axis=0, tiled=True)  48.6 us
    pallas_call x1, Pallas kernels, slab_call(): pl.pallas_call(slab_kernel, out_shape=jax.ShapeDtypeStruct((2560, 128), b...  16.3 us
    all_to_all x2, waiting for transfers between devices, exchange(): lax.all_to_all(blocks, axis, split_axis=0, concat_axis=0, tiled=True)  13.3 us
    all_to_all x2, starting transfers between devices, exchange(): lax.all_to_all(blocks, axis, split_axis=0, concat_axis=0, tiled=True)  12.4 us
    pallas_call x1, Pallas kernels, conv_call(): pl.pallas_call(conv_kernel, out_shape=[pltpu.HBM((XP // SUB, C, Y, Z), bf...  9.86 us
    pallas_call x1, Pallas kernels, analyse_call(): pl.pallas_call(analyse_kernel, out_shape=jax.ShapeDtypeStruct((2560, 128)...  7.94 us
    pallas_call x6, Pallas kernels, small_call(): pl.pallas_call(kernel, out_shape=out_shape, scratch_shapes=scratch, compi...  6.55 us
  transfers between devices with their start and end apart: 2, of which 2 were waited for; matrix products, arithmetic and copies ran while one was open for 0% of the time, Pallas kernels for 9%

profile of v6, /device:TPU:1, one launch (start us, length us, event | category | flops | bytes accessed | tf_op | source)
XLA Modules:
  0.0 115.4 jit_solution(12961832438314006438)
XLA Ops:
  0.0 7.9 %analyse.1 = bf16[2560,128]{1,0:T(8,128)(2,1)} custom-call(bf16[1,16,20,128,128]{4,3,2,1,0:T(8,128)(2,1)} %refs_3_.3, bf16[1,16,20,128,128]{4,3,2,1,0:T(8,128)(2,1)} %refs_3_.3, bf16[1,16,20,128,128]{4,3,2,1,0:T(8,128)(2,1)} %refs_3_.3, bf16[1,16,20,128,128]{4,3,2,1,0:T(8,128)(2,1)} %refs_3_.3, bf16[4,256,256]{2,1,0:T(8,128)(2,1)} %constant.25.clone.refs_4_.refs_11_, ...), custom_call_target="tpu_custom_call" | custom-call | tf_op jit(solution)/shard_map/analyse/pallas_call | solution.py:210
  7.9 0.0 copy-start.13
  8.0 0.0 copy-start.2
  8.0 8.5 %all-to-all-start = ((bf16[8,320,128]{2,1,0:T(8,128)(2,1)}), bf16[8,320,128]{2,1,0:T(8,128)(2,1)S(1)}, u32[]{:S(2)}, u32[]{:S(2)}) async-start(bf16[8,320,128]{2,1,0:T(8,128)(2,1)} %bitcast), calls=%async_computation | async-start | bytes 1310720 | tf_op jit(solution)/shard_map/all_to_all | solution.py:522
  16.4 0.0 copy-done.14
  16.4 0.0 copy-start.8
  16.4 0.0 copy-start.12
  16.5 0.1 copy.19
  16.5 0.2 reshape.44.w_ref
  16.7 0.0 copy-start.9
  16.7 0.0 copy-start.10
  16.7 0.3 weights.1.w_ref
  17.0 11.2 %all-to-all-done = bf16[8,320,128]{2,1,0:T(8,128)(2,1)S(1)} async-done(((bf16[8,320,128]{2,1,0:T(8,128)(2,1)}), bf16[8,320,128]{2,1,0:T(8,128)(2,1)S(1)}, u32[]{:S(2)}, u32[]{:S(2)}) %all-to-all-start) | async-done | bytes 655392 | tf_op jit(solution)/shard_map/all_to_all | solution.py:522
  28.3 0.4 forward_x.2
  28.7 12.1 %all_to_all.30 = bf16[16,40,128]{2,1,0:T(8,128)(2,1)S(1)} all-to-all(bf16[16,40,128]{2,1,0:T(8,128)(2,1)S(1)} %bitcast.24), channel_id=1, replica_groups=mesh['dp'=16,'mp'=8] {'dp'}, dimensions={0} | all-to-all | bytes 327680 | tf_op jit(solution)/shard_map/all_to_all | solution.py:522
  40.8 1.3 %mix.1 = bf16[640,128]{1,0:T(8,128)(2,1)S(1)} custom-call(bf16[640,128]{1,0:T(8,128)(2,1)S(1)} %bitcast.19, bf16[128,512]{1,0:T(8,128)(2,1)S(1)} %copy-done.2, f32[2,400,128]{2,1,0:T(8,128)S(1)} %weights.1.w_ref), custom_call_target="tpu_custom_call" | custom-call | tf_op jit(solution)/shard_map/mix/pallas_call | solution.py:383
  42.2 9.3 %all_to_all.31 = bf16[16,40,128]{2,1,0:T(8,128)(2,1)S(1)} all-to-all(bf16[16,40,128]{2,1,0:T(8,128)(2,1)S(1)} %bitcast.25), channel_id=1, replica_groups=mesh['dp'=16,'mp'=8] {'dp'}, dimensions={0} | all-to-all | bytes 327680 | tf_op jit(solution)/shard_map/all_to_all | solution.py:522
  51.5 1.3 %inverse_x.1 = bf16[2560,128]{1,0:T(8,128)(2,1)} custom-call(bf16[640,128]{1,0:T(8,128)(2,1)S(1)} %bitcast.22, bf16[256,128]{1,0:T(8,128)(2,1)S(1)} %copy-done.8, f32[1,128]{1,0:T(1,128)S(1)} %copy-done.12), custom_call_target="tpu_custom_call" | custom-call | tf_op jit(solution)/shard_map/inverse_x/pallas_call | solution.py:383
  52.8 3.9 %all-to-all-start.3 = ((bf16[8,320,128]{2,1,0:T(8,128)(2,1)}), bf16[8,320,128]{2,1,0:T(8,128)(2,1)S(1)}, u32[]{:S(2)}, u32[]{:S(2)}) async-start(bf16[8,320,128]{2,1,0:T(8,128)(2,1)} %bitcast.6), calls=%async_computation.3 | async-start | bytes 1310720 | tf_op jit(solution)/shard_map/all_to_all | solution.py:522
  56.7 0.0 copy-start
  56.7 0.0 copy-start.3
  56.7 0.0 copy-start.4
  56.8 0.0 copy-start.7
  56.8 9.9 %conv.1 = (bf16[4,20,128,128]{3,2,1,0:T(8,128)(2,1)}, bf16[4,20,128,128]{3,2,1,0:T(8,128)(2,1)}, bf16[4,20,128,128]{3,2,1,0:T(8,128)(2,1)}, bf16[4,20,128,128]{3,2,1,0:T(8,128)(2,1)}) custom-call(bf16[1,16,20,128,128]{4,3,2,1,0:T(8,128)(2,1)} %refs_3_.3, bf16[1,16,20,128,128]{4,3,2,1,0:T(8,128)(2,1)} %refs_3_.3, bf16[1,16,20,128,128]{4,3,2,1,0:T(8,128)(2,1)} %refs_3_.3, ...), custom_call_target="tpu_custom_call" | custom-call | flops 3355443200 | bytes 20971520 | tf_op jit(solution)/shard_map/conv/pallas_call | solution.py:266
  66.6 2.0 %all-to-all-done.3 = bf16[8,320,128]{2,1,0:T(8,128)(2,1)S(1)} async-done(((bf16[8,320,128]{2,1,0:T(8,128)(2,1)}), bf16[8,320,128]{2,1,0:T(8,128)(2,1)S(1)}, u32[]{:S(2)}, u32[]{:S(2)}) %all-to-all-start.3) | async-done | bytes 655392 | tf_op jit(solution)/shard_map/all_to_all | solution.py:522
  68.7 0.0 copy-start.11
  68.7 16.3 %slab.1 = bf16[2560,128]{1,0:T(8,128)(2,1)S(1)} custom-call(bf16[4,20,128,128]{3,2,1,0:T(8,128)(2,1)} %get-tuple-element.16.refs_0_, bf16[4,20,128,128]{3,2,1,0:T(8,128)(2,1)} %get-tuple-element.17.refs_1_, bf16[4,20,128,128]{3,2,1,0:T(8,128)(2,1)} %get-tuple-element.18.refs_2_, bf16[4,20,128,128]{3,2,1,0:T(8,128)(2,1)} %get-tuple-element.19.refs_3_, ...), custom_call_target="tpu_custom_call" | custom-call | tf_op jit(solution)/shard_map/slab/pallas_call | solution.py:352
  85.0 0.0 copy-start.1
  85.0 15.5 %all_to_all.32 = bf16[8,320,128]{2,1,0:T(8,128)(2,1)S(1)} all-to-all(bf16[8,320,128]{2,1,0:T(8,128)(2,1)S(1)} %bitcast.18), channel_id=1, replica_groups=mesh['dp'=16,'mp'=8] {'mp'}, dimensions={0} | all-to-all | bytes 1310720 | tf_op jit(solution)/shard_map/all_to_all | solution.py:522
  100.5 0.4 forward_x.3
  100.9 11.7 %all_to_all.33 = bf16[16,40,128]{2,1,0:T(8,128)(2,1)S(1)} all-to-all(bf16[16,40,128]{2,1,0:T(8,128)(2,1)S(1)} %bitcast.23), channel_id=1, replica_groups=mesh['dp'=16,'mp'=8] {'dp'}, dimensions={0} | all-to-all | bytes 327680 | tf_op jit(solution)/shard_map/all_to_all | solution.py:522
  112.6 2.8 %grad.1 = f32[1600,64]{1,0:T(8,128)} custom-call(bf16[640,128]{1,0:T(8,128)(2,1)S(1)} %bitcast.20, bf16[640,128]{1,0:T(8,128)(2,1)S(1)} %bitcast.21, bf16[128,512]{1,0:T(8,128)(2,1)S(1)} %copy-done.2, bf16[512,512]{1,0:T(8,128)(2,1)S(1)} %copy-done.1), custom_call_target="tpu_custom_call" | custom-call | tf_op jit(solution)/shard_map/grad/pallas_call | solution.py:383
  (17 shorter events, 0.0 us)
Async XLA Ops:
  0.0 16.4 %copy-start.14 = (bf16[2,2,20,20,64]{4,1,3,2,0:T(2,128)(2,1)S(1)}, bf16[2,2,20,20,64]{4,1,3,2,0:T(2,128)(2,1)}, u32[]{:S(2)}) copy-start(bf16[2,2,20,20,64]{4,1,3,2,0:T(2,128)(2,1)} %param.19) | copy-start | bytes 614404
  7.9 8.8 %copy-start.6 = (bf16[256,256]{1,0:T(8,128)(2,1)S(1)}, bf16[256,256]{1,0:T(8,128)(2,1)}, u32[]{:S(2)}) copy-start(bf16[256,256]{1,0:T(8,128)(2,1)} %constant.35.clone.place_ref) | copy-start | bytes 393220
  7.9 20.3 %copy-start.5 = (bf16[128,256]{1,0:T(8,128)(2,1)S(1)}, bf16[128,256]{1,0:T(8,128)(2,1)}, u32[]{:S(2)}) copy-start(bf16[128,256]{1,0:T(8,128)(2,1)} %constant.32.clone.fx_ref) | copy-start | bytes 196612
  7.9 20.3 %copy-start.13 = (f32[1,128]{1,0:T(1,128)S(1)}, f32[1,128]{1,0:T(1,128)}, u32[]{:S(2)}) copy-start(f32[1,128]{1,0:T(1,128)} %constant.27.clone.un_ref) | copy-start | bytes 1540
  8.0 32.9 %copy-start.2 = (bf16[128,512]{1,0:T(8,128)(2,1)S(1)}, bf16[128,512]{1,0:T(8,128)(2,1)}, u32[]{:S(2)}) copy-start(bf16[128,512]{1,0:T(8,128)(2,1)} %constant.34.clone.spread_ref) | copy-start | bytes 393220
  8.0 20.3 %all-to-all-start = ((bf16[8,320,128]{2,1,0:T(8,128)(2,1)}), bf16[8,320,128]{2,1,0:T(8,128)(2,1)S(1)}, u32[]{:S(2)}, u32[]{:S(2)}) async-start(bf16[8,320,128]{2,1,0:T(8,128)(2,1)} %bitcast), calls=%async_computation | async-start | bytes 1310720 | tf_op jit(solution)/shard_map/all_to_all | solution.py:522
  16.4 35.1 %copy-start.8 = (bf16[256,128]{1,0:T(8,128)(2,1)S(1)}, bf16[256,128]{1,0:T(8,128)(2,1)}, u32[]{:S(2)}) copy-start(bf16[256,128]{1,0:T(8,128)(2,1)} %constant.33.clone.ix_ref) | copy-start | bytes 196612
  16.4 35.1 %copy-start.12 = (f32[1,128]{1,0:T(1,128)S(1)}, f32[1,128]{1,0:T(1,128)}, u32[]{:S(2)}) copy-start(f32[1,128]{1,0:T(1,128)} %constant.29.clone.un_ref) | copy-start | bytes 1540
  16.7 40.0 %copy-start.9 = (bf16[20,20]{1,0:T(8,128)(2,1)S(1)}, bf16[20,20]{1,0:T(8,128)(2,1)}, u32[]{:S(2)}) copy-start(bf16[20,20]{1,0:T(8,128)(2,1)} %refs_4_.2) | copy-start | bytes 2404
  16.7 40.0 %copy-start.10 = (f32[20]{0:T(128)S(1)}, f32[20]{0:T(128)}, u32[]{:S(2)}) copy-start(f32[20]{0:T(128)} %refs_5_.3) | copy-start | bytes 244
  52.8 15.9 %all-to-all-start.3 = ((bf16[8,320,128]{2,1,0:T(8,128)(2,1)}), bf16[8,320,128]{2,1,0:T(8,128)(2,1)S(1)}, u32[]{:S(2)}, u32[]{:S(2)}) async-start(bf16[8,320,128]{2,1,0:T(8,128)(2,1)} %bitcast.6), calls=%async_computation.3 | async-start | bytes 1310720 | tf_op jit(solution)/shard_map/all_to_all | solution.py:522
  56.7 12.0 %copy-start = (bf16[4,256,256]{2,1,0:T(8,128)(2,1)S(1)}, bf16[4,256,256]{2,1,0:T(8,128)(2,1)}, u32[]{:S(2)}) copy-start(bf16[4,256,256]{2,1,0:T(8,128)(2,1)} %constant.25.clone.refs_4_.refs_11_) | copy-start | bytes 1572868
  56.7 11.9 %copy-start.3 = (bf16[4,256,256]{2,1,0:T(8,128)(2,1)S(1)}, bf16[4,256,256]{2,1,0:T(8,128)(2,1)}, u32[]{:S(2)}) copy-start(bf16[4,256,256]{2,1,0:T(8,128)(2,1)} %constant.26.clone.refs_10_) | copy-start | bytes 1572868
  56.7 11.9 %copy-start.4 = (bf16[128,256]{1,0:T(8,128)(2,1)S(1)}, bf16[128,256]{1,0:T(8,128)(2,1)}, u32[]{:S(2)}) copy-start(bf16[128,256]{1,0:T(8,128)(2,1)} %constant.30.clone.refs_5_.refs_12_) | copy-start | bytes 196612
  56.8 11.9 %copy-start.7 = (bf16[256,128]{1,0:T(8,128)(2,1)S(1)}, bf16[256,128]{1,0:T(8,128)(2,1)}, u32[]{:S(2)}) copy-start(bf16[256,128]{1,0:T(8,128)(2,1)} %constant.31.clone.refs_9_) | copy-start | bytes 196612
  68.7 31.8 %copy-start.11 = (f32[1,128]{1,0:T(1,128)S(1)}, f32[1,128]{1,0:T(1,128)}, u32[]{:S(2)}) copy-start(f32[1,128]{1,0:T(1,128)} %constant.28.clone.un_ref) | copy-start | bytes 1540
  85.0 27.6 %copy-start.1 = (bf16[512,512]{1,0:T(8,128)(2,1)S(1)}, bf16[512,512]{1,0:T(8,128)(2,1)}, u32[]{:S(2)}) copy-start(bf16[512,512]{1,0:T(8,128)(2,1)} %constant.24.clone.gather_ref) | copy-start | bytes 1572868
